TPU v7x, 256 devices: a whole 4x4x8 slice. The times are simulated.
256 devices in a mesh: seq: 128 (over y, z, x), head: 2 (over core).
Axes of the slice: x: 4, y: 4, z: 8, core: 2. Of those that a mesh axis runs over, the one named last changes fastest.
Arguments:
- queries: bfloat16 [32768, 4096], P('seq', 'head'), may hold values from -6 to 6
- keys: bfloat16 [32768, 4096], P('seq', 'head'), may hold values from -6 to 6
- values: bfloat16 [32768, 4096], P('seq', 'head'), may hold values from -6 to 6
- gain: float32 [4096], P('head'), may hold values from 0.1 to 1.9
- w_out: bfloat16 [4096, 3072], P('head', 'seq'), may hold values from -0.09375 to 0.09375
Outputs:
- mixed: bfloat16 [32768, 3072], P(('seq', 'head'))
All inputs are finite; a program needn't handle non-finite values.
Results may differ from a plain program's by a relative error of at most 0.0049.
Values may be sent and summed in bfloat16 or wider, within the bound.
No kernel may reach another device: no remote copies, remote signals or barrier semaphores. Data moves between devices by JAX's collectives and lax.ppermute only.
A program may use at most 320 MiB of HBM per device.

v0:
```python
import jax
import jax.numpy as jnp
from jax import lax
from jax.sharding import PartitionSpec as P

DH = 128


def prefix(array, axis, combine, identity):
    devices, place = (lax.axis_size(axis), lax.axis_index(axis))
    everything = lax.all_gather(array, axis)
    start = jnp.broadcast_to(jnp.asarray(identity, array.dtype), array.shape)

    def lap(k, before):
        reached = k < place
        new = combine(before, everything[k])
        return jnp.where(reached, new, before)

    return lax.fori_loop(0, devices, lap, start)


def add_states(earlier, later):
    return earlier + later


def per_device(queries, keys, values, gain, w_out):
    tok_rows = queries.shape[0]
    group_heads = queries.shape[1] // DH
    block_count = tok_rows // DH
    query_blocks = queries.reshape(block_count, DH, group_heads, DH)
    key_blocks = keys.reshape(block_count, DH, group_heads, DH)
    value_blocks = values.reshape(block_count, DH, group_heads, DH)
    highest = lax.Precision.HIGHEST
    block_states = jnp.einsum(
        "bthd,bthe->bhde", key_blocks, value_blocks, preferred_element_type=jnp.float32
    )
    local_state = jnp.sum(block_states, axis=0)
    prior = prefix(local_state, "seq", add_states, jnp.zeros_like(local_state))
    earlier_blocks = jnp.concatenate(
        [jnp.zeros_like(block_states[:1]), jnp.cumsum(block_states[:-1], axis=0)], axis=0
    )
    starts = prior[None] + earlier_blocks
    cross = jnp.einsum(
        "bthd,bhde->bthe", query_blocks.astype(jnp.float32), starts, precision=highest
    )
    scores = jnp.einsum(
        "bthd,bshd->bhts", query_blocks, key_blocks, preferred_element_type=jnp.float32
    )
    causal_mask = jnp.arange(DH)[:, None] >= jnp.arange(DH)[None, :]
    scores = jnp.where(causal_mask[None, None], scores, jnp.float32(0.0))
    inner = jnp.einsum(
        "bhts,bshe->bthe", scores, value_blocks.astype(jnp.float32), precision=highest
    )
    attn = cross + inner
    gain_rows = gain.reshape(group_heads, DH)
    meansq = jnp.mean(attn * attn, axis=-1, keepdims=True)
    normed = (attn * lax.rsqrt(meansq + 1e-06) * gain_rows).astype(jnp.bfloat16)
    normed = normed.reshape(tok_rows, group_heads * DH)
    terms = jnp.dot(
        normed, lax.all_gather(w_out, "seq", axis=1, tiled=True), preferred_element_type=jnp.float32
    )
    return lax.psum_scatter(terms, "head", scatter_dimension=0, tiled=True).astype(jnp.bfloat16)


def solution(mesh):
    return jax.shard_map(
        per_device,
        mesh=mesh,
        in_specs=(
            P("seq", "head"),
            P("seq", "head"),
            P("seq", "head"),
            P("head"),
            P("head", "seq"),
        ),
        out_specs=P(("seq", "head"), None),
        check_vma=False,
    )
```

profile of v0, /device:TPU:1, one launch (start us, length us, event | category | flops | bytes accessed | tf_op | source)
XLA Modules:
  0.0 869.8 jit_solution(16932997771402640793)
XLA Ops:
  9.3 3.3 fusion.21
  13.5 2.4 slice.4
  17.3 2.2 fusion.15
  19.5 602.6 %all-gather.6.cloned.1.call-done = f32[2048,128,128]{2,1,0:T(8,128)} async-done(((f32[16,128,128]{2,1,0:T(8,128)}), f32[2048,128,128]{2,1,0:T(8,128)}) %all-gather.6.cloned.1.call-update) | async-done | bytes 134217744 | tf_op jit(solution)/shard_map/all_gather | solution.py:11
  622.1 207.6 %while.14 = (s32[]{:T(128)}, f32[16,128,128]{2,1,0:T(8,128)S(1)}, s32[]{:T(128)}, f32[128,16,128,128]{3,2,1,0:T(8,128)}, s32[]{:T(128)}, /*index=5*/s32[]{:T(128)}) while((s32[]{:T(128)}, f32[16,128,128]{2,1,0:T(8,128)S(1)}, s32[]{:T(128)}, f32[128,16,128,128]{3,2,1,0:T(8,128)}, s32[]{:T(128)}, /*index=5*/s32[]{:T(128)}) %tuple.34), condition=%wide.region_2.3_spmd.clone, body=%wide.region_1.2_spmd.clone.sunk | while | flops 786436 | bytes 3145821 | solution.py:19
  627.0 1.6 add_select_fusion.2
  628.6 1.6 add_select_fusion.2
  630.2 1.6 add_select_fusion.2
  635.0 1.6 add_select_fusion.2
  636.7 1.6 add_select_fusion.2
  638.3 1.6 add_select_fusion.2
  639.9 1.6 add_select_fusion.2
  641.5 1.6 add_select_fusion.2
  643.1 1.6 add_select_fusion.2
  644.7 1.6 add_select_fusion.2
  646.4 1.6 add_select_fusion.2
  648.0 1.6 add_select_fusion.2
  649.6 1.6 add_select_fusion.2
  651.2 1.6 add_select_fusion.2
  654.4 1.6 add_select_fusion.2
  656.1 1.6 add_select_fusion.2
  657.7 1.6 add_select_fusion.2
  662.5 1.6 add_select_fusion.2
  664.1 1.6 add_select_fusion.2
  665.7 1.6 add_select_fusion.2
  669.0 1.6 add_select_fusion.2
  670.6 1.6 add_select_fusion.2
  672.2 1.6 add_select_fusion.2
  673.8 1.6 add_select_fusion.2
  675.4 1.6 add_select_fusion.2
  677.0 1.6 add_select_fusion.2
  678.6 1.6 add_select_fusion.2
  680.3 1.6 add_select_fusion.2
  681.9 1.6 add_select_fusion.2
  683.5 1.6 add_select_fusion.2
  685.2 1.6 add_select_fusion.2
  686.8 1.6 add_select_fusion.2
  690.1 1.6 add_select_fusion.2
  691.7 1.6 add_select_fusion.2
  693.3 1.6 add_select_fusion.2
  694.9 1.6 add_select_fusion.2
  698.1 1.6 add_select_fusion.2
  711.1 1.9 add_select_fusion.2
  717.8 1.6 add_select_fusion.2
  721.1 1.6 add_select_fusion.2
  724.4 1.6 add_select_fusion.2
  726.0 1.6 add_select_fusion.2
  729.3 1.6 add_select_fusion.2
  732.5 1.7 add_select_fusion.2
  734.3 1.6 add_select_fusion.2
  735.9 1.6 add_select_fusion.2
  737.5 1.7 add_select_fusion.2
  739.2 1.6 add_select_fusion.2
  740.8 1.6 add_select_fusion.2
  742.5 1.6 add_select_fusion.2
  744.1 1.6 add_select_fusion.2
  749.0 1.6 add_select_fusion.2
  750.6 1.6 add_select_fusion.2
  752.2 1.6 add_select_fusion.2
  829.7 3.2 fusion.2
  833.0 2.4 multiply_reduce_fusion
  836.8 9.7 %fusion.7 = f32[256,3072]{1,0:T(8,128)} fusion(bf16[2048,3072]{0,1:T(8,128)(2,1)} %all-gather.4.cloned.1.call-done, bf16[32,8,16,128]{3,2,1,0:T(8,128)(2,1)S(1)} %bitcast.35), kind=kOutput, calls=%fused_computation.9 | convolution fusion | flops 3221225472 | bytes 16777216 | tf_op jit(solution)/shard_map/dot_general | solution.py:59
  846.5 14.4 %reduce-scatter.2.cloned.1.call-done = f32[128,3072]{1,0:T(8,128)} async-done(((f32[256,3072]{1,0:T(8,128)}), f32[128,3072]{1,0:T(8,128)}) %reduce-scatter.2.cloned.1.call-update) | async-done | bytes 1572880 | tf_op jit(solution)/shard_map/reduce_scatter | solution.py:62
  860.9 2.4 convert_element_type.9
  (100 shorter events, 124.1 us)
Async XLA Ops:
  6.5 615.6 %all-gather.6.cloned.1.call-start = ((), (), s32[]{:S(2)}) async-start(), calls=%async_computation.3 | async-start | bytes 135266304 | tf_op jit(solution)/shard_map/all_gather | solution.py:11
  6.5 2.5 copy-start.3
  9.3 3.3 copy-start
  12.6 824.2 %all-gather.4.cloned.1.call-start = ((), (), s32[]{:S(2)}) async-start(), calls=%async_computation.1 | async-start | bytes 12681216 | tf_op jit(solution)/shard_map/all_gather | solution.py:60
  13.4 847.5 %reduce-scatter.2.cloned.1.call-start = ((), (), s32[]{:S(2)}) async-start(), calls=%async_computation.2 | async-start | bytes 4718592 | tf_op jit(solution)/shard_map/reduce_scatter | solution.py:62
  13.4 3.9 copy-start.1
  829.7 3.2 copy-start.2
  833.0 2.4 copy-start.4
Sparse Core Ops, SparseCore 0:
  12.7 609.3 all-gather.5
  625.8 132.8 all-gather.3
  846.6 14.2 reduce-scatter.1
where the time goes:
time: 875 us; the launch traced here: 870 us
  waiting for transfers between devices  618 us (71%)
  other arithmetic  207 us (24%)
  matrix products  20.7 us (2%)
  between operations  13.3 us (2%)
    all_gather x1, waiting for transfers between devices, prefix(): everything = lax.all_gather(array, axis)  603 us
    select_n x128, other arithmetic, lap(): return jnp.where(reached, new, before)  204 us
  transfers between devices with their start and end apart: 3, of which 2 were waited for; matrix products, arithmetic and copies ran while one was open for 25% of the time, Pallas kernels for 0%

commit v1 on v0

v1 whole, which is shorter than its diff:
```python
import jax
import jax.numpy as jnp
from jax import lax
from jax.experimental import pallas as pl
from jax.experimental.pallas import tpu as pltpu
from jax.sharding import PartitionSpec as P

DH = 128
BF = jnp.bfloat16
F32 = jnp.float32


def dot(a, b, dims):
    return lax.dot_general(a, b, (dims, ((), ())), preferred_element_type=F32)


def states_kernel(k_ref, v_ref, o_ref):
    for h in range(k_ref.shape[1] // DH):
        c = slice(h * DH, (h + 1) * DH)
        o_ref[c, :] = dot(k_ref[:, c], v_ref[:, c], ((0,), (0,))).astype(BF)


def local_states(keys, values, heads_per_step=4):
    rows, cols = keys.shape
    width = heads_per_step * DH
    spec = pl.BlockSpec((rows, width), lambda i: (0, i))
    return pl.pallas_call(
        states_kernel,
        grid=(cols // width,),
        in_specs=[spec, spec],
        out_specs=pl.BlockSpec((width, DH), lambda i: (i, 0)),
        out_shape=jax.ShapeDtypeStruct((cols, DH), BF),
        name="local_states",
    )(keys, values)


def running_kernel(x_ref, o_ref):
    def step(j, total):
        o_ref[j] = total.astype(BF)
        return total + x_ref[j].astype(F32)

    lax.fori_loop(0, x_ref.shape[0], step, jnp.zeros(x_ref.shape[1:], F32), unroll=8)


def exclusive_sums(pieces):
    return pl.pallas_call(
        running_kernel,
        out_shape=jax.ShapeDtypeStruct(pieces.shape, BF),
        name="exclusive_sums",
    )(pieces)


def attention_kernel(q_ref, k_ref, v_ref, s_ref, g_ref, o_ref):
    rows = q_ref.shape[0]
    t = lax.broadcasted_iota(jnp.int32, (rows, rows), 0)
    s = lax.broadcasted_iota(jnp.int32, (rows, rows), 1)
    causal = t >= s
    for h in range(q_ref.shape[1] // DH):
        c = slice(h * DH, (h + 1) * DH)
        q, k, v = q_ref[:, c], k_ref[:, c], v_ref[:, c]
        scores = jnp.where(causal, dot(q, k, ((1,), (1,))), 0.0)
        high = scores.astype(BF)
        low = (scores - high.astype(F32)).astype(BF)
        attn = dot(q, s_ref[c, :], ((1,), (0,)))
        attn = attn + dot(high, v, ((1,), (0,)))
        attn = attn + dot(low, v, ((1,), (0,)))
        meansq = jnp.mean(attn * attn, axis=-1, keepdims=True)
        o_ref[:, c] = (attn * lax.rsqrt(meansq + 1e-06) * g_ref[:, c]).astype(BF)


def attention(queries, keys, values, prior, gain, heads_per_step=4):
    rows, cols = queries.shape
    width = heads_per_step * DH
    spec = pl.BlockSpec((rows, width), lambda i: (0, i))
    return pl.pallas_call(
        attention_kernel,
        grid=(cols // width,),
        in_specs=[
            spec,
            spec,
            spec,
            pl.BlockSpec((width, DH), lambda i: (i, 0)),
            pl.BlockSpec((1, width), lambda i: (0, i)),
        ],
        out_specs=spec,
        out_shape=jax.ShapeDtypeStruct((rows, cols), BF),
        name="attention",
    )(queries, keys, values, prior, gain)


def project_kernel(place_ref, n_ref, w_ref, mine_ref, theirs_ref):
    half = mine_ref.shape[0]
    me = place_ref[0]
    terms = dot(n_ref[...], w_ref[...], ((1,), (1,)))
    first, second = terms[:half], terms[half:]
    mine_ref[...] = jnp.where(me == 0, first, second)
    theirs_ref[...] = jnp.where(me == 0, second, first)


def project(place, normed, w_rows, block=384):
    rows, depth = normed.shape
    width = w_rows.shape[0]
    half = jax.ShapeDtypeStruct((rows // 2, width), F32)
    out = pl.BlockSpec((rows // 2, block), lambda i, p: (0, i))
    return pl.pallas_call(
        project_kernel,
        grid_spec=pltpu.PrefetchScalarGridSpec(
            num_scalar_prefetch=1,
            grid=(width // block,),
            in_specs=[
                pl.BlockSpec((rows, depth), lambda i, p: (0, 0)),
                pl.BlockSpec((block, depth), lambda i, p: (i, 0)),
            ],
            out_specs=[out, out],
        ),
        out_shape=[half, half],
        name="project",
    )(place, normed, w_rows)


def per_device(queries, keys, values, gain, w_out):
    devices = lax.axis_size("seq")
    w_rows = lax.all_gather(w_out.T, "seq", axis=0, tiled=True)
    states = local_states(keys, values)
    pieces = lax.all_to_all(states, "seq", 0, 0, tiled=True)
    sums = exclusive_sums(pieces.reshape(devices, -1, DH))
    prior = lax.all_to_all(sums.reshape(-1, DH), "seq", 0, 0, tiled=True)
    normed = attention(queries, keys, values, prior, gain.reshape(1, -1))
    place = lax.axis_index("head").astype(jnp.int32).reshape(1)
    mine, theirs = project(place, normed, w_rows)
    other = lax.ppermute(theirs, "head", [(0, 1), (1, 0)])
    return (mine + other).astype(BF)


def solution(mesh):
    return jax.shard_map(
        per_device,
        mesh=mesh,
        in_specs=(
            P("seq", "head"),
            P("seq", "head"),
            P("seq", "head"),
            P("head"),
            P("head", "seq"),
        ),
        out_specs=P(("seq", "head"), None),
        check_vma=False,
    )
```

time: 875 us -> 176 us (0.20)
  waiting for transfers between devices: 618 us -> 91.1 us
  other arithmetic: 207 us -> 2.51 us
  blocking collectives: 0 us -> 34.2 us
  Pallas kernels: 0 us -> 23.6 us
  matrix products: 20.7 us -> 0 us
  starting transfers between devices: 0.08 us -> 9.85 us
    all_gather x2 -> x1, waiting for transfers between devices: 603 us -> 71.2 us  [per_device(): w_rows = lax.all_gather(w_out.T, 'seq', axis=0, tiled=True)]
    select_n x128 -> x0, other arithmetic: 204 us -> none  [lap(): return jnp.where(reached, new, before)]
    all_to_all x0 -> x1, blocking collectives: none -> 34.2 us  [per_device(): pieces = lax.all_to_all(states, 'seq', 0, 0, tiled=True)]
    pallas_call x0 -> x4, Pallas kernels: none -> 23.6 us  [the longest x1 11.2 us: project(): pl.pallas_call(project_kernel, grid_spec=pltpu.PrefetchScalarGridSpec(num...]
    dot_general x5 -> x0, matrix products: 20.7 us -> none  [the longest x1 9.67 us: per_device(): jnp.dot(normed, lax.all_gather(w_out, 'seq', axis=1, tiled=True), preferr...]
    all_to_all x0 -> x1, waiting for transfers between devices: none -> 15.9 us  [per_device(): prior = lax.all_to_all(sums.reshape(-1, DH), 'seq', 0, 0, tiled=True)]
    reduce_scatter x1 -> x0, waiting for transfers between devices: 14.4 us -> none  [per_device(): lax.psum_scatter(terms, 'head', scatter_dimension=0, tiled=True)]
  transfers between devices with their start and end apart: 3 -> 3, of which waited for: 2 -> 3; matrix products, arithmetic and copies ran while one was open for 25% -> 0% of each run, Pallas kernels for 0% -> 7%
where the time goes in v1:
time: 176 us
  waiting for transfers between devices  91.1 us (52%)
  blocking collectives  34.2 us (19%)
  Pallas kernels  23.6 us (13%)
  between operations  13.4 us (8%)
  starting transfers between devices  9.85 us (6%)
  other arithmetic  2.51 us (1%)
    all_gather x1, waiting for transfers between devices, per_device(): w_rows = lax.all_gather(w_out.T, 'seq', axis=0, tiled=True)  71.2 us
    all_to_all x1, blocking collectives, per_device(): pieces = lax.all_to_all(states, 'seq', 0, 0, tiled=True)  34.2 us
    all_to_all x1, waiting for transfers between devices, per_device(): prior = lax.all_to_all(sums.reshape(-1, DH), 'seq', 0, 0, tiled=True)  15.9 us
    pallas_call x1, Pallas kernels, project(): pl.pallas_call(project_kernel, grid_spec=pltpu.PrefetchScalarGridSpec(num...  11.2 us
    all_to_all x1, starting transfers between devices, per_device(): prior = lax.all_to_all(sums.reshape(-1, DH), 'seq', 0, 0, tiled=True)  8.45 us
    pallas_call x1, Pallas kernels, attention(): pl.pallas_call(attention_kernel, grid=(cols // width,), in_specs=[spec, s...  6.48 us
    pallas_call x1, Pallas kernels, local_states(): pl.pallas_call(states_kernel, grid=(cols // width,), in_specs=[spec, spec...  3.97 us
  transfers between devices with their start and end apart: 3, of which 3 were waited for; matrix products, arithmetic and copies ran while one was open for 0% of the time, Pallas kernels for 7%

profile of v1, /device:TPU:1, one launch (start us, length us, event | category | flops | bytes accessed | tf_op | source)
XLA Modules:
  0.0 175.5 jit_solution(13707935733352922934)
XLA Ops:
  6.5 0.0 all-gather.2.cloned.1.call-start
  6.5 0.7 all-gather.2.cloned.1.call-update
  7.3 4.0 %local_states.1 = bf16[2048,128]{1,0:T(8,128)(2,1)} custom-call(bf16[256,2048]{1,0:T(8,128)(2,1)} %k_ref.3, bf16[256,2048]{1,0:T(8,128)(2,1)} %v_ref.3), custom_call_target="tpu_custom_call" | custom-call | tf_op jit(solution)/shard_map/local_states/pallas_call | solution.py:27
  11.2 34.2 %all_to_all.17.x_ref = bf16[128,16,128]{2,1,0:T(8,128)(2,1)} all-to-all(bf16[128,16,128]{2,1,0:T(8,128)(2,1)} %bitcast.6), channel_id=1, replica_groups=mesh['seq'=128,'head'=2] {'seq'}, dimensions={0} | all-to-all | bytes 1048576 | tf_op jit(solution)/shard_map/all_to_all | solution.py:125
  45.5 2.0 %exclusive_sums.1 = bf16[128,16,128]{2,1,0:T(8,128)(2,1)} custom-call(bf16[128,16,128]{2,1,0:T(8,128)(2,1)} %all_to_all.17.x_ref), custom_call_target="tpu_custom_call" | custom-call | tf_op jit(solution)/shard_map/exclusive_sums/pallas_call | solution.py:46
  47.5 8.5 %all-to-all-start.1 = ((bf16[128,16,128]{2,1,0:T(8,128)(2,1)}), bf16[128,16,128]{2,1,0:T(8,128)(2,1)S(1)}, u32[]{:S(2)}, u32[]{:S(2)}) async-start(bf16[128,16,128]{2,1,0:T(8,128)(2,1)} %exclusive_sums.1), calls=%async_computation.1 | async-start | bytes 1048576 | tf_op jit(solution)/shard_map/all_to_all | solution.py:127
  56.0 15.9 %all-to-all-done.1 = bf16[128,16,128]{2,1,0:T(8,128)(2,1)S(1)} async-done(((bf16[128,16,128]{2,1,0:T(8,128)(2,1)}), bf16[128,16,128]{2,1,0:T(8,128)(2,1)S(1)}, u32[]{:S(2)}, u32[]{:S(2)}) %all-to-all-start.1) | async-done | bytes 524320 | tf_op jit(solution)/shard_map/all_to_all | solution.py:127
  71.9 0.0 copy-start
  71.9 0.8 copy-done
  72.7 6.5 %attention.1.n_ref = bf16[256,2048]{1,0:T(8,128)(2,1)} custom-call(bf16[256,2048]{1,0:T(8,128)(2,1)} %q_ref.1, bf16[256,2048]{1,0:T(8,128)(2,1)} %k_ref.3, bf16[256,2048]{1,0:T(8,128)(2,1)} %v_ref.3, bf16[2048,128]{1,0:T(8,128)(2,1)} %bitcast.5, f32[1,2048]{1,0:T(1,128)} %bitcast.8), custom_call_target="tpu_custom_call" | custom-call | tf_op jit(solution)/shard_map/attention/pallas_call | solution.py:75
  79.1 71.2 %all-gather.2.cloned.1.call-done.w_ref = bf16[3072,2048]{1,0:T(8,128)(2,1)} async-done(((bf16[24,2048]{1,0:T(8,128)(2,1)}), bf16[3072,2048]{1,0:T(8,128)(2,1)}) %all-gather.2.cloned.1.call-update) | async-done | bytes 12582928 | tf_op jit(solution)/shard_map/all_gather | solution.py:123
  150.4 11.2 %project.1 = (f32[128,3072]{1,0:T(8,128)}, f32[128,3072]{1,0:T(8,128)}) custom-call(s32[1]{0:T(128)} %bitcast.place_ref, bf16[256,2048]{1,0:T(8,128)(2,1)} %attention.1.n_ref, bf16[3072,2048]{1,0:T(8,128)(2,1)} %all-gather.2.cloned.1.call-done.w_ref), custom_call_target="tpu_custom_call" | custom-call | tf_op jit(solution)/shard_map/project/pallas_call | solution.py:105
  161.5 1.4 collective-permute-start
  162.9 3.2 %collective-permute-done = f32[128,3072]{1,0:T(8,128)S(1)} collective-permute-done((f32[128,3072]{1,0:T(8,128)}, f32[128,3072]{1,0:T(8,128)S(1)}, u32[]{:S(2)}, u32[]{:S(2)}) %collective-permute-start) | collective-permute-done | bytes 1572896 | tf_op jit(solution)/shard_map/ppermute | solution.py:131
  166.2 2.5 %add_convert_fusion = bf16[128,3072]{1,0:T(8,128)(2,1)} fusion(f32[128,3072]{1,0:T(8,128)} %get-tuple-element.7, f32[128,3072]{1,0:T(8,128)S(1)} %collective-permute-done), kind=kLoop, calls=%fused_computation | loop fusion | flops 786432 | bytes 3932160 | tf_op jit(solution)/shard_map/convert_element_type | solution.py:132
Async XLA Ops:
  6.5 143.8 %all-gather.2.cloned.1.call-start = ((), (), s32[]{:S(2)}) async-start(), calls=%async_computation.2 | async-start | bytes 12681216 | tf_op jit(solution)/shard_map/all_gather | solution.py:123
  47.5 24.4 %all-to-all-start.1 = ((bf16[128,16,128]{2,1,0:T(8,128)(2,1)}), bf16[128,16,128]{2,1,0:T(8,128)(2,1)S(1)}, u32[]{:S(2)}, u32[]{:S(2)}) async-start(bf16[128,16,128]{2,1,0:T(8,128)(2,1)} %exclusive_sums.1), calls=%async_computation.1 | async-start | bytes 1048576 | tf_op jit(solution)/shard_map/all_to_all | solution.py:127
  71.9 0.8 copy-start
  161.5 4.6 %collective-permute-start = (f32[128,3072]{1,0:T(8,128)}, f32[128,3072]{1,0:T(8,128)S(1)}, u32[]{:S(2)}, u32[]{:S(2)}) collective-permute-start(f32[128,3072]{1,0:T(8,128)} %get-tuple-element.8), channel_id=1, source_target_pairs={{0,1},{1,0},{2,3},{3,2},{4,5},{5,4},{6,7},{7,6},{8,9},{9,8},{10,11... | collective-permute-start | bytes 4718600 | tf_op jit(solution)/shard_map/ppermute | solution.py:131
Sparse Core Ops, SparseCore 0:
  11.0 139.3 all-gather.1

commit v2 on v1

--- a/solution.py
+++ b/solution.py
@@ -4,6 +4,7 @@
 from jax.experimental import pallas as pl
 from jax.experimental.pallas import tpu as pltpu
 from jax.sharding import PartitionSpec as P
+
 
 DH = 128
 BF = jnp.bfloat16
@@ -88,61 +89,155 @@
     )(queries, keys, values, prior, gain)
 
 
-def project_kernel(place_ref, n_ref, w_ref, mine_ref, theirs_ref):
-    half = mine_ref.shape[0]
-    me = place_ref[0]
-    terms = dot(n_ref[...], w_ref[...], ((1,), (1,)))
-    first, second = terms[:half], terms[half:]
-    mine_ref[...] = jnp.where(me == 0, first, second)
-    theirs_ref[...] = jnp.where(me == 0, second, first)
-
-
-def project(place, normed, w_rows, block=384):
-    rows, depth = normed.shape
-    width = w_rows.shape[0]
-    half = jax.ShapeDtypeStruct((rows // 2, width), F32)
-    out = pl.BlockSpec((rows // 2, block), lambda i, p: (0, i))
+SEQ = ("y", "z", "x")
+NY, NZ, NX = 4, 8, 4
+PART_B, PART_C = 1024, 1024
+
+
+def shift(block, axis, by):
+    pairs = []
+    for y in range(NY):
+        for z in range(NZ):
+            for x in range(NX):
+                ty = (y + by) % NY if axis == "y" else y
+                tz = (z + by) % NZ if axis == "z" else z
+                tx = (x + by) % NX if axis == "x" else x
+                pairs.append(((y * NZ + z) * NX + x, (ty * NZ + tz) * NX + tx))
+    return lax.ppermute(block, SEQ, pairs)
+
+
+def wrap(index, count):
+    return lax.rem(index + count, count)
+
+
+def assemble(place, which, pieces, outs, cuts):
+    count = len(pieces)
+
+    def kernel(place_ref, *refs):
+        for by in range(count):
+            cuts(refs[by], refs[count:], wrap(place_ref[which] - by, count))
+
+    vmem = pl.BlockSpec(memory_space=pltpu.VMEM)
+    return pl.pallas_call(
+        kernel,
+        in_specs=[pl.BlockSpec(memory_space=pltpu.SMEM)] + [vmem] * count,
+        out_specs=[vmem] * len(outs),
+        out_shape=[jax.ShapeDtypeStruct(o, BF) for o in outs],
+    )(place, *pieces)
+
+
+def both_ways(low, high, axis):
+    below_low = shift(low, axis, 1)
+    above_high = shift(high, axis, -1)
+    below_high = shift(high, axis, 1)
+    above_low = shift(low, axis, -1)
+    far_low = shift(below_low, axis, 1)
+    far_high = shift(above_high, axis, -1)
+    return [low, high, below_low, below_high, far_low, far_high, above_low, above_high]
+
+
+def gather(own, place):
+    n = own.shape[0]
+    half = NZ // 2
+    pieces = [own] + [shift(own, "z", by) for by in range(1, NZ)]
+
+    def cut_z(piece, outs, i):
+        outs[0][i] = piece[:, :PART_B]
+        outs[1][i] = piece[:, PART_B:]
+
+    def cut_y(piece, outs, i):
+        outs[0][i] = piece[:half]
+        outs[1][i] = piece[half:]
+
+    def cut_x(piece, outs, i):
+        outs[0][:, i] = piece[:half]
+        outs[1][:, i] = piece[half:]
+
+    col_b, col_c = assemble(place, 1, pieces, [(NZ, n, PART_B), (NZ, n, PART_C)], cut_z)
+    along_y = [col_b] + [shift(col_b, "y", by) for by in (1, 2, 3)]
+    along_x = [col_c] + [shift(col_c, "x", by) for by in (1, 2, 3)]
+    plane_b = assemble(place, 0, along_y, [(NY, half, n, PART_B)] * 2, cut_y)
+    plane_c = assemble(place, 2, along_x, [(half, NX, n, PART_C)] * 2, cut_x)
+    return both_ways(*plane_b, "x"), both_ways(*plane_c, "y")
+
+
+def project_kernel(place_ref, n_ref, *refs):
+    pieces_b, pieces_c = refs[:8], refs[8:16]
+    mine_ref, theirs_ref, wb_ref, wc_ref, sems = refs[16:]
+    y, x, me = place_ref[0], place_ref[2], place_ref[3]
+    half = NZ // 2
+    pairs = []
+    for by in range(4):
+        for part, lane in enumerate((slice(0, half), slice(half, NZ))):
+            pairs.append((pieces_b[2 * by + part], wb_ref.at[:, lane, wrap(x - by, NX)]))
+            pairs.append((pieces_c[2 * by + part], wc_ref.at[wrap(y - by, NY), lane]))
+    copies = [pltpu.make_async_copy(s, d, sems.at[i]) for i, (s, d) in enumerate(pairs)]
+    for copy in copies:
+        copy.start()
+    for copy in copies:
+        copy.wait()
+    rows = mine_ref.shape[0]
+    n = wb_ref.shape[3]
+    parts = ((wb_ref, n_ref[:, :PART_B]), (wc_ref, n_ref[:, PART_B:]))
+    wide = half * NX * n
+    for row in range(NY):
+        for start in (0, half):
+            terms = None
+            for w_ref, normed in parts:
+                w = w_ref[row, start : start + half].reshape(wide, normed.shape[1])
+                term = dot(normed, w, ((1,), (1,)))
+                terms = term if terms is None else terms + term
+            first, second = terms[:rows], terms[rows:]
+            at = slice((row * NZ + start) * NX * n, (row * NZ + start) * NX * n + wide)
+            mine_ref[:, at] = jnp.where(me == 0, first, second)
+            theirs_ref[:, at] = jnp.where(me == 0, second, first)
+
+
+def project(place, normed, pieces):
+    rows = normed.shape[0]
+    n = pieces[0].shape[2]
+    half = jax.ShapeDtypeStruct((rows // 2, NY * NZ * NX * n), F32)
+    hbm = pl.BlockSpec(memory_space=pl.ANY)
     return pl.pallas_call(
         project_kernel,
-        grid_spec=pltpu.PrefetchScalarGridSpec(
-            num_scalar_prefetch=1,
-            grid=(width // block,),
-            in_specs=[
-                pl.BlockSpec((rows, depth), lambda i, p: (0, 0)),
-                pl.BlockSpec((block, depth), lambda i, p: (i, 0)),
-            ],
-            out_specs=[out, out],
-        ),
+        in_specs=[pl.BlockSpec(memory_space=pltpu.SMEM), pl.BlockSpec(memory_space=pltpu.VMEM)]
+        + [hbm] * len(pieces),
         out_shape=[half, half],
+        scratch_shapes=[
+            pltpu.VMEM((NY, NZ, NX, n, part), BF) for part in (PART_B, PART_C)
+        ]
+        + [pltpu.SemaphoreType.DMA((16,))],
         name="project",
-    )(place, normed, w_rows)
-
-
-def per_device(queries, keys, values, gain, w_out):
-    devices = lax.axis_size("seq")
-    w_rows = lax.all_gather(w_out.T, "seq", axis=0, tiled=True)
+    )(place, normed, *pieces)
+
+
+def whole(queries, keys, values, gain, w_out):
+    devices = lax.axis_size(SEQ)
+    own = w_out.T
+    place = jnp.stack([lax.axis_index(a) for a in SEQ + ("head",)]).astype(jnp.int32)
+    parts_b, parts_c = gather(own, place)
     states = local_states(keys, values)
-    pieces = lax.all_to_all(states, "seq", 0, 0, tiled=True)
-    sums = exclusive_sums(pieces.reshape(devices, -1, DH))
-    prior = lax.all_to_all(sums.reshape(-1, DH), "seq", 0, 0, tiled=True)
+    shares = lax.all_to_all(states, SEQ, 0, 0, tiled=True)
+    sums = exclusive_sums(shares.reshape(devices, -1, DH))
+    prior = lax.all_to_all(sums.reshape(-1, DH), SEQ, 0, 0, tiled=True)
     normed = attention(queries, keys, values, prior, gain.reshape(1, -1))
-    place = lax.axis_index("head").astype(jnp.int32).reshape(1)
-    mine, theirs = project(place, normed, w_rows)
+    mine, theirs = project(place, normed, parts_b + parts_c)
     other = lax.ppermute(theirs, "head", [(0, 1), (1, 0)])
     return (mine + other).astype(BF)
 
 
 def solution(mesh):
+    torus = jax.sharding.Mesh(mesh.devices.reshape(NY, NZ, NX, 2), SEQ + ("head",))
     return jax.shard_map(
-        per_device,
-        mesh=mesh,
+        whole,
+        mesh=torus,
         in_specs=(
-            P("seq", "head"),
-            P("seq", "head"),
-            P("seq", "head"),
+            P(SEQ, "head"),
+            P(SEQ, "head"),
+            P(SEQ, "head"),
             P("head"),
-            P("head", "seq"),
+            P("head", SEQ),
         ),
-        out_specs=P(("seq", "head"), None),
+        out_specs=P(SEQ + ("head",), None),
         check_vma=False,
     )

time: 176 us -> 189 us (1.074)
  starting transfers between devices: 9.85 us -> 55.9 us
  blocking collectives: 34.2 us -> 0 us
  between operations: 13.4 us -> 0.17 us
  Pallas kernels: 23.6 us -> 32 us
  local copies, waits for them, and re-layouts: 0.79 us -> 3.78 us
  waiting for transfers between devices: 91.1 us -> 93.8 us
    ppermute x1 -> x26, waiting for transfers between devices: 3.25 us -> 93.8 us  [the longest x25 90.6 us: shift(): return lax.ppermute(block, SEQ, pairs)]
    all_gather x1 -> x0, waiting for transfers between devices: 71.2 us -> none  [per_device(): w_rows = lax.all_gather(w_out.T, 'seq', axis=0, tiled=True)]
    ppermute x1 -> x26, starting transfers between devices: 1.4 us -> 38.6 us  [the longest x25 36.1 us: shift(): return lax.ppermute(block, SEQ, pairs)]
    all_to_all x1 -> x0, blocking collectives: 34.2 us -> none  [per_device(): pieces = lax.all_to_all(states, 'seq', 0, 0, tiled=True)]
    all_to_all x1 -> x2, waiting for transfers between devices: 15.9 us -> 0.01 us  [the longest x1 0.01 us: whole(): shares = lax.all_to_all(states, SEQ, 0, 0, tiled=True)]
    all_to_all x1 -> x2, starting transfers between devices: 8.45 us -> 17.2 us  [the longest x1 8.76 us: whole(): shares = lax.all_to_all(states, SEQ, 0, 0, tiled=True)]
    pallas_call x1 -> x4, Pallas kernels: 11.2 us -> 19.5 us  [the longest x1 12.1 us: project(): pl.pallas_call(project_kernel, in_specs=[pl.BlockSpec(memory_space=pltpu....]
    unnamed x2 -> x38, local copies, waits for them, and re-layouts: 0.79 us -> 3.78 us
  transfers between devices with their start and end apart: 3 -> 28, of which waited for: 3 -> 14; matrix products, arithmetic and copies ran while one was open for 0% -> 0% of each run, Pallas kernels for 7% -> 8%
where the time goes in v2:
time: 189 us
  waiting for transfers between devices  93.8 us (50%)
  starting transfers between devices  55.9 us (30%)
  Pallas kernels  32 us (17%)
  local copies, waits for them, and re-layouts  3.78 us (2%)
  other arithmetic  3.12 us (2%)
    ppermute x25, waiting for transfers between devices, shift(): return lax.ppermute(block, SEQ, pairs)  90.6 us
    ppermute x25, starting transfers between devices, shift(): return lax.ppermute(block, SEQ, pairs)  36.1 us
    pallas_call x1, Pallas kernels, project(): pl.pallas_call(project_kernel, in_specs=[pl.BlockSpec(memory_space=pltpu....  12.1 us
    all_to_all x1, starting transfers between devices, whole(): shares = lax.all_to_all(states, SEQ, 0, 0, tiled=True)  8.76 us
    all_to_all x1, starting transfers between devices, whole(): prior = lax.all_to_all(sums.reshape(-1, DH), SEQ, 0, 0, tiled=True)  8.44 us
    pallas_call x3, Pallas kernels, assemble(): pl.pallas_call(kernel, in_specs=[pl.BlockSpec(memory_space=pltpu.SMEM)] +...  7.43 us
    pallas_call x1, Pallas kernels, attention(): pl.pallas_call(attention_kernel, grid=(cols // width,), in_specs=[spec, s...  6.46 us
    pallas_call x1, Pallas kernels, local_states(): pl.pallas_call(states_kernel, grid=(cols // width,), in_specs=[spec, spec...  3.94 us
  transfers between devices with their start and end apart: 28, of which 14 were waited for; matrix products, arithmetic and copies ran while one was open for 0% of the time, Pallas kernels for 8%

profile of v2, /device:TPU:1, one launch (start us, length us, event | category | flops | bytes accessed | tf_op | source)
XLA Modules:
  0.0 188.7 jit_solution(11738760820358826126)
XLA Ops:
  0.0 6.4 %collective-permute-start.6 = (bf16[24,2048]{1,0:T(8,128)(2,1)}, bf16[24,2048]{1,0:T(8,128)(2,1)S(1)}, u32[]{:S(2)}, u32[]{:S(2)}) collective-permute-start(bf16[24,2048]{1,0:T(8,128)(2,1)} %bitcast.10), channel_id=1, source_target_pairs={{0,56},{2,58},{4,60},{6,62},{8,0},{10,2},{12,4},{14,6},{16,8},{18,... | collective-permute-start | bytes 294920 | tf_op jit(solution)/shard_map/ppermute | solution.py:106
  6.4 1.2 collective-permute-start.5
  7.6 0.4 collective-permute-start.4
  8.0 4.5 %collective-permute-start.3 = (bf16[24,2048]{1,0:T(8,128)(2,1)}, bf16[24,2048]{1,0:T(8,128)(2,1)S(1)}, u32[]{:S(2)}, u32[]{:S(2)}) collective-permute-start(bf16[24,2048]{1,0:T(8,128)(2,1)} %bitcast.13), channel_id=1, source_target_pairs={{0,32},{2,34},{4,36},{6,38},{8,40},{10,42},{12,44},{14,46},{16,48}... | collective-permute-start | bytes 294920 | tf_op jit(solution)/shard_map/ppermute | solution.py:106
  12.5 0.0 collective-permute-start.2
  12.5 0.0 collective-permute-done.6.refs_7_
  12.5 2.1 %collective-permute-start.1 = (bf16[24,2048]{1,0:T(8,128)(2,1)}, bf16[24,2048]{1,0:T(8,128)(2,1)S(1)}, u32[]{:S(2)}, u32[]{:S(2)}) collective-permute-start(bf16[24,2048]{1,0:T(8,128)(2,1)} %bitcast.15), channel_id=1, source_target_pairs={{0,16},{2,18},{4,20},{6,22},{8,24},{10,26},{12,28},{14,30},{16,32}... | collective-permute-start | bytes 294920 | tf_op jit(solution)/shard_map/ppermute | solution.py:106
  14.6 0.0 collective-permute-done.5.refs_6_
  14.6 1.5 collective-permute-start
  16.0 0.6 pad_add_fusion.place_ref
  16.7 0.0 collective-permute-done.4.refs_5_
  16.7 1.7 collective-permute-done.3.refs_4_
  18.4 4.5 %collective-permute-done.2.refs_3_ = bf16[24,2048]{1,0:T(8,128)(2,1)S(1)} collective-permute-done((bf16[24,2048]{1,0:T(8,128)(2,1)}, bf16[24,2048]{1,0:T(8,128)(2,1)S(1)}, u32[]{:S(2)}, u32[]{:S(2)}) %collective-permute-start.2) | collective-permute-done | bytes 98336 | tf_op jit(solution)/shard_map/ppermute | solution.py:106
  22.9 5.0 %collective-permute-done.1.refs_2_ = bf16[24,2048]{1,0:T(8,128)(2,1)S(1)} collective-permute-done((bf16[24,2048]{1,0:T(8,128)(2,1)}, bf16[24,2048]{1,0:T(8,128)(2,1)S(1)}, u32[]{:S(2)}, u32[]{:S(2)}) %collective-permute-start.1) | collective-permute-done | bytes 98336 | tf_op jit(solution)/shard_map/ppermute | solution.py:106
  28.0 3.3 %collective-permute-done.refs_1_ = bf16[24,2048]{1,0:T(8,128)(2,1)S(1)} collective-permute-done((bf16[24,2048]{1,0:T(8,128)(2,1)}, bf16[24,2048]{1,0:T(8,128)(2,1)S(1)}, u32[]{:S(2)}, u32[]{:S(2)}) %collective-permute-start) | collective-permute-done | bytes 98336 | tf_op jit(solution)/shard_map/ppermute | solution.py:106
  31.3 0.6 copy-done.18
  32.0 2.2 %shard_map.55 = (bf16[8,24,1024]{2,1,0:T(8,128)(2,1)}, bf16[8,24,1024]{2,1,0:T(8,128)(2,1)}) custom-call(s32[4]{0:T(128)} %pad_add_fusion.place_ref, bf16[24,2048]{1,0:T(8,128)(2,1)} %bitcast.17, bf16[24,2048]{1,0:T(8,128)(2,1)} %copy-done.18, bf16[24,2048]{1,0:T(8,128)(2,1)} %copy-done.17, bf16[24,2048]{1,0:T(8,128)(2,1)} %copy-done.16, ...), custom_call_target="tpu_custom_call" | custom-call | tf_op jit(solution)/shard_map/pallas_call | solution.py:121
  34.1 2.5 %collective-permute-start.18 = (bf16[8,24,1024]{2,1,0:T(8,128)(2,1)}, bf16[8,24,1024]{2,1,0:T(8,128)(2,1)S(1)}, u32[]{:S(2)}, u32[]{:S(2)}) collective-permute-start(bf16[8,24,1024]{2,1,0:T(8,128)(2,1)} %get-tuple-element.16.refs_0_), channel_id=1, source_target_pairs={{0,6},{2,0},{4,2},{6,4},{8,14},{10,8},{12,10},{14,12},{16,22},{18,... | collective-permute-start | bytes 1179656 | tf_op jit(solution)/shard_map/ppermute | solution.py:106
  36.6 0.5 collective-permute-start.17
  37.1 0.6 collective-permute-start.16
  37.7 7.8 %collective-permute-done.18.refs_3_ = bf16[8,24,1024]{2,1,0:T(8,128)(2,1)S(1)} collective-permute-done((bf16[8,24,1024]{2,1,0:T(8,128)(2,1)}, bf16[8,24,1024]{2,1,0:T(8,128)(2,1)S(1)}, u32[]{:S(2)}, u32[]{:S(2)}) %collective-permute-start.18) | collective-permute-done | bytes 393248 | tf_op jit(solution)/shard_map/ppermute | solution.py:106
  45.5 2.6 %collective-permute-done.17.refs_2_ = bf16[8,24,1024]{2,1,0:T(8,128)(2,1)S(1)} collective-permute-done((bf16[8,24,1024]{2,1,0:T(8,128)(2,1)}, bf16[8,24,1024]{2,1,0:T(8,128)(2,1)S(1)}, u32[]{:S(2)}, u32[]{:S(2)}) %collective-permute-start.17) | collective-permute-done | bytes 393248 | tf_op jit(solution)/shard_map/ppermute | solution.py:106
  48.1 9.7 %collective-permute-done.16.refs_1_ = bf16[8,24,1024]{2,1,0:T(8,128)(2,1)S(1)} collective-permute-done((bf16[8,24,1024]{2,1,0:T(8,128)(2,1)}, bf16[8,24,1024]{2,1,0:T(8,128)(2,1)S(1)}, u32[]{:S(2)}, u32[]{:S(2)}) %collective-permute-start.16) | collective-permute-done | bytes 393248 | tf_op jit(solution)/shard_map/ppermute | solution.py:106
  57.8 0.8 copy-done.11
  58.5 2.7 %shard_map.57 = (bf16[4,4,24,1024]{3,2,1,0:T(8,128)(2,1)}, bf16[4,4,24,1024]{3,2,1,0:T(8,128)(2,1)}) custom-call(s32[4]{0:T(128)} %pad_add_fusion.place_ref, bf16[8,24,1024]{2,1,0:T(8,128)(2,1)} %get-tuple-element.16.refs_0_, bf16[8,24,1024]{2,1,0:T(8,128)(2,1)} %copy-done.11, bf16[8,24,1024]{2,1,0:T(8,128)(2,1)} %copy-done.10, bf16[8,24,1024]{2,1,0:T(8,128)(2,1)} %copy-done.9), custom_call_target="tpu_custom_call" | custom-call | tf_op jit(solution)/shard_map/pallas_call | solution.py:121
  61.2 2.7 %collective-permute-start.24 = (bf16[4,4,24,1024]{3,2,1,0:T(8,128)(2,1)}, bf16[4,4,24,1024]{3,2,1,0:T(8,128)(2,1)S(1)}, u32[]{:S(2)}, u32[]{:S(2)}) collective-permute-start(bf16[4,4,24,1024]{3,2,1,0:T(8,128)(2,1)} %get-tuple-element.17.refs_8_), channel_id=1, source_target_pairs={{0,192},{2,194},{4,196},{6,198},{8,200},{10,202},{12,204},{14,206}... | collective-permute-start | bytes 2359304 | tf_op jit(solution)/shard_map/ppermute | solution.py:106
  63.9 0.0 collective-permute-start.19
  63.9 3.9 %local_states.1 = bf16[2048,128]{1,0:T(8,128)(2,1)} custom-call(bf16[256,2048]{1,0:T(8,128)(2,1)} %k_ref.3, bf16[256,2048]{1,0:T(8,128)(2,1)} %v_ref.3), custom_call_target="tpu_custom_call" | custom-call | tf_op jit(solution)/shard_map/local_states/pallas_call | solution.py:28
  67.9 8.8 %all-to-all-start = ((bf16[128,16,128]{2,1,0:T(8,128)(2,1)}), bf16[128,16,128]{2,1,0:T(8,128)(2,1)S(1)}, u32[]{:S(2)}, u32[]{:S(2)}) async-start(bf16[128,16,128]{2,1,0:T(8,128)(2,1)} %bitcast.8), calls=%async_computation | async-start | bytes 1048576 | tf_op jit(solution)/shard_map/all_to_all | solution.py:220
  76.7 2.4 %collective-permute-start.9 = (bf16[8,24,1024]{2,1,0:T(8,128)(2,1)S(1)}, bf16[8,24,1024]{2,1,0:T(8,128)(2,1)S(1)}, u32[]{:S(2)}, u32[]{:S(2)}) collective-permute-start(bf16[8,24,1024]{2,1,0:T(8,128)(2,1)S(1)} %copy-done.6), channel_id=1, source_target_pairs={{0,192},{2,194},{4,196},{6,198},{8,200},{10,202},{12,204},{14,206}... | collective-permute-start | bytes 1179656 | tf_op jit(solution)/shard_map/ppermute | solution.py:106
  79.1 0.4 collective-permute-start.8
  79.4 0.6 collective-permute-start.7
  80.0 22.9 %collective-permute-done.9.refs_3_ = bf16[8,24,1024]{2,1,0:T(8,128)(2,1)S(1)} collective-permute-done((bf16[8,24,1024]{2,1,0:T(8,128)(2,1)S(1)}, bf16[8,24,1024]{2,1,0:T(8,128)(2,1)S(1)}, u32[]{:S(2)}, u32[]{:S(2)}) %collective-permute-start.9) | collective-permute-done | bytes 393248 | tf_op jit(solution)/shard_map/ppermute | solution.py:106
  102.9 3.6 %collective-permute-start.22 = (bf16[4,4,24,1024]{3,2,1,0:T(8,128)(2,1)S(1)}, bf16[4,4,24,1024]{3,2,1,0:T(8,128)(2,1)}, u32[]{:S(2)}, u32[]{:S(2)}) collective-permute-start(bf16[4,4,24,1024]{3,2,1,0:T(8,128)(2,1)S(1)} %copy-done.2), channel_id=1, source_target_pairs={{0,192},{2,194},{4,196},{6,198},{8,200},{10,202},{12,204},{14,206}... | collective-permute-start | bytes 2359304 | tf_op jit(solution)/shard_map/ppermute | solution.py:106
  106.4 0.0 collective-permute-done.8.refs_2_
  106.5 0.7 copy-done.8
  107.2 0.0 collective-permute-done.7.refs_1_
  107.2 2.6 %shard_map.56 = (bf16[4,4,24,1024]{3,2,1,0:T(8,128)(2,1)}, bf16[4,4,24,1024]{3,2,1,0:T(8,128)(2,1)}) custom-call(s32[4]{0:T(128)} %pad_add_fusion.place_ref, bf16[8,24,1024]{2,1,0:T(8,128)(2,1)} %get-tuple-element.13.refs_0_, bf16[8,24,1024]{2,1,0:T(8,128)(2,1)} %collective-permute-done.7.refs_1_, bf16[8,24,1024]{2,1,0:T(8,128)(2,1)} %copy-done.8, ...), custom_call_target="tpu_custom_call" | custom-call | tf_op jit(solution)/shard_map/pallas_call | solution.py:121
  109.8 1.5 collective-permute-start.10
  111.3 0.0 collective-permute-done.19.refs_10_
  111.3 1.3 collective-permute-start.13
  112.6 0.0 all-to-all-done.x_ref
  112.6 0.8 copy-done.1
  113.4 2.0 %exclusive_sums.1 = bf16[128,16,128]{2,1,0:T(8,128)(2,1)} custom-call(bf16[128,16,128]{2,1,0:T(8,128)(2,1)} %copy-done.1), custom_call_target="tpu_custom_call" | custom-call | tf_op jit(solution)/shard_map/exclusive_sums/pallas_call | solution.py:47
  115.4 8.4 %all-to-all-start.1 = ((bf16[128,16,128]{2,1,0:T(8,128)(2,1)}), bf16[128,16,128]{2,1,0:T(8,128)(2,1)S(1)}, u32[]{:S(2)}, u32[]{:S(2)}) async-start(bf16[128,16,128]{2,1,0:T(8,128)(2,1)} %exclusive_sums.1), calls=%async_computation.1 | async-start | bytes 1048576 | tf_op jit(solution)/shard_map/all_to_all | solution.py:222
  123.9 0.7 collective-permute-start.11
  124.5 0.7 collective-permute-done.20.refs_11_
  125.2 0.6 collective-permute-start.21
  125.8 2.2 %collective-permute-done.15.refs_6_ = bf16[4,4,24,1024]{3,2,1,0:T(8,128)(2,1)} collective-permute-done((bf16[4,4,24,1024]{3,2,1,0:T(8,128)(2,1)}, bf16[4,4,24,1024]{3,2,1,0:T(8,128)(2,1)}, u32[]{:S(2)}, u32[]{:S(2)}) %collective-permute-start.15) | collective-permute-done | bytes 786464 | tf_op jit(solution)/shard_map/ppermute | solution.py:106
  128.0 1.3 collective-permute-start.23
  129.4 0.5 collective-permute-done.10.refs_2_
  129.9 0.0 collective-permute-start.12
  129.9 19.5 %collective-permute-done.13.refs_7_ = bf16[4,4,24,1024]{3,2,1,0:T(8,128)(2,1)} collective-permute-done((bf16[4,4,24,1024]{3,2,1,0:T(8,128)(2,1)}, bf16[4,4,24,1024]{3,2,1,0:T(8,128)(2,1)}, u32[]{:S(2)}, u32[]{:S(2)}) %collective-permute-start.13) | collective-permute-done | bytes 786464 | tf_op jit(solution)/shard_map/ppermute | solution.py:106
  149.4 1.5 collective-permute-start.14
  150.9 0.0 all-to-all-done.1
  150.9 0.8 copy-done
  151.7 6.5 %attention.1.n_ref = bf16[256,2048]{1,0:T(8,128)(2,1)} custom-call(bf16[256,2048]{1,0:T(8,128)(2,1)} %q_ref.1, bf16[256,2048]{1,0:T(8,128)(2,1)} %k_ref.3, bf16[256,2048]{1,0:T(8,128)(2,1)} %v_ref.3, bf16[2048,128]{1,0:T(8,128)(2,1)} %bitcast.9, f32[1,2048]{1,0:T(1,128)} %bitcast.18), custom_call_target="tpu_custom_call" | custom-call | tf_op jit(solution)/shard_map/attention/pallas_call | solution.py:76
  158.1 0.0 collective-permute-done.11.refs_3_
  158.1 0.0 collective-permute-done.21.refs_12_
  158.1 10.1 %collective-permute-done.12.refs_4_ = bf16[4,4,24,1024]{3,2,1,0:T(8,128)(2,1)} collective-permute-done((bf16[4,4,24,1024]{3,2,1,0:T(8,128)(2,1)}, bf16[4,4,24,1024]{3,2,1,0:T(8,128)(2,1)}, u32[]{:S(2)}, u32[]{:S(2)}) %collective-permute-start.12) | collective-permute-done | bytes 786464 | tf_op jit(solution)/shard_map/ppermute | solution.py:106
  168.2 12.1 %project.1 = (f32[128,3072]{1,0:T(8,128)}, f32[128,3072]{1,0:T(8,128)}) custom-call(s32[4]{0:T(128)} %pad_add_fusion.place_ref, bf16[256,2048]{1,0:T(8,128)(2,1)} %attention.1.n_ref, bf16[4,4,24,1024]{3,2,1,0:T(8,128)(2,1)} %get-tuple-element.14.refs_0_, bf16[4,4,24,1024]{3,2,1,0:T(8,128)(2,1)} %get-tuple-element.15.refs_1_, ...), custom_call_target="tpu_custom_call" | custom-call | tf_op jit(solution)/shard_map/project/pallas_call | solution.py:201
  180.4 2.6 %collective-permute-start.25 = (f32[128,3072]{1,0:T(8,128)}, f32[128,3072]{1,0:T(8,128)S(1)}, u32[]{:S(2)}, u32[]{:S(2)}) collective-permute-start(f32[128,3072]{1,0:T(8,128)} %get-tuple-element.20), channel_id=1, source_target_pairs={{0,1},{1,0},{2,3},{3,2},{4,5},{5,4},{6,7},{7,6},{8,9},{9,8},{10,11... | collective-permute-start | bytes 4718600 | tf_op jit(solution)/shard_map/ppermute | solution.py:225
  182.9 3.2 %collective-permute-done.25 = f32[128,3072]{1,0:T(8,128)S(1)} collective-permute-done((f32[128,3072]{1,0:T(8,128)}, f32[128,3072]{1,0:T(8,128)S(1)}, u32[]{:S(2)}, u32[]{:S(2)}) %collective-permute-start.25) | collective-permute-done | bytes 1572896 | tf_op jit(solution)/shard_map/ppermute | solution.py:225
  186.2 2.5 %add_convert_fusion = bf16[128,3072]{1,0:T(8,128)(2,1)} fusion(f32[128,3072]{1,0:T(8,128)} %get-tuple-element.19, f32[128,3072]{1,0:T(8,128)S(1)} %collective-permute-done.25), kind=kLoop, calls=%fused_computation | loop fusion | flops 786432 | bytes 3932160 | tf_op jit(solution)/shard_map/convert_element_type | solution.py:226
  (39 shorter events, 0.1 us)
Async XLA Ops:
  0.0 12.5 %collective-permute-start.6 = (bf16[24,2048]{1,0:T(8,128)(2,1)}, bf16[24,2048]{1,0:T(8,128)(2,1)S(1)}, u32[]{:S(2)}, u32[]{:S(2)}) collective-permute-start(bf16[24,2048]{1,0:T(8,128)(2,1)} %bitcast.10), channel_id=1, source_target_pairs={{0,56},{2,58},{4,60},{6,62},{8,0},{10,2},{12,4},{14,6},{16,8},{18,... | collective-permute-start | bytes 294920 | tf_op jit(solution)/shard_map/ppermute | solution.py:106
  6.4 8.2 %collective-permute-start.5 = (bf16[24,2048]{1,0:T(8,128)(2,1)}, bf16[24,2048]{1,0:T(8,128)(2,1)S(1)}, u32[]{:S(2)}, u32[]{:S(2)}) collective-permute-start(bf16[24,2048]{1,0:T(8,128)(2,1)} %bitcast.11), channel_id=1, source_target_pairs={{0,48},{2,50},{4,52},{6,54},{8,56},{10,58},{12,60},{14,62},{16,0},... | collective-permute-start | bytes 294920 | tf_op jit(solution)/shard_map/ppermute | solution.py:106
  7.6 9.1 %collective-permute-start.4 = (bf16[24,2048]{1,0:T(8,128)(2,1)}, bf16[24,2048]{1,0:T(8,128)(2,1)S(1)}, u32[]{:S(2)}, u32[]{:S(2)}) collective-permute-start(bf16[24,2048]{1,0:T(8,128)(2,1)} %bitcast.12), channel_id=1, source_target_pairs={{0,40},{2,42},{4,44},{6,46},{8,48},{10,50},{12,52},{14,54},{16,56}... | collective-permute-start | bytes 294920 | tf_op jit(solution)/shard_map/ppermute | solution.py:106
  8.0 10.4 %collective-permute-start.3 = (bf16[24,2048]{1,0:T(8,128)(2,1)}, bf16[24,2048]{1,0:T(8,128)(2,1)S(1)}, u32[]{:S(2)}, u32[]{:S(2)}) collective-permute-start(bf16[24,2048]{1,0:T(8,128)(2,1)} %bitcast.13), channel_id=1, source_target_pairs={{0,32},{2,34},{4,36},{6,38},{8,40},{10,42},{12,44},{14,46},{16,48}... | collective-permute-start | bytes 294920 | tf_op jit(solution)/shard_map/ppermute | solution.py:106
  12.5 10.4 %collective-permute-start.2 = (bf16[24,2048]{1,0:T(8,128)(2,1)}, bf16[24,2048]{1,0:T(8,128)(2,1)S(1)}, u32[]{:S(2)}, u32[]{:S(2)}) collective-permute-start(bf16[24,2048]{1,0:T(8,128)(2,1)} %bitcast.14), channel_id=1, source_target_pairs={{0,24},{2,26},{4,28},{6,30},{8,32},{10,34},{12,36},{14,38},{16,40}... | collective-permute-start | bytes 294920 | tf_op jit(solution)/shard_map/ppermute | solution.py:106
  12.5 18.8 %copy-start.12 = (bf16[24,2048]{1,0:T(8,128)(2,1)}, bf16[24,2048]{1,0:T(8,128)(2,1)S(1)}, u32[]{:S(2)}) copy-start(bf16[24,2048]{1,0:T(8,128)(2,1)S(1)} %collective-permute-done.6.refs_7_) | copy-start | bytes 294916
  12.5 15.5 %collective-permute-start.1 = (bf16[24,2048]{1,0:T(8,128)(2,1)}, bf16[24,2048]{1,0:T(8,128)(2,1)S(1)}, u32[]{:S(2)}, u32[]{:S(2)}) collective-permute-start(bf16[24,2048]{1,0:T(8,128)(2,1)} %bitcast.15), channel_id=1, source_target_pairs={{0,16},{2,18},{4,20},{6,22},{8,24},{10,26},{12,28},{14,30},{16,32}... | collective-permute-start | bytes 294920 | tf_op jit(solution)/shard_map/ppermute | solution.py:106
  14.6 16.7 %copy-start.13 = (bf16[24,2048]{1,0:T(8,128)(2,1)}, bf16[24,2048]{1,0:T(8,128)(2,1)S(1)}, u32[]{:S(2)}) copy-start(bf16[24,2048]{1,0:T(8,128)(2,1)S(1)} %collective-permute-done.5.refs_6_) | copy-start | bytes 294916
  14.6 16.7 %collective-permute-start = (bf16[24,2048]{1,0:T(8,128)(2,1)}, bf16[24,2048]{1,0:T(8,128)(2,1)S(1)}, u32[]{:S(2)}, u32[]{:S(2)}) collective-permute-start(bf16[24,2048]{1,0:T(8,128)(2,1)} %bitcast.16), channel_id=1, source_target_pairs={{0,8},{2,10},{4,12},{6,14},{8,16},{10,18},{12,20},{14,22},{16,24},... | collective-permute-start | bytes 294920 | tf_op jit(solution)/shard_map/ppermute | solution.py:106
  16.7 14.6 %copy-start.14 = (bf16[24,2048]{1,0:T(8,128)(2,1)}, bf16[24,2048]{1,0:T(8,128)(2,1)S(1)}, u32[]{:S(2)}) copy-start(bf16[24,2048]{1,0:T(8,128)(2,1)S(1)} %collective-permute-done.4.refs_5_) | copy-start | bytes 294916
  18.4 12.9 %copy-start.15 = (bf16[24,2048]{1,0:T(8,128)(2,1)}, bf16[24,2048]{1,0:T(8,128)(2,1)S(1)}, u32[]{:S(2)}) copy-start(bf16[24,2048]{1,0:T(8,128)(2,1)S(1)} %collective-permute-done.3.refs_4_) | copy-start | bytes 294916
  22.9 8.4 %copy-start.16 = (bf16[24,2048]{1,0:T(8,128)(2,1)}, bf16[24,2048]{1,0:T(8,128)(2,1)S(1)}, u32[]{:S(2)}) copy-start(bf16[24,2048]{1,0:T(8,128)(2,1)S(1)} %collective-permute-done.2.refs_3_) | copy-start | bytes 294916
  28.0 3.3 %copy-start.17 = (bf16[24,2048]{1,0:T(8,128)(2,1)}, bf16[24,2048]{1,0:T(8,128)(2,1)S(1)}, u32[]{:S(2)}) copy-start(bf16[24,2048]{1,0:T(8,128)(2,1)S(1)} %collective-permute-done.1.refs_2_) | copy-start | bytes 294916
  31.3 0.6 copy-start.18
  34.1 11.4 %collective-permute-start.18 = (bf16[8,24,1024]{2,1,0:T(8,128)(2,1)}, bf16[8,24,1024]{2,1,0:T(8,128)(2,1)S(1)}, u32[]{:S(2)}, u32[]{:S(2)}) collective-permute-start(bf16[8,24,1024]{2,1,0:T(8,128)(2,1)} %get-tuple-element.16.refs_0_), channel_id=1, source_target_pairs={{0,6},{2,0},{4,2},{6,4},{8,14},{10,8},{12,10},{14,12},{16,22},{18,... | collective-permute-start | bytes 1179656 | tf_op jit(solution)/shard_map/ppermute | solution.py:106
  36.6 11.5 %collective-permute-start.17 = (bf16[8,24,1024]{2,1,0:T(8,128)(2,1)}, bf16[8,24,1024]{2,1,0:T(8,128)(2,1)S(1)}, u32[]{:S(2)}, u32[]{:S(2)}) collective-permute-start(bf16[8,24,1024]{2,1,0:T(8,128)(2,1)} %get-tuple-element.16.refs_0_), channel_id=1, source_target_pairs={{0,4},{2,6},{4,0},{6,2},{8,12},{10,14},{12,8},{14,10},{16,20},{18,... | collective-permute-start | bytes 1179656 | tf_op jit(solution)/shard_map/ppermute | solution.py:106
  37.1 20.7 %collective-permute-start.16 = (bf16[8,24,1024]{2,1,0:T(8,128)(2,1)}, bf16[8,24,1024]{2,1,0:T(8,128)(2,1)S(1)}, u32[]{:S(2)}, u32[]{:S(2)}) collective-permute-start(bf16[8,24,1024]{2,1,0:T(8,128)(2,1)} %get-tuple-element.16.refs_0_), channel_id=1, source_target_pairs={{0,2},{2,4},{4,6},{6,0},{8,10},{10,12},{12,14},{14,8},{16,18},{18,... | collective-permute-start | bytes 1179656 | tf_op jit(solution)/shard_map/ppermute | solution.py:106
  45.5 12.3 %copy-start.9 = (bf16[8,24,1024]{2,1,0:T(8,128)(2,1)}, bf16[8,24,1024]{2,1,0:T(8,128)(2,1)S(1)}, u32[]{:S(2)}) copy-start(bf16[8,24,1024]{2,1,0:T(8,128)(2,1)S(1)} %collective-permute-done.18.refs_3_) | copy-start | bytes 1179652
  48.1 9.7 %copy-start.10 = (bf16[8,24,1024]{2,1,0:T(8,128)(2,1)}, bf16[8,24,1024]{2,1,0:T(8,128)(2,1)S(1)}, u32[]{:S(2)}) copy-start(bf16[8,24,1024]{2,1,0:T(8,128)(2,1)S(1)} %collective-permute-done.17.refs_2_) | copy-start | bytes 1179652
  57.8 0.8 copy-start.11
  61.2 15.5 %copy-start.6 = (bf16[8,24,1024]{2,1,0:T(8,128)(2,1)S(1)}, bf16[8,24,1024]{2,1,0:T(8,128)(2,1)}, u32[]{:S(2)}) copy-start(bf16[8,24,1024]{2,1,0:T(8,128)(2,1)} %get-tuple-element.13.refs_0_) | copy-start | bytes 1179652
  61.2 41.7 %copy-start.2 = (bf16[4,4,24,1024]{3,2,1,0:T(8,128)(2,1)S(1)}, bf16[4,4,24,1024]{3,2,1,0:T(8,128)(2,1)}, u32[]{:S(2)}) copy-start(bf16[4,4,24,1024]{3,2,1,0:T(8,128)(2,1)} %get-tuple-element.18.refs_9_) | copy-start | bytes 2359300
  61.2 48.6 %collective-permute-start.24 = (bf16[4,4,24,1024]{3,2,1,0:T(8,128)(2,1)}, bf16[4,4,24,1024]{3,2,1,0:T(8,128)(2,1)S(1)}, u32[]{:S(2)}, u32[]{:S(2)}) collective-permute-start(bf16[4,4,24,1024]{3,2,1,0:T(8,128)(2,1)} %get-tuple-element.17.refs_8_), channel_id=1, source_target_pairs={{0,192},{2,194},{4,196},{6,198},{8,200},{10,202},{12,204},{14,206}... | collective-permute-start | bytes 2359304 | tf_op jit(solution)/shard_map/ppermute | solution.py:106
  63.9 47.3 %collective-permute-start.19 = (bf16[4,4,24,1024]{3,2,1,0:T(8,128)(2,1)}, bf16[4,4,24,1024]{3,2,1,0:T(8,128)(2,1)S(1)}, u32[]{:S(2)}, u32[]{:S(2)}) collective-permute-start(bf16[4,4,24,1024]{3,2,1,0:T(8,128)(2,1)} %get-tuple-element.17.refs_8_), channel_id=1, source_target_pairs={{0,64},{2,66},{4,68},{6,70},{8,72},{10,74},{12,76},{14,78},{16,80}... | collective-permute-start | bytes 2359304 | tf_op jit(solution)/shard_map/ppermute | solution.py:106
  67.9 44.7 %all-to-all-start = ((bf16[128,16,128]{2,1,0:T(8,128)(2,1)}), bf16[128,16,128]{2,1,0:T(8,128)(2,1)S(1)}, u32[]{:S(2)}, u32[]{:S(2)}) async-start(bf16[128,16,128]{2,1,0:T(8,128)(2,1)} %bitcast.8), calls=%async_computation | async-start | bytes 1048576 | tf_op jit(solution)/shard_map/all_to_all | solution.py:220
  76.7 26.2 %collective-permute-start.9 = (bf16[8,24,1024]{2,1,0:T(8,128)(2,1)S(1)}, bf16[8,24,1024]{2,1,0:T(8,128)(2,1)S(1)}, u32[]{:S(2)}, u32[]{:S(2)}) collective-permute-start(bf16[8,24,1024]{2,1,0:T(8,128)(2,1)S(1)} %copy-done.6), channel_id=1, source_target_pairs={{0,192},{2,194},{4,196},{6,198},{8,200},{10,202},{12,204},{14,206}... | collective-permute-start | bytes 1179656 | tf_op jit(solution)/shard_map/ppermute | solution.py:106
  79.1 27.4 %collective-permute-start.8 = (bf16[8,24,1024]{2,1,0:T(8,128)(2,1)S(1)}, bf16[8,24,1024]{2,1,0:T(8,128)(2,1)S(1)}, u32[]{:S(2)}, u32[]{:S(2)}) collective-permute-start(bf16[8,24,1024]{2,1,0:T(8,128)(2,1)S(1)} %copy-done.6), channel_id=1, source_target_pairs={{0,128},{2,130},{4,132},{6,134},{8,136},{10,138},{12,140},{14,142}... | collective-permute-start | bytes 1179656 | tf_op jit(solution)/shard_map/ppermute | solution.py:106
  79.4 27.8 %collective-permute-start.7 = (bf16[8,24,1024]{2,1,0:T(8,128)(2,1)S(1)}, bf16[8,24,1024]{2,1,0:T(8,128)(2,1)}, u32[]{:S(2)}, u32[]{:S(2)}) collective-permute-start(bf16[8,24,1024]{2,1,0:T(8,128)(2,1)S(1)} %copy-done.6), channel_id=1, source_target_pairs={{0,64},{2,66},{4,68},{6,70},{8,72},{10,74},{12,76},{14,78},{16,80}... | collective-permute-start | bytes 1179656 | tf_op jit(solution)/shard_map/ppermute | solution.py:106
  102.9 3.6 %copy-start.7 = (bf16[8,24,1024]{2,1,0:T(8,128)(2,1)}, bf16[8,24,1024]{2,1,0:T(8,128)(2,1)S(1)}, u32[]{:S(2)}) copy-start(bf16[8,24,1024]{2,1,0:T(8,128)(2,1)S(1)} %collective-permute-done.9.refs_3_) | copy-start | bytes 1179652
  102.9 21.0 %collective-permute-start.22 = (bf16[4,4,24,1024]{3,2,1,0:T(8,128)(2,1)S(1)}, bf16[4,4,24,1024]{3,2,1,0:T(8,128)(2,1)}, u32[]{:S(2)}, u32[]{:S(2)}) collective-permute-start(bf16[4,4,24,1024]{3,2,1,0:T(8,128)(2,1)S(1)} %copy-done.2), channel_id=1, source_target_pairs={{0,192},{2,194},{4,196},{6,198},{8,200},{10,202},{12,204},{14,206}... | collective-permute-start | bytes 2359304 | tf_op jit(solution)/shard_map/ppermute | solution.py:106
  106.5 0.7 copy-start.8
  106.5 18.8 %collective-permute-start.20 = (bf16[4,4,24,1024]{3,2,1,0:T(8,128)(2,1)S(1)}, bf16[4,4,24,1024]{3,2,1,0:T(8,128)(2,1)}, u32[]{:S(2)}, u32[]{:S(2)}) collective-permute-start(bf16[4,4,24,1024]{3,2,1,0:T(8,128)(2,1)S(1)} %copy-done.2), channel_id=1, source_target_pairs={{0,64},{2,66},{4,68},{6,70},{8,72},{10,74},{12,76},{14,78},{16,80}... | collective-permute-start | bytes 2359304 | tf_op jit(solution)/shard_map/ppermute | solution.py:106
  109.8 18.2 %collective-permute-start.15 = (bf16[4,4,24,1024]{3,2,1,0:T(8,128)(2,1)}, bf16[4,4,24,1024]{3,2,1,0:T(8,128)(2,1)}, u32[]{:S(2)}, u32[]{:S(2)}) collective-permute-start(bf16[4,4,24,1024]{3,2,1,0:T(8,128)(2,1)} %get-tuple-element.14.refs_0_), channel_id=1, source_target_pairs={{0,6},{2,0},{4,2},{6,4},{8,14},{10,8},{12,10},{14,12},{16,22},{18,... | collective-permute-start | bytes 2359304 | tf_op jit(solution)/shard_map/ppermute | solution.py:106
  109.8 58.4 %copy-start.3 = (bf16[4,4,24,1024]{3,2,1,0:T(8,128)(2,1)}, bf16[4,4,24,1024]{3,2,1,0:T(8,128)(2,1)S(1)}, u32[]{:S(2)}) copy-start(bf16[4,4,24,1024]{3,2,1,0:T(8,128)(2,1)S(1)} %collective-permute-done.24.refs_14_) | copy-start | bytes 2359300
  109.8 20.0 %collective-permute-start.10 = (bf16[4,4,24,1024]{3,2,1,0:T(8,128)(2,1)}, bf16[4,4,24,1024]{3,2,1,0:T(8,128)(2,1)}, u32[]{:S(2)}, u32[]{:S(2)}) collective-permute-start(bf16[4,4,24,1024]{3,2,1,0:T(8,128)(2,1)} %get-tuple-element.14.refs_0_), channel_id=1, source_target_pairs={{0,2},{2,4},{4,6},{6,0},{8,10},{10,12},{12,14},{14,8},{16,18},{18,... | collective-permute-start | bytes 2359304 | tf_op jit(solution)/shard_map/ppermute | solution.py:106
  111.3 57.0 %copy-start.4 = (bf16[4,4,24,1024]{3,2,1,0:T(8,128)(2,1)}, bf16[4,4,24,1024]{3,2,1,0:T(8,128)(2,1)S(1)}, u32[]{:S(2)}) copy-start(bf16[4,4,24,1024]{3,2,1,0:T(8,128)(2,1)S(1)} %collective-permute-done.19.refs_10_) | copy-start | bytes 2359300
  111.3 38.1 %collective-permute-start.13 = (bf16[4,4,24,1024]{3,2,1,0:T(8,128)(2,1)}, bf16[4,4,24,1024]{3,2,1,0:T(8,128)(2,1)}, u32[]{:S(2)}, u32[]{:S(2)}) collective-permute-start(bf16[4,4,24,1024]{3,2,1,0:T(8,128)(2,1)} %get-tuple-element.15.refs_1_), channel_id=1, source_target_pairs={{0,6},{2,0},{4,2},{6,4},{8,14},{10,8},{12,10},{14,12},{16,22},{18,... | collective-permute-start | bytes 2359304 | tf_op jit(solution)/shard_map/ppermute | solution.py:106
  112.6 0.8 copy-start.1
  115.4 35.4 %all-to-all-start.1 = ((bf16[128,16,128]{2,1,0:T(8,128)(2,1)}), bf16[128,16,128]{2,1,0:T(8,128)(2,1)S(1)}, u32[]{:S(2)}, u32[]{:S(2)}) async-start(bf16[128,16,128]{2,1,0:T(8,128)(2,1)} %exclusive_sums.1), calls=%async_computation.1 | async-start | bytes 1048576 | tf_op jit(solution)/shard_map/all_to_all | solution.py:222
  123.9 34.2 %collective-permute-start.11 = (bf16[4,4,24,1024]{3,2,1,0:T(8,128)(2,1)}, bf16[4,4,24,1024]{3,2,1,0:T(8,128)(2,1)}, u32[]{:S(2)}, u32[]{:S(2)}) collective-permute-start(bf16[4,4,24,1024]{3,2,1,0:T(8,128)(2,1)} %get-tuple-element.15.refs_1_), channel_id=1, source_target_pairs={{0,2},{2,4},{4,6},{6,0},{8,10},{10,12},{12,14},{14,8},{16,18},{18,... | collective-permute-start | bytes 2359304 | tf_op jit(solution)/shard_map/ppermute | solution.py:106
  125.2 32.9 %collective-permute-start.21 = (bf16[4,4,24,1024]{3,2,1,0:T(8,128)(2,1)S(1)}, bf16[4,4,24,1024]{3,2,1,0:T(8,128)(2,1)S(1)}, u32[]{:S(2)}, u32[]{:S(2)}) collective-permute-start(bf16[4,4,24,1024]{3,2,1,0:T(8,128)(2,1)S(1)} %collective-permute-done.19.refs_10_), channel_id=1, source_target_pairs={{0,64},{2,66},{4,68},{6,70},{8,72},{10,74},{12,76},{14,78},{16,80}... | collective-permute-start | bytes 2359304 | tf_op jit(solution)/shard_map/ppermute | solution.py:106
  128.0 30.1 %collective-permute-start.23 = (bf16[4,4,24,1024]{3,2,1,0:T(8,128)(2,1)}, bf16[4,4,24,1024]{3,2,1,0:T(8,128)(2,1)}, u32[]{:S(2)}, u32[]{:S(2)}) collective-permute-start(bf16[4,4,24,1024]{3,2,1,0:T(8,128)(2,1)} %collective-permute-done.22.refs_15_), channel_id=1, source_target_pairs={{0,192},{2,194},{4,196},{6,198},{8,200},{10,202},{12,204},{14,206}... | collective-permute-start | bytes 2359304 | tf_op jit(solution)/shard_map/ppermute | solution.py:106
  129.9 38.4 %collective-permute-start.12 = (bf16[4,4,24,1024]{3,2,1,0:T(8,128)(2,1)}, bf16[4,4,24,1024]{3,2,1,0:T(8,128)(2,1)}, u32[]{:S(2)}, u32[]{:S(2)}) collective-permute-start(bf16[4,4,24,1024]{3,2,1,0:T(8,128)(2,1)} %collective-permute-done.10.refs_2_), channel_id=1, source_target_pairs={{0,2},{2,4},{4,6},{6,0},{8,10},{10,12},{12,14},{14,8},{16,18},{18,... | collective-permute-start | bytes 2359304 | tf_op jit(solution)/shard_map/ppermute | solution.py:106
  149.4 18.9 %collective-permute-start.14 = (bf16[4,4,24,1024]{3,2,1,0:T(8,128)(2,1)}, bf16[4,4,24,1024]{3,2,1,0:T(8,128)(2,1)}, u32[]{:S(2)}, u32[]{:S(2)}) collective-permute-start(bf16[4,4,24,1024]{3,2,1,0:T(8,128)(2,1)} %collective-permute-done.13.refs_7_), channel_id=1, source_target_pairs={{0,6},{2,0},{4,2},{6,4},{8,14},{10,8},{12,10},{14,12},{16,22},{18,... | collective-permute-start | bytes 2359304 | tf_op jit(solution)/shard_map/ppermute | solution.py:106
  150.9 0.8 copy-start
  158.1 10.1 %copy-start.5 = (bf16[4,4,24,1024]{3,2,1,0:T(8,128)(2,1)}, bf16[4,4,24,1024]{3,2,1,0:T(8,128)(2,1)S(1)}, u32[]{:S(2)}) copy-start(bf16[4,4,24,1024]{3,2,1,0:T(8,128)(2,1)S(1)} %collective-permute-done.21.refs_12_) | copy-start | bytes 2359300
  180.4 5.8 %collective-permute-start.25 = (f32[128,3072]{1,0:T(8,128)}, f32[128,3072]{1,0:T(8,128)S(1)}, u32[]{:S(2)}, u32[]{:S(2)}) collective-permute-start(f32[128,3072]{1,0:T(8,128)} %get-tuple-element.20), channel_id=1, source_target_pairs={{0,1},{1,0},{2,3},{3,2},{4,5},{5,4},{6,7},{7,6},{8,9},{9,8},{10,11... | collective-permute-start | bytes 4718600 | tf_op jit(solution)/shard_map/ppermute | solution.py:225

commit v3 on v2

--- a/solution.py
+++ b/solution.py
@@ -8,7 +8,12 @@
 
 DH = 128
 BF = jnp.bfloat16
+SMALL = pltpu.CompilerParams(vmem_limit_bytes=16 << 20)
 F32 = jnp.float32
+
+
+def near(*arrays):
+    return [pltpu.with_memory_space_constraint(a, pltpu.VMEM) for a in arrays]
 
 
 def dot(a, b, dims):
@@ -31,6 +36,7 @@
         in_specs=[spec, spec],
         out_specs=pl.BlockSpec((width, DH), lambda i: (i, 0)),
         out_shape=jax.ShapeDtypeStruct((cols, DH), BF),
+        compiler_params=SMALL,
         name="local_states",
     )(keys, values)
 
@@ -46,9 +52,10 @@
 def exclusive_sums(pieces):
     return pl.pallas_call(
         running_kernel,
-        out_shape=jax.ShapeDtypeStruct(pieces.shape, BF),
+        out_shape=pltpu.VMEM(pieces.shape, BF),
+        compiler_params=SMALL,
         name="exclusive_sums",
-    )(pieces)
+    )(*near(pieces))
 
 
 def attention_kernel(q_ref, k_ref, v_ref, s_ref, g_ref, o_ref):
@@ -85,6 +92,7 @@
         ],
         out_specs=spec,
         out_shape=jax.ShapeDtypeStruct((rows, cols), BF),
+        compiler_params=SMALL,
         name="attention",
     )(queries, keys, values, prior, gain)
 
@@ -122,8 +130,9 @@
         kernel,
         in_specs=[pl.BlockSpec(memory_space=pltpu.SMEM)] + [vmem] * count,
         out_specs=[vmem] * len(outs),
-        out_shape=[jax.ShapeDtypeStruct(o, BF) for o in outs],
-    )(place, *pieces)
+        out_shape=[pltpu.VMEM(o, BF) for o in outs],
+        compiler_params=SMALL,
+    )(place, *near(*pieces))
 
 
 def both_ways(low, high, axis):
@@ -161,54 +170,98 @@
     return both_ways(*plane_b, "x"), both_ways(*plane_c, "y")
 
 
-def project_kernel(place_ref, n_ref, *refs):
-    pieces_b, pieces_c = refs[:8], refs[8:16]
-    mine_ref, theirs_ref, wb_ref, wc_ref, sems = refs[16:]
+def multiply(w, normed):
+    flat = w.reshape(w.shape[0] * w.shape[1] * w.shape[2], w.shape[3])
+    return dot(flat, normed, ((1,), (1,))).reshape(w.shape[:3] + normed.shape[:1])
+
+
+def split(terms, me):
+    rows = terms.shape[-1] // 2
+    first, second = terms[..., :rows], terms[..., rows:]
+    return jnp.where(me == 0, first, second), jnp.where(me == 0, second, first)
+
+
+def early_kernel(place_ref, n_ref, *refs):
+    pieces, (mine_ref, theirs_ref) = refs[:12], refs[12:]
     y, x, me = place_ref[0], place_ref[2], place_ref[3]
     half = NZ // 2
-    pairs = []
-    for by in range(4):
-        for part, lane in enumerate((slice(0, half), slice(half, NZ))):
-            pairs.append((pieces_b[2 * by + part], wb_ref.at[:, lane, wrap(x - by, NX)]))
-            pairs.append((pieces_c[2 * by + part], wc_ref.at[wrap(y - by, NY), lane]))
-    copies = [pltpu.make_async_copy(s, d, sems.at[i]) for i, (s, d) in enumerate(pairs)]
-    for copy in copies:
-        copy.start()
-    for copy in copies:
-        copy.wait()
-    rows = mine_ref.shape[0]
-    n = wb_ref.shape[3]
-    parts = ((wb_ref, n_ref[:, :PART_B]), (wc_ref, n_ref[:, PART_B:]))
-    wide = half * NX * n
-    for row in range(NY):
-        for start in (0, half):
-            terms = None
-            for w_ref, normed in parts:
-                w = w_ref[row, start : start + half].reshape(wide, normed.shape[1])
-                term = dot(normed, w, ((1,), (1,)))
-                terms = term if terms is None else terms + term
-            first, second = terms[:rows], terms[rows:]
-            at = slice((row * NZ + start) * NX * n, (row * NZ + start) * NX * n + wide)
-            mine_ref[:, at] = jnp.where(me == 0, first, second)
-            theirs_ref[:, at] = jnp.where(me == 0, second, first)
-
-
-def project(place, normed, pieces):
-    rows = normed.shape[0]
+    lanes = (slice(0, half), slice(half, NZ))
+    normed_b, normed_c = n_ref[:, :PART_B], n_ref[:, PART_B:]
+    for ref in (mine_ref, theirs_ref):
+        ref[:, :, wrap(x - 2, NX)] = jnp.zeros(ref.shape[:2] + ref.shape[3:], F32)
+    for i, by in enumerate((0, 1, 3)):
+        for part in (0, 1):
+            at = (slice(None), lanes[part], wrap(x - by, NX))
+            kept, sent = split(multiply(pieces[2 * i + part][...], normed_b), me)
+            mine_ref[at] = kept
+            theirs_ref[at] = sent
+    for i, by in enumerate((0, 1, 3)):
+        for part in (0, 1):
+            at = (wrap(y - by, NY), lanes[part])
+            kept, sent = split(multiply(pieces[6 + 2 * i + part][...], normed_c), me)
+            mine_ref[at] += kept
+            theirs_ref[at] += sent
+
+
+def late_kernel(place_ref, n_ref, _mine, _theirs, *refs):
+    pieces, (mine_ref, theirs_ref) = refs[:4], refs[4:]
+    y, x, me = place_ref[0], place_ref[2], place_ref[3]
+    half = NZ // 2
+    lanes = (slice(0, half), slice(half, NZ))
+    for part in (0, 1):
+        for at, piece, normed in (
+            ((slice(None), lanes[part], wrap(x - 2, NX)), pieces[part], n_ref[:, :PART_B]),
+            ((wrap(y - 2, NY), lanes[part]), pieces[2 + part], n_ref[:, PART_B:]),
+        ):
+            kept, sent = split(multiply(piece[...], normed), me)
+            mine_ref[at] += kept
+            theirs_ref[at] += sent
+
+
+def finish_kernel(mine_ref, other_ref, o_ref):
+    wide = o_ref.shape[0]
+    for start in range(0, o_ref.shape[1], wide):
+        at = slice(start, start + wide)
+        o_ref[:, at] = (mine_ref[at] + other_ref[at]).T.astype(BF)
+
+
+SMEM = pl.BlockSpec(memory_space=pltpu.SMEM)
+VMEM = pl.BlockSpec(memory_space=pltpu.VMEM)
+
+
+def project_early(place, normed, pieces):
     n = pieces[0].shape[2]
-    half = jax.ShapeDtypeStruct((rows // 2, NY * NZ * NX * n), F32)
-    hbm = pl.BlockSpec(memory_space=pl.ANY)
-    return pl.pallas_call(
-        project_kernel,
-        in_specs=[pl.BlockSpec(memory_space=pltpu.SMEM), pl.BlockSpec(memory_space=pltpu.VMEM)]
-        + [hbm] * len(pieces),
+    half = pltpu.VMEM((NY, NZ, NX, n, normed.shape[0] // 2), F32)
+    return pl.pallas_call(
+        early_kernel,
+        in_specs=[SMEM] + [VMEM] * 13,
+        out_specs=[VMEM, VMEM],
         out_shape=[half, half],
-        scratch_shapes=[
-            pltpu.VMEM((NY, NZ, NX, n, part), BF) for part in (PART_B, PART_C)
-        ]
-        + [pltpu.SemaphoreType.DMA((16,))],
-        name="project",
-    )(place, normed, *pieces)
+        compiler_params=SMALL,
+        name="project_early",
+    )(place, *near(normed, *pieces))
+
+
+def project_late(place, normed, terms, pieces):
+    half = pltpu.VMEM(terms[0].shape, F32)
+    return pl.pallas_call(
+        late_kernel,
+        in_specs=[SMEM] + [VMEM] * 7,
+        out_specs=[VMEM, VMEM],
+        out_shape=[half, half],
+        input_output_aliases={2: 0, 3: 1},
+        compiler_params=SMALL,
+        name="project_late",
+    )(place, *near(normed, *terms, *pieces))
+
+
+def finish(mine, other):
+    return pl.pallas_call(
+        finish_kernel,
+        out_shape=jax.ShapeDtypeStruct((mine.shape[1], mine.shape[0]), BF),
+        compiler_params=SMALL,
+        name="finish",
+    )(*near(mine, other))
 
 
 def whole(queries, keys, values, gain, w_out):
@@ -221,9 +274,13 @@
     sums = exclusive_sums(shares.reshape(devices, -1, DH))
     prior = lax.all_to_all(sums.reshape(-1, DH), SEQ, 0, 0, tiled=True)
     normed = attention(queries, keys, values, prior, gain.reshape(1, -1))
-    mine, theirs = project(place, normed, parts_b + parts_c)
+    early = parts_b[:4] + parts_b[6:] + parts_c[:4] + parts_c[6:]
+    late = parts_b[4:6] + parts_c[4:6]
+    terms = project_early(place, normed, early)
+    mine, theirs = project_late(place, normed, terms, late)
+    mine, theirs = (a.reshape(-1, a.shape[-1]) for a in (mine, theirs))
     other = lax.ppermute(theirs, "head", [(0, 1), (1, 0)])
-    return (mine + other).astype(BF)
+    return finish(mine, other)
 
 
 def solution(mesh):

time: 189 us -> 188 us (level)
  Pallas kernels: 32 us -> 21.8 us
  starting transfers between devices: 55.9 us -> 65.9 us
  other arithmetic: 3.12 us -> 0.08 us
    ppermute x25, starting transfers between devices: 36.1 us -> 42.3 us  [shift(): return lax.ppermute(block, SEQ, pairs)]
    pallas_call x3, Pallas kernels: 7.43 us -> 3.95 us  [assemble(): pl.pallas_call(kernel, in_specs=[pl.BlockSpec(memory_space=pltpu.SMEM)] +...]
    pallas_call x2 -> x4, Pallas kernels: 14.1 us -> 11 us  [the longest x1 6.14 us: project_early(): pl.pallas_call(early_kernel, in_specs=[SMEM] + [VMEM] * 13, out_specs=[VM...]
    convert_element_type x1 -> x0, other arithmetic: 2.51 us -> none  [whole(): return (mine + other).astype(BF)]
    all_to_all x1, starting transfers between devices: 8.76 us -> 10.7 us  [whole(): shares = lax.all_to_all(states, SEQ, 0, 0, tiled=True)]
    unnamed x38 -> x18, local copies, waits for them, and re-layouts: 3.78 us -> 3.87 us
  transfers between devices with their start and end apart: 28 -> 28, of which waited for: 14 -> 15; matrix products, arithmetic and copies ran while one was open for 0% -> 0% of each run, Pallas kernels for 8% -> 8%
where the time goes in v3:
time: 188 us; the launch traced here: 187 us
  waiting for transfers between devices  94.9 us (50%)
  starting transfers between devices  65.9 us (35%)
  Pallas kernels  21.8 us (12%)
  local copies, waits for them, and re-layouts  3.87 us (2%)
    ppermute x25, waiting for transfers between devices, shift(): return lax.ppermute(block, SEQ, pairs)  91.4 us
    ppermute x25, starting transfers between devices, shift(): return lax.ppermute(block, SEQ, pairs)  42.3 us
    all_to_all x1, starting transfers between devices, whole(): shares = lax.all_to_all(states, SEQ, 0, 0, tiled=True)  10.7 us
    all_to_all x1, starting transfers between devices, whole(): prior = lax.all_to_all(sums.reshape(-1, DH), SEQ, 0, 0, tiled=True)  9.85 us
    pallas_call x1, Pallas kernels, project_early(): pl.pallas_call(early_kernel, in_specs=[SMEM] + [VMEM] * 13, out_specs=[VM...  6.14 us
    pallas_call x1, Pallas kernels, attention(): pl.pallas_call(attention_kernel, grid=(cols // width,), in_specs=[spec, s...  4.6 us
    pallas_call x3, Pallas kernels, assemble(): pl.pallas_call(kernel, in_specs=[pl.BlockSpec(memory_space=pltpu.SMEM)] +...  3.95 us
    unnamed x18, local copies, waits for them, and re-layouts  3.87 us
  transfers between devices with their start and end apart: 28, of which 15 were waited for; matrix products, arithmetic and copies ran while one was open for 0% of the time, Pallas kernels for 8%

profile of v3, /device:TPU:1, one launch (start us, length us, event | category | flops | bytes accessed | tf_op | source)
XLA Modules:
  0.0 186.7 jit_solution(3537238657518294851)
XLA Ops:
  0.0 2.5 %collective-permute-start = (bf16[24,2048]{1,0:T(8,128)(2,1)}, bf16[24,2048]{1,0:T(8,128)(2,1)S(1)}, u32[]{:S(2)}, u32[]{:S(2)}) collective-permute-start(bf16[24,2048]{1,0:T(8,128)(2,1)} %bitcast.13), channel_id=1, source_target_pairs={{0,8},{2,10},{4,12},{6,14},{8,16},{10,18},{12,20},{14,22},{16,24},... | collective-permute-start | bytes 294920 | tf_op jit(solution)/shard_map/ppermute | solution.py:114
  2.5 3.0 %collective-permute-start.1 = (bf16[24,2048]{1,0:T(8,128)(2,1)}, bf16[24,2048]{1,0:T(8,128)(2,1)S(1)}, u32[]{:S(2)}, u32[]{:S(2)}) collective-permute-start(bf16[24,2048]{1,0:T(8,128)(2,1)} %bitcast.14), channel_id=1, source_target_pairs={{0,16},{2,18},{4,20},{6,22},{8,24},{10,26},{12,28},{14,30},{16,32}... | collective-permute-start | bytes 294920 | tf_op jit(solution)/shard_map/ppermute | solution.py:114
  5.5 3.8 %collective-permute-start.2 = (bf16[24,2048]{1,0:T(8,128)(2,1)}, bf16[24,2048]{1,0:T(8,128)(2,1)S(1)}, u32[]{:S(2)}, u32[]{:S(2)}) collective-permute-start(bf16[24,2048]{1,0:T(8,128)(2,1)} %bitcast.15), channel_id=1, source_target_pairs={{0,24},{2,26},{4,28},{6,30},{8,32},{10,34},{12,36},{14,38},{16,40}... | collective-permute-start | bytes 294920 | tf_op jit(solution)/shard_map/ppermute | solution.py:114
  9.2 0.5 collective-permute-start.3
  9.7 4.5 %collective-permute-start.4 = (bf16[24,2048]{1,0:T(8,128)(2,1)}, bf16[24,2048]{1,0:T(8,128)(2,1)S(1)}, u32[]{:S(2)}, u32[]{:S(2)}) collective-permute-start(bf16[24,2048]{1,0:T(8,128)(2,1)} %bitcast.17), channel_id=1, source_target_pairs={{0,40},{2,42},{4,44},{6,46},{8,48},{10,50},{12,52},{14,54},{16,56}... | collective-permute-start | bytes 294920 | tf_op jit(solution)/shard_map/ppermute | solution.py:114
  14.1 0.0 collective-permute-done.refs_1_
  14.1 2.4 %collective-permute-start.5 = (bf16[24,2048]{1,0:T(8,128)(2,1)}, bf16[24,2048]{1,0:T(8,128)(2,1)S(1)}, u32[]{:S(2)}, u32[]{:S(2)}) collective-permute-start(bf16[24,2048]{1,0:T(8,128)(2,1)} %bitcast.18), channel_id=1, source_target_pairs={{0,48},{2,50},{4,52},{6,54},{8,56},{10,58},{12,60},{14,62},{16,0},... | collective-permute-start | bytes 294920 | tf_op jit(solution)/shard_map/ppermute | solution.py:114
  16.5 0.0 collective-permute-done.1.refs_2_
  16.5 0.7 collective-permute-start.6
  17.3 0.1 pad_add_fusion.place_ref
  17.3 2.3 %collective-permute-done.2.refs_3_ = bf16[24,2048]{1,0:T(8,128)(2,1)S(1)} collective-permute-done((bf16[24,2048]{1,0:T(8,128)(2,1)}, bf16[24,2048]{1,0:T(8,128)(2,1)S(1)}, u32[]{:S(2)}, u32[]{:S(2)}) %collective-permute-start.2) | collective-permute-done | bytes 98336 | tf_op jit(solution)/shard_map/ppermute | solution.py:114
  19.6 2.0 %collective-permute-done.3.refs_4_ = bf16[24,2048]{1,0:T(8,128)(2,1)S(1)} collective-permute-done((bf16[24,2048]{1,0:T(8,128)(2,1)}, bf16[24,2048]{1,0:T(8,128)(2,1)S(1)}, u32[]{:S(2)}, u32[]{:S(2)}) %collective-permute-start.3) | collective-permute-done | bytes 98336 | tf_op jit(solution)/shard_map/ppermute | solution.py:114
  21.6 1.2 collective-permute-done.4.refs_5_
  22.8 6.5 %collective-permute-done.5.refs_6_ = bf16[24,2048]{1,0:T(8,128)(2,1)S(1)} collective-permute-done((bf16[24,2048]{1,0:T(8,128)(2,1)}, bf16[24,2048]{1,0:T(8,128)(2,1)S(1)}, u32[]{:S(2)}, u32[]{:S(2)}) %collective-permute-start.5) | collective-permute-done | bytes 98336 | tf_op jit(solution)/shard_map/ppermute | solution.py:114
  29.3 0.7 collective-permute-done.6.refs_7_
  30.1 0.9 copy-done.7
  30.9 0.6 shard_map.55
  31.6 0.0 copy-start.5
  31.6 0.7 copy-done.5
  32.3 1.2 collective-permute-start.14
  33.5 2.5 %collective-permute-start.15 = (bf16[8,24,1024]{2,1,0:T(8,128)(2,1)S(1)}, bf16[8,24,1024]{2,1,0:T(8,128)(2,1)S(1)}, u32[]{:S(2)}, u32[]{:S(2)}) collective-permute-start(bf16[8,24,1024]{2,1,0:T(8,128)(2,1)S(1)} %get-tuple-element.18.refs_0_), channel_id=1, source_target_pairs={{0,4},{2,6},{4,0},{6,2},{8,12},{10,14},{12,8},{14,10},{16,20},{18,... | collective-permute-start | bytes 1179656 | tf_op jit(solution)/shard_map/ppermute | solution.py:114
  36.0 1.2 collective-permute-start.16
  37.1 6.4 %collective-permute-done.14.refs_1_ = bf16[8,24,1024]{2,1,0:T(8,128)(2,1)S(1)} collective-permute-done((bf16[8,24,1024]{2,1,0:T(8,128)(2,1)S(1)}, bf16[8,24,1024]{2,1,0:T(8,128)(2,1)S(1)}, u32[]{:S(2)}, u32[]{:S(2)}) %collective-permute-start.14) | collective-permute-done | bytes 393248 | tf_op jit(solution)/shard_map/ppermute | solution.py:114
  43.5 9.4 %collective-permute-done.15.refs_2_ = bf16[8,24,1024]{2,1,0:T(8,128)(2,1)S(1)} collective-permute-done((bf16[8,24,1024]{2,1,0:T(8,128)(2,1)S(1)}, bf16[8,24,1024]{2,1,0:T(8,128)(2,1)S(1)}, u32[]{:S(2)}, u32[]{:S(2)}) %collective-permute-start.15) | collective-permute-done | bytes 393248 | tf_op jit(solution)/shard_map/ppermute | solution.py:114
  52.9 0.0 collective-permute-done.16.refs_3_
  52.9 1.6 shard_map.57
  54.5 1.3 collective-permute-start.17
  55.8 1.3 collective-permute-start.18
  57.1 2.3 %local_states.1 = bf16[2048,128]{1,0:T(8,128)(2,1)} custom-call(bf16[256,2048]{1,0:T(8,128)(2,1)S(1)} %copy-done, bf16[256,2048]{1,0:T(8,128)(2,1)S(1)} %copy-done.1), custom_call_target="tpu_custom_call" | custom-call | tf_op jit(solution)/shard_map/local_states/pallas_call | solution.py:33
  59.3 10.7 %all-to-all-start = ((bf16[128,16,128]{2,1,0:T(8,128)(2,1)}), bf16[128,16,128]{2,1,0:T(8,128)(2,1)S(1)}, u32[]{:S(2)}, u32[]{:S(2)}) async-start(bf16[128,16,128]{2,1,0:T(8,128)(2,1)} %bitcast.4), calls=%async_computation | async-start | bytes 1048576 | tf_op jit(solution)/shard_map/all_to_all | solution.py:273
  70.0 0.8 collective-permute-start.7
  70.8 2.8 %collective-permute-start.8 = (bf16[8,24,1024]{2,1,0:T(8,128)(2,1)}, bf16[8,24,1024]{2,1,0:T(8,128)(2,1)S(1)}, u32[]{:S(2)}, u32[]{:S(2)}) collective-permute-start(bf16[8,24,1024]{2,1,0:T(8,128)(2,1)} %copy-done.5), channel_id=1, source_target_pairs={{0,128},{2,130},{4,132},{6,134},{8,136},{10,138},{12,140},{14,142}... | collective-permute-start | bytes 1179656 | tf_op jit(solution)/shard_map/ppermute | solution.py:114
  73.6 1.0 collective-permute-start.9
  74.6 29.7 %collective-permute-done.7.refs_1_ = bf16[8,24,1024]{2,1,0:T(8,128)(2,1)S(1)} collective-permute-done((bf16[8,24,1024]{2,1,0:T(8,128)(2,1)}, bf16[8,24,1024]{2,1,0:T(8,128)(2,1)S(1)}, u32[]{:S(2)}, u32[]{:S(2)}) %collective-permute-start.7) | collective-permute-done | bytes 393248 | tf_op jit(solution)/shard_map/ppermute | solution.py:114
  104.3 1.4 collective-permute-start.19
  105.7 8.1 %collective-permute-done.8.refs_2_ = bf16[8,24,1024]{2,1,0:T(8,128)(2,1)S(1)} collective-permute-done((bf16[8,24,1024]{2,1,0:T(8,128)(2,1)}, bf16[8,24,1024]{2,1,0:T(8,128)(2,1)S(1)}, u32[]{:S(2)}, u32[]{:S(2)}) %collective-permute-start.8) | collective-permute-done | bytes 393248 | tf_op jit(solution)/shard_map/ppermute | solution.py:114
  113.8 0.0 collective-permute-start.20
  113.8 0.0 collective-permute-done.9.refs_3_
  113.8 1.0 copy-done.6
  114.8 1.8 shard_map.56
  116.6 1.8 collective-permute-start.10
  118.4 0.0 collective-permute-done.17.refs_8_
  118.4 0.0 collective-permute-start.11
  118.4 0.0 collective-permute-done.18.refs_9_
  118.4 2.7 %collective-permute-start.13 = (bf16[4,4,24,1024]{3,2,1,0:T(8,128)(2,1)}, bf16[4,4,24,1024]{3,2,1,0:T(8,128)(2,1)}, u32[]{:S(2)}, u32[]{:S(2)}) collective-permute-start(bf16[4,4,24,1024]{3,2,1,0:T(8,128)(2,1)} %get-tuple-element.17.refs_1_), channel_id=1, source_target_pairs={{0,6},{2,0},{4,2},{6,4},{8,14},{10,8},{12,10},{14,12},{16,22},{18,... | collective-permute-start | bytes 2359304 | tf_op jit(solution)/shard_map/ppermute | solution.py:114
  121.1 0.0 all-to-all-done.x_ref
  121.1 1.0 exclusive_sums.1
  122.1 9.8 %all-to-all-start.1 = ((bf16[128,16,128]{2,1,0:T(8,128)(2,1)}), bf16[128,16,128]{2,1,0:T(8,128)(2,1)S(1)}, u32[]{:S(2)}, u32[]{:S(2)}) async-start(bf16[128,16,128]{2,1,0:T(8,128)(2,1)} %exclusive_sums.1), calls=%async_computation.1 | async-start | bytes 1048576 | tf_op jit(solution)/shard_map/all_to_all | solution.py:275
  131.9 1.9 collective-permute-start.12
  133.8 4.0 %collective-permute-done.20.refs_11_ = bf16[4,4,24,1024]{3,2,1,0:T(8,128)(2,1)} collective-permute-done((bf16[4,4,24,1024]{3,2,1,0:T(8,128)(2,1)}, bf16[4,4,24,1024]{3,2,1,0:T(8,128)(2,1)}, u32[]{:S(2)}, u32[]{:S(2)}) %collective-permute-start.20) | collective-permute-done | bytes 786464 | tf_op jit(solution)/shard_map/ppermute | solution.py:114
  137.8 2.7 %collective-permute-start.24 = (bf16[4,4,24,1024]{3,2,1,0:T(8,128)(2,1)}, bf16[4,4,24,1024]{3,2,1,0:T(8,128)(2,1)}, u32[]{:S(2)}, u32[]{:S(2)}) collective-permute-start(bf16[4,4,24,1024]{3,2,1,0:T(8,128)(2,1)} %collective-permute-done.20.refs_11_), channel_id=1, source_target_pairs={{0,192},{2,194},{4,196},{6,198},{8,200},{10,202},{12,204},{14,206}... | collective-permute-start | bytes 2359304 | tf_op jit(solution)/shard_map/ppermute | solution.py:114
  140.5 17.5 %collective-permute-done.11.refs_3_ = bf16[4,4,24,1024]{3,2,1,0:T(8,128)(2,1)} collective-permute-done((bf16[4,4,24,1024]{3,2,1,0:T(8,128)(2,1)}, bf16[4,4,24,1024]{3,2,1,0:T(8,128)(2,1)}, u32[]{:S(2)}, u32[]{:S(2)}) %collective-permute-start.11) | collective-permute-done | bytes 786464 | tf_op jit(solution)/shard_map/ppermute | solution.py:114
  158.0 2.7 %collective-permute-start.22 = (bf16[4,4,24,1024]{3,2,1,0:T(8,128)(2,1)}, bf16[4,4,24,1024]{3,2,1,0:T(8,128)(2,1)}, u32[]{:S(2)}, u32[]{:S(2)}) collective-permute-start(bf16[4,4,24,1024]{3,2,1,0:T(8,128)(2,1)} %collective-permute-done.13.refs_5_), channel_id=1, source_target_pairs={{0,6},{2,0},{4,2},{6,4},{8,14},{10,8},{12,10},{14,12},{16,22},{18,... | collective-permute-start | bytes 2359304 | tf_op jit(solution)/shard_map/ppermute | solution.py:114
  160.7 0.5 all-to-all-done.1
  161.2 1.2 copy-done.2
  162.4 4.6 %attention.1.n_ref = bf16[256,2048]{1,0:T(8,128)(2,1)S(1)} custom-call(bf16[256,2048]{1,0:T(8,128)(2,1)S(1)} %copy-done.2, bf16[256,2048]{1,0:T(8,128)(2,1)S(1)} %copy-done, bf16[256,2048]{1,0:T(8,128)(2,1)S(1)} %copy-done.1, bf16[2048,128]{1,0:T(8,128)(2,1)S(1)} %bitcast.11, f32[1,2048]{1,0:T(1,128)S(1)} %bitcast.21), custom_call_target="tpu_custom_call" | custom-call | tf_op jit(solution)/shard_map/attention/pallas_call | solution.py:83
  167.1 6.1 %project_early.1 = (f32[4,8,4,24,128]{4,3,2,1,0:T(8,128)S(1)}, f32[4,8,4,24,128]{4,3,2,1,0:T(8,128)S(1)}) custom-call(s32[4]{0:T(128)S(1)} %pad_add_fusion.place_ref, bf16[256,2048]{1,0:T(8,128)(2,1)S(1)} %attention.1.n_ref, bf16[4,4,24,1024]{3,2,1,0:T(8,128)(2,1)} %get-tuple-element.16.refs_0_, bf16[4,4,24,1024]{3,2,1,0:T(8,128)(2,1)} %get-tuple-element.17.refs_1_, ...), custom_call_target="tpu_custom_call" | custom-call | tf_op jit(solution)/shard_map/project_early/pallas_call | solution.py:235
  173.2 0.0 collective-permute-done.24.refs_3_
  173.2 2.2 %collective-permute-done.21.refs_0_ = bf16[4,4,24,1024]{3,2,1,0:T(8,128)(2,1)} collective-permute-done((bf16[4,4,24,1024]{3,2,1,0:T(8,128)(2,1)}, bf16[4,4,24,1024]{3,2,1,0:T(8,128)(2,1)}, u32[]{:S(2)}, u32[]{:S(2)}) %collective-permute-start.21) | collective-permute-done | bytes 786464 | tf_op jit(solution)/shard_map/ppermute | solution.py:114
  175.4 1.3 collective-permute-done.22.refs_1_
  176.7 2.7 %project_late.1 = (f32[4,8,4,24,128]{4,3,2,1,0:T(8,128)S(1)}, f32[4,8,4,24,128]{4,3,2,1,0:T(8,128)S(1)}) custom-call(s32[4]{0:T(128)S(1)} %pad_add_fusion.place_ref, bf16[256,2048]{1,0:T(8,128)(2,1)S(1)} %attention.1.n_ref, f32[4,8,4,24,128]{4,3,2,1,0:T(8,128)S(1)} %get-tuple-element.21._mine, ...), custom_call_target="tpu_custom_call", output_to_operand_aliasing={{0}: (2, {}), {1}: (3, {})} | custom-call | tf_op jit(solution)/shard_map/project_late/pallas_call | solution.py:247
  179.4 3.1 %collective-permute-start.25 = (f32[3072,128]{1,0:T(8,128)S(1)}, f32[3072,128]{1,0:T(8,128)S(1)}, u32[]{:S(2)}, u32[]{:S(2)}) collective-permute-start(f32[3072,128]{1,0:T(8,128)S(1)} %bitcast.12), channel_id=1, source_target_pairs={{0,1},{1,0},{2,3},{3,2},{4,5},{5,4},{6,7},{7,6},{8,9},{9,8},{10,11... | collective-permute-start | bytes 4718600 | tf_op jit(solution)/shard_map/ppermute | solution.py:282
  182.5 3.0 %collective-permute-done.25.other_ref = f32[3072,128]{1,0:T(8,128)S(1)} collective-permute-done((f32[3072,128]{1,0:T(8,128)S(1)}, f32[3072,128]{1,0:T(8,128)S(1)}, u32[]{:S(2)}, u32[]{:S(2)}) %collective-permute-start.25) | collective-permute-done | bytes 1572896 | tf_op jit(solution)/shard_map/ppermute | solution.py:282
  185.6 1.2 finish.1
  (20 shorter events, 0.0 us)
Async XLA Ops:
  0.0 57.1 %copy-start = (bf16[256,2048]{1,0:T(8,128)(2,1)S(1)}, bf16[256,2048]{1,0:T(8,128)(2,1)}, u32[]{:S(2)}) copy-start(bf16[256,2048]{1,0:T(8,128)(2,1)} %k_ref.3) | copy-start | bytes 3145732
  0.0 57.1 %copy-start.1 = (bf16[256,2048]{1,0:T(8,128)(2,1)S(1)}, bf16[256,2048]{1,0:T(8,128)(2,1)}, u32[]{:S(2)}) copy-start(bf16[256,2048]{1,0:T(8,128)(2,1)} %v_ref.3) | copy-start | bytes 3145732
  0.0 14.1 %collective-permute-start = (bf16[24,2048]{1,0:T(8,128)(2,1)}, bf16[24,2048]{1,0:T(8,128)(2,1)S(1)}, u32[]{:S(2)}, u32[]{:S(2)}) collective-permute-start(bf16[24,2048]{1,0:T(8,128)(2,1)} %bitcast.13), channel_id=1, source_target_pairs={{0,8},{2,10},{4,12},{6,14},{8,16},{10,18},{12,20},{14,22},{16,24},... | collective-permute-start | bytes 294920 | tf_op jit(solution)/shard_map/ppermute | solution.py:114
  2.5 14.1 %collective-permute-start.1 = (bf16[24,2048]{1,0:T(8,128)(2,1)}, bf16[24,2048]{1,0:T(8,128)(2,1)S(1)}, u32[]{:S(2)}, u32[]{:S(2)}) collective-permute-start(bf16[24,2048]{1,0:T(8,128)(2,1)} %bitcast.14), channel_id=1, source_target_pairs={{0,16},{2,18},{4,20},{6,22},{8,24},{10,26},{12,28},{14,30},{16,32}... | collective-permute-start | bytes 294920 | tf_op jit(solution)/shard_map/ppermute | solution.py:114
  5.5 14.2 %collective-permute-start.2 = (bf16[24,2048]{1,0:T(8,128)(2,1)}, bf16[24,2048]{1,0:T(8,128)(2,1)S(1)}, u32[]{:S(2)}, u32[]{:S(2)}) collective-permute-start(bf16[24,2048]{1,0:T(8,128)(2,1)} %bitcast.15), channel_id=1, source_target_pairs={{0,24},{2,26},{4,28},{6,30},{8,32},{10,34},{12,36},{14,38},{16,40}... | collective-permute-start | bytes 294920 | tf_op jit(solution)/shard_map/ppermute | solution.py:114
  9.2 12.4 %collective-permute-start.3 = (bf16[24,2048]{1,0:T(8,128)(2,1)}, bf16[24,2048]{1,0:T(8,128)(2,1)S(1)}, u32[]{:S(2)}, u32[]{:S(2)}) collective-permute-start(bf16[24,2048]{1,0:T(8,128)(2,1)} %bitcast.16), channel_id=1, source_target_pairs={{0,32},{2,34},{4,36},{6,38},{8,40},{10,42},{12,44},{14,46},{16,48}... | collective-permute-start | bytes 294920 | tf_op jit(solution)/shard_map/ppermute | solution.py:114
  9.7 13.1 %collective-permute-start.4 = (bf16[24,2048]{1,0:T(8,128)(2,1)}, bf16[24,2048]{1,0:T(8,128)(2,1)S(1)}, u32[]{:S(2)}, u32[]{:S(2)}) collective-permute-start(bf16[24,2048]{1,0:T(8,128)(2,1)} %bitcast.17), channel_id=1, source_target_pairs={{0,40},{2,42},{4,44},{6,46},{8,48},{10,50},{12,52},{14,54},{16,56}... | collective-permute-start | bytes 294920 | tf_op jit(solution)/shard_map/ppermute | solution.py:114
  14.1 15.2 %collective-permute-start.5 = (bf16[24,2048]{1,0:T(8,128)(2,1)}, bf16[24,2048]{1,0:T(8,128)(2,1)S(1)}, u32[]{:S(2)}, u32[]{:S(2)}) collective-permute-start(bf16[24,2048]{1,0:T(8,128)(2,1)} %bitcast.18), channel_id=1, source_target_pairs={{0,48},{2,50},{4,52},{6,54},{8,56},{10,58},{12,60},{14,62},{16,0},... | collective-permute-start | bytes 294920 | tf_op jit(solution)/shard_map/ppermute | solution.py:114
  16.5 13.5 %collective-permute-start.6 = (bf16[24,2048]{1,0:T(8,128)(2,1)}, bf16[24,2048]{1,0:T(8,128)(2,1)S(1)}, u32[]{:S(2)}, u32[]{:S(2)}) collective-permute-start(bf16[24,2048]{1,0:T(8,128)(2,1)} %bitcast.19), channel_id=1, source_target_pairs={{0,56},{2,58},{4,60},{6,62},{8,0},{10,2},{12,4},{14,6},{16,8},{18,... | collective-permute-start | bytes 294920 | tf_op jit(solution)/shard_map/ppermute | solution.py:114
  30.1 0.9 copy-start.7
  31.6 0.7 copy-start.5
  32.3 11.2 %collective-permute-start.14 = (bf16[8,24,1024]{2,1,0:T(8,128)(2,1)S(1)}, bf16[8,24,1024]{2,1,0:T(8,128)(2,1)S(1)}, u32[]{:S(2)}, u32[]{:S(2)}) collective-permute-start(bf16[8,24,1024]{2,1,0:T(8,128)(2,1)S(1)} %get-tuple-element.18.refs_0_), channel_id=1, source_target_pairs={{0,2},{2,4},{4,6},{6,0},{8,10},{10,12},{12,14},{14,8},{16,18},{18,... | collective-permute-start | bytes 1179656 | tf_op jit(solution)/shard_map/ppermute | solution.py:114
  33.5 19.4 %collective-permute-start.15 = (bf16[8,24,1024]{2,1,0:T(8,128)(2,1)S(1)}, bf16[8,24,1024]{2,1,0:T(8,128)(2,1)S(1)}, u32[]{:S(2)}, u32[]{:S(2)}) collective-permute-start(bf16[8,24,1024]{2,1,0:T(8,128)(2,1)S(1)} %get-tuple-element.18.refs_0_), channel_id=1, source_target_pairs={{0,4},{2,6},{4,0},{6,2},{8,12},{10,14},{12,8},{14,10},{16,20},{18,... | collective-permute-start | bytes 1179656 | tf_op jit(solution)/shard_map/ppermute | solution.py:114
  36.0 17.0 %collective-permute-start.16 = (bf16[8,24,1024]{2,1,0:T(8,128)(2,1)S(1)}, bf16[8,24,1024]{2,1,0:T(8,128)(2,1)S(1)}, u32[]{:S(2)}, u32[]{:S(2)}) collective-permute-start(bf16[8,24,1024]{2,1,0:T(8,128)(2,1)S(1)} %get-tuple-element.18.refs_0_), channel_id=1, source_target_pairs={{0,6},{2,0},{4,2},{6,4},{8,14},{10,8},{12,10},{14,12},{16,22},{18,... | collective-permute-start | bytes 1179656 | tf_op jit(solution)/shard_map/ppermute | solution.py:114
  54.5 49.8 %copy-start.3 = (bf16[4,4,24,1024]{3,2,1,0:T(8,128)(2,1)}, bf16[4,4,24,1024]{3,2,1,0:T(8,128)(2,1)S(1)}, u32[]{:S(2)}) copy-start(bf16[4,4,24,1024]{3,2,1,0:T(8,128)(2,1)S(1)} %get-tuple-element.19.refs_6_) | copy-start | bytes 2359300
  54.5 63.9 %collective-permute-start.17 = (bf16[4,4,24,1024]{3,2,1,0:T(8,128)(2,1)S(1)}, bf16[4,4,24,1024]{3,2,1,0:T(8,128)(2,1)}, u32[]{:S(2)}, u32[]{:S(2)}) collective-permute-start(bf16[4,4,24,1024]{3,2,1,0:T(8,128)(2,1)S(1)} %get-tuple-element.19.refs_6_), channel_id=1, source_target_pairs={{0,64},{2,66},{4,68},{6,70},{8,72},{10,74},{12,76},{14,78},{16,80}... | collective-permute-start | bytes 2359304 | tf_op jit(solution)/shard_map/ppermute | solution.py:114
  55.8 62.7 %collective-permute-start.18 = (bf16[4,4,24,1024]{3,2,1,0:T(8,128)(2,1)}, bf16[4,4,24,1024]{3,2,1,0:T(8,128)(2,1)}, u32[]{:S(2)}, u32[]{:S(2)}) collective-permute-start(bf16[4,4,24,1024]{3,2,1,0:T(8,128)(2,1)} %get-tuple-element.20.refs_7_), channel_id=1, source_target_pairs={{0,64},{2,66},{4,68},{6,70},{8,72},{10,74},{12,76},{14,78},{16,80}... | collective-permute-start | bytes 2359304 | tf_op jit(solution)/shard_map/ppermute | solution.py:114
  59.3 101.9 %copy-start.8 = (f32[2048]{0:T(1024)S(1)}, f32[2048]{0:T(1024)}, u32[]{:S(2)}) copy-start(f32[2048]{0:T(1024)} %param.8) | copy-start | bytes 24580
  59.3 61.8 %all-to-all-start = ((bf16[128,16,128]{2,1,0:T(8,128)(2,1)}), bf16[128,16,128]{2,1,0:T(8,128)(2,1)S(1)}, u32[]{:S(2)}, u32[]{:S(2)}) async-start(bf16[128,16,128]{2,1,0:T(8,128)(2,1)} %bitcast.4), calls=%async_computation | async-start | bytes 1048576 | tf_op jit(solution)/shard_map/all_to_all | solution.py:273
  70.0 34.3 %collective-permute-start.7 = (bf16[8,24,1024]{2,1,0:T(8,128)(2,1)}, bf16[8,24,1024]{2,1,0:T(8,128)(2,1)S(1)}, u32[]{:S(2)}, u32[]{:S(2)}) collective-permute-start(bf16[8,24,1024]{2,1,0:T(8,128)(2,1)} %copy-done.5), channel_id=1, source_target_pairs={{0,64},{2,66},{4,68},{6,70},{8,72},{10,74},{12,76},{14,78},{16,80}... | collective-permute-start | bytes 1179656 | tf_op jit(solution)/shard_map/ppermute | solution.py:114
  70.8 43.1 %collective-permute-start.8 = (bf16[8,24,1024]{2,1,0:T(8,128)(2,1)}, bf16[8,24,1024]{2,1,0:T(8,128)(2,1)S(1)}, u32[]{:S(2)}, u32[]{:S(2)}) collective-permute-start(bf16[8,24,1024]{2,1,0:T(8,128)(2,1)} %copy-done.5), channel_id=1, source_target_pairs={{0,128},{2,130},{4,132},{6,134},{8,136},{10,138},{12,140},{14,142}... | collective-permute-start | bytes 1179656 | tf_op jit(solution)/shard_map/ppermute | solution.py:114
  73.6 40.2 %collective-permute-start.9 = (bf16[8,24,1024]{2,1,0:T(8,128)(2,1)}, bf16[8,24,1024]{2,1,0:T(8,128)(2,1)S(1)}, u32[]{:S(2)}, u32[]{:S(2)}) collective-permute-start(bf16[8,24,1024]{2,1,0:T(8,128)(2,1)} %copy-done.5), channel_id=1, source_target_pairs={{0,192},{2,194},{4,196},{6,198},{8,200},{10,202},{12,204},{14,206}... | collective-permute-start | bytes 1179656 | tf_op jit(solution)/shard_map/ppermute | solution.py:114
  104.3 27.7 %collective-permute-start.19 = (bf16[4,4,24,1024]{3,2,1,0:T(8,128)(2,1)S(1)}, bf16[4,4,24,1024]{3,2,1,0:T(8,128)(2,1)}, u32[]{:S(2)}, u32[]{:S(2)}) collective-permute-start(bf16[4,4,24,1024]{3,2,1,0:T(8,128)(2,1)S(1)} %get-tuple-element.19.refs_6_), channel_id=1, source_target_pairs={{0,192},{2,194},{4,196},{6,198},{8,200},{10,202},{12,204},{14,206}... | collective-permute-start | bytes 2359304 | tf_op jit(solution)/shard_map/ppermute | solution.py:114
  113.8 24.0 %collective-permute-start.20 = (bf16[4,4,24,1024]{3,2,1,0:T(8,128)(2,1)}, bf16[4,4,24,1024]{3,2,1,0:T(8,128)(2,1)}, u32[]{:S(2)}, u32[]{:S(2)}) collective-permute-start(bf16[4,4,24,1024]{3,2,1,0:T(8,128)(2,1)} %get-tuple-element.20.refs_7_), channel_id=1, source_target_pairs={{0,192},{2,194},{4,196},{6,198},{8,200},{10,202},{12,204},{14,206}... | collective-permute-start | bytes 2359304 | tf_op jit(solution)/shard_map/ppermute | solution.py:114
  113.8 1.0 copy-start.6
  116.6 21.2 %collective-permute-start.10 = (bf16[4,4,24,1024]{3,2,1,0:T(8,128)(2,1)}, bf16[4,4,24,1024]{3,2,1,0:T(8,128)(2,1)}, u32[]{:S(2)}, u32[]{:S(2)}) collective-permute-start(bf16[4,4,24,1024]{3,2,1,0:T(8,128)(2,1)} %get-tuple-element.16.refs_0_), channel_id=1, source_target_pairs={{0,2},{2,4},{4,6},{6,0},{8,10},{10,12},{12,14},{14,8},{16,18},{18,... | collective-permute-start | bytes 2359304 | tf_op jit(solution)/shard_map/ppermute | solution.py:114
  118.4 39.6 %collective-permute-start.11 = (bf16[4,4,24,1024]{3,2,1,0:T(8,128)(2,1)}, bf16[4,4,24,1024]{3,2,1,0:T(8,128)(2,1)}, u32[]{:S(2)}, u32[]{:S(2)}) collective-permute-start(bf16[4,4,24,1024]{3,2,1,0:T(8,128)(2,1)} %get-tuple-element.17.refs_1_), channel_id=1, source_target_pairs={{0,2},{2,4},{4,6},{6,0},{8,10},{10,12},{12,14},{14,8},{16,18},{18,... | collective-permute-start | bytes 2359304 | tf_op jit(solution)/shard_map/ppermute | solution.py:114
  118.4 39.6 %collective-permute-start.13 = (bf16[4,4,24,1024]{3,2,1,0:T(8,128)(2,1)}, bf16[4,4,24,1024]{3,2,1,0:T(8,128)(2,1)}, u32[]{:S(2)}, u32[]{:S(2)}) collective-permute-start(bf16[4,4,24,1024]{3,2,1,0:T(8,128)(2,1)} %get-tuple-element.17.refs_1_), channel_id=1, source_target_pairs={{0,6},{2,0},{4,2},{6,4},{8,14},{10,8},{12,10},{14,12},{16,22},{18,... | collective-permute-start | bytes 2359304 | tf_op jit(solution)/shard_map/ppermute | solution.py:114
  122.1 39.1 %all-to-all-start.1 = ((bf16[128,16,128]{2,1,0:T(8,128)(2,1)}), bf16[128,16,128]{2,1,0:T(8,128)(2,1)S(1)}, u32[]{:S(2)}, u32[]{:S(2)}) async-start(bf16[128,16,128]{2,1,0:T(8,128)(2,1)} %exclusive_sums.1), calls=%async_computation.1 | async-start | bytes 1048576 | tf_op jit(solution)/shard_map/all_to_all | solution.py:275
  131.9 35.1 %collective-permute-start.12 = (bf16[4,4,24,1024]{3,2,1,0:T(8,128)(2,1)}, bf16[4,4,24,1024]{3,2,1,0:T(8,128)(2,1)}, u32[]{:S(2)}, u32[]{:S(2)}) collective-permute-start(bf16[4,4,24,1024]{3,2,1,0:T(8,128)(2,1)} %get-tuple-element.16.refs_0_), channel_id=1, source_target_pairs={{0,6},{2,0},{4,2},{6,4},{8,14},{10,8},{12,10},{14,12},{16,22},{18,... | collective-permute-start | bytes 2359304 | tf_op jit(solution)/shard_map/ppermute | solution.py:114
  137.8 35.4 %collective-permute-start.23 = (bf16[4,4,24,1024]{3,2,1,0:T(8,128)(2,1)}, bf16[4,4,24,1024]{3,2,1,0:T(8,128)(2,1)S(1)}, u32[]{:S(2)}, u32[]{:S(2)}) collective-permute-start(bf16[4,4,24,1024]{3,2,1,0:T(8,128)(2,1)} %collective-permute-done.17.refs_8_), channel_id=1, source_target_pairs={{0,64},{2,66},{4,68},{6,70},{8,72},{10,74},{12,76},{14,78},{16,80}... | collective-permute-start | bytes 2359304 | tf_op jit(solution)/shard_map/ppermute | solution.py:114
  137.8 35.4 %collective-permute-start.24 = (bf16[4,4,24,1024]{3,2,1,0:T(8,128)(2,1)}, bf16[4,4,24,1024]{3,2,1,0:T(8,128)(2,1)}, u32[]{:S(2)}, u32[]{:S(2)}) collective-permute-start(bf16[4,4,24,1024]{3,2,1,0:T(8,128)(2,1)} %collective-permute-done.20.refs_11_), channel_id=1, source_target_pairs={{0,192},{2,194},{4,196},{6,198},{8,200},{10,202},{12,204},{14,206}... | collective-permute-start | bytes 2359304 | tf_op jit(solution)/shard_map/ppermute | solution.py:114
  158.0 17.4 %collective-permute-start.21 = (bf16[4,4,24,1024]{3,2,1,0:T(8,128)(2,1)}, bf16[4,4,24,1024]{3,2,1,0:T(8,128)(2,1)}, u32[]{:S(2)}, u32[]{:S(2)}) collective-permute-start(bf16[4,4,24,1024]{3,2,1,0:T(8,128)(2,1)} %collective-permute-done.10.refs_2_), channel_id=1, source_target_pairs={{0,2},{2,4},{4,6},{6,0},{8,10},{10,12},{12,14},{14,8},{16,18},{18,... | collective-permute-start | bytes 2359304 | tf_op jit(solution)/shard_map/ppermute | solution.py:114
  158.0 18.6 %collective-permute-start.22 = (bf16[4,4,24,1024]{3,2,1,0:T(8,128)(2,1)}, bf16[4,4,24,1024]{3,2,1,0:T(8,128)(2,1)}, u32[]{:S(2)}, u32[]{:S(2)}) collective-permute-start(bf16[4,4,24,1024]{3,2,1,0:T(8,128)(2,1)} %collective-permute-done.13.refs_5_), channel_id=1, source_target_pairs={{0,6},{2,0},{4,2},{6,4},{8,14},{10,8},{12,10},{14,12},{16,22},{18,... | collective-permute-start | bytes 2359304 | tf_op jit(solution)/shard_map/ppermute | solution.py:114
  161.2 1.2 copy-start.2
  162.4 4.6 %copy-start.4 = (bf16[4,4,24,1024]{3,2,1,0:T(8,128)(2,1)S(1)}, bf16[4,4,24,1024]{3,2,1,0:T(8,128)(2,1)}, u32[]{:S(2)}) copy-start(bf16[4,4,24,1024]{3,2,1,0:T(8,128)(2,1)} %copy-done.3) | copy-start | bytes 2359300
  179.4 6.2 %collective-permute-start.25 = (f32[3072,128]{1,0:T(8,128)S(1)}, f32[3072,128]{1,0:T(8,128)S(1)}, u32[]{:S(2)}, u32[]{:S(2)}) collective-permute-start(f32[3072,128]{1,0:T(8,128)S(1)} %bitcast.12), channel_id=1, source_target_pairs={{0,1},{1,0},{2,3},{3,2},{4,5},{5,4},{6,7},{7,6},{8,9},{9,8},{10,11... | collective-permute-start | bytes 4718600 | tf_op jit(solution)/shard_map/ppermute | solution.py:282

commit v4 on v3

v4 whole, which is shorter than its diff:
```python
import jax
import jax.numpy as jnp
from jax import lax
from jax.experimental import pallas as pl
from jax.experimental.pallas import tpu as pltpu
from jax.sharding import PartitionSpec as P


DH = 128
BF = jnp.bfloat16
SMALL = pltpu.CompilerParams(vmem_limit_bytes=16 << 20)
SMEM = pl.BlockSpec(memory_space=pltpu.SMEM)
VMEM = pl.BlockSpec(memory_space=pltpu.VMEM)
F32 = jnp.float32


def near(*arrays):
    return [pltpu.with_memory_space_constraint(a, pltpu.VMEM) for a in arrays]


def away(*arrays):
    return [pltpu.with_memory_space_constraint(a, pltpu.HBM) for a in arrays]


def dot(a, b, dims):
    return lax.dot_general(a, b, (dims, ((), ())), preferred_element_type=F32)


def states_kernel(k_ref, v_ref, o_ref):
    for h in range(k_ref.shape[1] // DH):
        c = slice(h * DH, (h + 1) * DH)
        o_ref[c, :] = dot(k_ref[:, c], v_ref[:, c], ((0,), (0,))).astype(BF)


def local_states(keys, values, heads_per_step=4):
    rows, cols = keys.shape
    width = heads_per_step * DH
    spec = pl.BlockSpec((rows, width), lambda i: (0, i))
    return pl.pallas_call(
        states_kernel,
        grid=(cols // width,),
        in_specs=[spec, spec],
        out_specs=pl.BlockSpec((width, DH), lambda i: (i, 0)),
        out_shape=jax.ShapeDtypeStruct((cols, DH), BF),
        compiler_params=SMALL,
        name="local_states",
    )(*away(keys, values))


def running_kernel(x_ref, o_ref):
    def step(j, total):
        o_ref[j] = total.astype(BF)
        return total + x_ref[j].astype(F32)

    lax.fori_loop(0, x_ref.shape[0], step, jnp.zeros(x_ref.shape[1:], F32), unroll=8)


def exclusive_sums(pieces):
    return pl.pallas_call(
        running_kernel,
        out_shape=pltpu.VMEM(pieces.shape, BF),
        compiler_params=SMALL,
        name="exclusive_sums",
    )(*near(pieces))


def inner_kernel(q_ref, k_ref, v_ref, o_ref):
    rows = q_ref.shape[0]
    t = lax.broadcasted_iota(jnp.int32, (rows, rows), 0)
    s = lax.broadcasted_iota(jnp.int32, (rows, rows), 1)
    causal = t >= s
    for h in range(q_ref.shape[1] // DH):
        c = slice(h * DH, (h + 1) * DH)
        q, k, v = q_ref[:, c], k_ref[:, c], v_ref[:, c]
        scores = jnp.where(causal, dot(q, k, ((1,), (1,))), 0.0)
        high = scores.astype(BF)
        low = (scores - high.astype(F32)).astype(BF)
        o_ref[:, c] = dot(high, v, ((1,), (0,))) + dot(low, v, ((1,), (0,)))


def inner_attention(queries, keys, values, heads_per_step=4):
    rows, cols = queries.shape
    width = heads_per_step * DH
    spec = pl.BlockSpec((rows, width), lambda i: (0, i))
    return pl.pallas_call(
        inner_kernel,
        grid=(cols // width,),
        in_specs=[spec, spec, spec],
        out_specs=spec,
        out_shape=pltpu.VMEM((rows, cols), F32),
        compiler_params=SMALL,
        name="inner_attention",
    )(*away(queries, keys, values))


def normed_kernel(q_ref, i_ref, s_ref, g_ref, o_ref):
    for h in range(q_ref.shape[1] // DH):
        c = slice(h * DH, (h + 1) * DH)
        attn = dot(q_ref[:, c], s_ref[c, :], ((1,), (0,))) + i_ref[:, c]
        meansq = jnp.mean(attn * attn, axis=-1, keepdims=True)
        o_ref[:, c] = (attn * lax.rsqrt(meansq + 1e-06) * g_ref[:, c]).astype(BF)


def normed_attention(queries, inner, prior, gain):
    return pl.pallas_call(
        normed_kernel,
        in_specs=[VMEM] * 4,
        out_specs=VMEM,
        out_shape=pltpu.VMEM(queries.shape, BF),
        compiler_params=SMALL,
        name="normed_attention",
    )(*near(queries, inner, prior, gain))


SEQ = ("y", "z", "x")
NY, NZ, NX = 4, 8, 4
PART_A, PART_B, PART_C = 512, 768, 768
CUT = PART_A + PART_B


def shift(block, axis, by):
    pairs = []
    for y in range(NY):
        for z in range(NZ):
            for x in range(NX):
                ty = (y + by) % NY if axis == "y" else y
                tz = (z + by) % NZ if axis == "z" else z
                tx = (x + by) % NX if axis == "x" else x
                pairs.append(((y * NZ + z) * NX + x, (ty * NZ + tz) * NX + tx))
    return lax.ppermute(block, SEQ, pairs)


def wrap(index, count):
    return lax.rem(index + count, count)


def turn(block, axis, by):
    pairs = []
    for y in range(NY):
        for z in range(NZ):
            for x in range(NX):
                for core in (0, 1):
                    step = -by if core else by
                    ty = (y + step) % NY if axis == "y" else y
                    tz = (z + step) % NZ if axis == "z" else z
                    tx = (x + step) % NX if axis == "x" else x
                    here, there = (y * NZ + z) * NX + x, (ty * NZ + tz) * NX + tx
                    pairs.append((2 * here + core, 2 * there + core))
    return lax.ppermute(block, SEQ + ("head",), pairs)


def around(block, axis):
    first = turn(block, axis, 1)
    second = turn(block, axis, -1)
    return [block, first, second, turn(first, axis, 1)]


def source(place_ref, which, i):
    step = 1 - 2 * place_ref[3]
    return lax.rem(place_ref[which] + 4 - (0, step, -step, 2)[i], 4)


def layer(place_ref, i):
    step = 1 - 2 * place_ref[3]
    return lax.rem(place_ref[1] + NZ - (0, 1, 2, 3, 4, -1, -2, -3)[i] * step, NZ)


def round_z(block):
    ahead, back = [block], [block]
    for step in range(1, 5):
        ahead.append(turn(ahead[-1], "z", 1))
        if step < 4:
            back.append(turn(back[-1], "z", -1))
    return ahead + back[1:]


def assemble(place, sources, pieces, outs, cuts):
    count = len(pieces)

    def kernel(place_ref, *refs):
        for i in range(count):
            cuts(refs[i], refs[count:], sources(place_ref, i))

    vmem = pl.BlockSpec(memory_space=pltpu.VMEM)
    return pl.pallas_call(
        kernel,
        in_specs=[pl.BlockSpec(memory_space=pltpu.SMEM)] + [vmem] * count,
        out_specs=[vmem] * len(outs),
        out_shape=[pltpu.VMEM(o, BF) for o in outs],
        compiler_params=SMALL,
    )(place, *near(*pieces))


def gather_a(own, place):
    n = own.shape[0]

    def cut(piece, outs, i):
        outs[0][i] = piece[...]

    on_x, on_y = (lambda p, i: wrap(p[2] - i, NX)), (lambda p, i: wrap(p[0] - i, NY))
    pieces = [own] + [shift(own, "x", by) for by in (1, 2, 3)]
    (row,) = assemble(place, on_x, pieces, [(NX, n, PART_A)], cut)
    pieces = [row] + [shift(row, "y", by) for by in (1, 2, 3)]
    (plane,) = assemble(place, on_y, pieces, [(NY, NX, n, PART_A)], cut)
    return round_z(plane)


def cut_own_kernel(own_ref, a_ref, copies_ref):
    a_ref[...] = own_ref[:, :PART_A]
    rest = own_ref[:, PART_A:]
    for i in range(NZ):
        copies_ref[i] = rest


def cut_own(own):
    n, depth = own.shape
    return pl.pallas_call(
        cut_own_kernel,
        in_specs=[VMEM],
        out_specs=[VMEM, VMEM],
        out_shape=[pltpu.VMEM((n, PART_A), BF), pltpu.VMEM((NZ, n, depth - PART_A), BF)],
        compiler_params=SMALL,
        name="cut_own",
    )(own)


def cut_column_kernel(column_ref, b_ref, c_ref):
    b_ref[...] = column_ref[:, :, :PART_B]
    c_ref[...] = column_ref[:, :, PART_B:]


def cut_column(column):
    shapes = [column.shape[:2] + (w,) for w in (PART_B, PART_C)]
    return pl.pallas_call(
        cut_column_kernel,
        in_specs=[VMEM],
        out_specs=[VMEM, VMEM],
        out_shape=[pltpu.VMEM(w, BF) for w in shapes],
        compiler_params=SMALL,
        name="cut_column",
    )(*near(column))


def gather_bc(copies, place):
    n = copies.shape[1]

    def cut_y(piece, outs, i):
        outs[0][i] = piece[...]

    def cut_x(piece, outs, i):
        outs[0][:, i] = piece[...]

    column = lax.all_to_all(copies, "z", 0, 0)
    col_b, col_c = cut_column(column)
    on_y, on_x = (lambda p, i: source(p, 0, i)), (lambda p, i: source(p, 2, i))
    along_y, along_x = around(col_b, "y"), around(col_c, "x")
    (plane_b,) = assemble(place, on_y, along_y, [(NY, NZ, n, PART_B)], cut_y)
    (plane_c,) = assemble(place, on_x, along_x, [(NZ, NX, n, PART_C)], cut_x)
    return around(plane_b, "x"), around(plane_c, "y")


def multiply(w, normed):
    flat = w.reshape(w.shape[0] * w.shape[1] * w.shape[2], w.shape[3])
    return dot(flat, normed, ((1,), (1,))).reshape(w.shape[:3] + normed.shape[:1])


def split(terms, me):
    rows = terms.shape[-1] // 2
    first, second = terms[..., :rows], terms[..., rows:]
    return jnp.where(me == 0, first, second), jnp.where(me == 0, second, first)


HALVES = (slice(0, NZ // 2), slice(NZ // 2, NZ))


HALVES = (slice(0, NZ // 2), slice(NZ // 2, NZ))
A_EARLY, A_LATE = (0, 1, 2, 3, 5, 6), (4, 7)


def parts_of(n_ref):
    return n_ref[:, :PART_A], n_ref[:, PART_A:CUT], n_ref[:, CUT:]


def adder(place_ref, mine_ref, theirs_ref):
    def add(at, piece, normed, fresh=False):
        kept, sent = split(multiply(piece, normed), place_ref[3])
        mine_ref[at] = kept if fresh else mine_ref[at] + kept
        theirs_ref[at] = sent if fresh else theirs_ref[at] + sent

    return add


def early_kernel(place_ref, n_ref, *refs):
    count = len(A_EARLY)
    pieces_a, pieces_b, pieces_c = refs[:count], refs[count : count + 3], refs[count + 3 : count + 6]
    mine_ref, theirs_ref = refs[count + 6 :]
    add = adder(place_ref, mine_ref, theirs_ref)
    normed_a, normed_b, normed_c = parts_of(n_ref)
    for ref in (mine_ref, theirs_ref):
        ref[:, :, source(place_ref, 2, 3)] = jnp.zeros(ref.shape[:2] + ref.shape[3:], F32)
    for i in range(3):
        for lane in HALVES:
            at = (slice(None), lane, source(place_ref, 2, i))
            add(at, pieces_b[i][:, lane], normed_b, fresh=True)
    for i in range(3):
        for lane in HALVES:
            add((source(place_ref, 0, i), lane), pieces_c[i][lane], normed_c)
    for i, piece in zip(A_EARLY, pieces_a):
        add((slice(None), layer(place_ref, i)), piece[...], normed_a)


def late_kernel(place_ref, n_ref, _mine, _theirs, *refs):
    count = len(A_LATE)
    pieces_a, (b_ref, c_ref, mine_ref, theirs_ref) = refs[:count], refs[count:]
    add = adder(place_ref, mine_ref, theirs_ref)
    normed_a, normed_b, normed_c = parts_of(n_ref)
    for i, piece in zip(A_LATE, pieces_a):
        add((slice(None), layer(place_ref, i)), piece[...], normed_a)
    for lane in HALVES:
        add((slice(None), lane, source(place_ref, 2, 3)), b_ref[:, lane], normed_b)
        add((source(place_ref, 0, 3), lane), c_ref[lane], normed_c)


def finish_kernel(mine_ref, other_ref, o_ref):
    wide = o_ref.shape[0]
    for start in range(0, o_ref.shape[1], wide):
        at = slice(start, start + wide)
        o_ref[:, at] = (mine_ref[at] + other_ref[at]).T.astype(BF)


def project_early(place, normed, pieces):
    n = pieces[-1].shape[2]
    half = pltpu.VMEM((NY, NZ, NX, n, normed.shape[0] // 2), F32)
    return pl.pallas_call(
        early_kernel,
        in_specs=[SMEM] + [VMEM] * (1 + len(pieces)),
        out_specs=[VMEM, VMEM],
        out_shape=[half, half],
        compiler_params=SMALL,
        name="project_early",
    )(place, *near(normed, *pieces))


def project_late(place, normed, terms, pieces):
    half = pltpu.VMEM(terms[0].shape, F32)
    return pl.pallas_call(
        late_kernel,
        in_specs=[SMEM] + [VMEM] * (3 + len(pieces)),
        out_specs=[VMEM, VMEM],
        out_shape=[half, half],
        input_output_aliases={2: 0, 3: 1},
        compiler_params=SMALL,
        name="project_late",
    )(place, *near(normed, *terms, *pieces))


def finish(mine, other):
    return pl.pallas_call(
        finish_kernel,
        out_shape=jax.ShapeDtypeStruct((mine.shape[1], mine.shape[0]), BF),
        compiler_params=SMALL,
        name="finish",
    )(*near(mine, other))


def whole(queries, keys, values, gain, w_out):
    devices = lax.axis_size(SEQ)
    own = w_out.T
    place = jnp.stack([lax.axis_index(a) for a in SEQ + ("head",)]).astype(jnp.int32)
    first, copies = cut_own(own)
    parts_b, parts_c = gather_bc(copies, place)
    parts_a = gather_a(first, place)
    states = local_states(keys, values)
    shares = lax.all_to_all(states, SEQ, 0, 0, tiled=True)
    sums = exclusive_sums(shares.reshape(devices, -1, DH))
    prior = lax.all_to_all(sums.reshape(-1, DH), SEQ, 0, 0, tiled=True)
    inner = inner_attention(queries, keys, values)
    normed = normed_attention(queries, inner, prior, gain.reshape(1, -1))
    early = [parts_a[i] for i in A_EARLY] + parts_b[:3] + parts_c[:3]
    late = [parts_a[i] for i in A_LATE] + parts_b[3:] + parts_c[3:]
    terms = project_early(place, normed, early)
    mine, theirs = project_late(place, normed, terms, late)
    mine, theirs = (a.reshape(-1, a.shape[-1]) for a in (mine, theirs))
    other = lax.ppermute(theirs, "head", [(0, 1), (1, 0)])
    return finish(mine, other)


def solution(mesh):
    torus = jax.sharding.Mesh(mesh.devices.reshape(NY, NZ, NX, 2), SEQ + ("head",))
    return jax.shard_map(
        whole,
        mesh=torus,
        in_specs=(
            P(SEQ, "head"),
            P(SEQ, "head"),
            P(SEQ, "head"),
            P("head"),
            P("head", SEQ),
        ),
        out_specs=P(SEQ + ("head",), None),
        check_vma=False,
    )
```

time: 188 us -> 161 us (0.86)
  waiting for transfers between devices: 94.9 us -> 37.4 us
  blocking collectives: 0 us -> 26.3 us
  Pallas kernels: 21.8 us -> 25.2 us
    ppermute x25 -> x6, waiting for transfers between devices: 91.4 us -> 6.84 us  [shift(): return lax.ppermute(block, SEQ, pairs)]
    ppermute x25 -> x6, starting transfers between devices: 42.3 us -> 7.98 us  [shift(): return lax.ppermute(block, SEQ, pairs)]
    ppermute x0 -> x19, starting transfers between devices: none -> 29.5 us  [turn(): return lax.ppermute(block, SEQ + ('head',), pairs)]
    ppermute x0 -> x19, waiting for transfers between devices: none -> 27.5 us  [turn(): return lax.ppermute(block, SEQ + ('head',), pairs)]
    all_to_all x0 -> x1, blocking collectives: none -> 26.3 us  [gather_bc(): column = lax.all_to_all(copies, 'z', 0, 0)]
    ppermute x1, starting transfers between devices: 3.13 us -> 10.7 us  [whole(): other = lax.ppermute(theirs, 'head', [(0, 1), (1, 0)])]
    pallas_call x3 -> x6, Pallas kernels: 13.4 us -> 15.7 us  [the longest x1 5.5 us: project_early(): pl.pallas_call(early_kernel, in_specs=[SMEM] + [VMEM] * (1 + len(pieces))...]
    all_to_all x1, starting transfers between devices: 10.7 us -> 8.49 us  [whole(): shares = lax.all_to_all(states, SEQ, 0, 0, tiled=True)]
  transfers between devices with their start and end apart: 28 -> 28, of which waited for: 15 -> 11; matrix products, arithmetic and copies ran while one was open for 0% -> 0% of each run, Pallas kernels for 8% -> 13%
where the time goes in v4:
time: 161 us; the launch traced here: 160 us
  starting transfers between devices  66.4 us (41%)
  waiting for transfers between devices  37.4 us (23%)
  blocking collectives  26.3 us (16%)
  Pallas kernels  25.2 us (16%)
  local copies, waits for them, and re-layouts  4.63 us (3%)
    ppermute x19, starting transfers between devices, turn(): return lax.ppermute(block, SEQ + ('head',), pairs)  29.5 us
    ppermute x19, waiting for transfers between devices, turn(): return lax.ppermute(block, SEQ + ('head',), pairs)  27.5 us
    all_to_all x1, blocking collectives, gather_bc(): column = lax.all_to_all(copies, 'z', 0, 0)  26.3 us
    ppermute x1, starting transfers between devices, whole(): other = lax.ppermute(theirs, 'head', [(0, 1), (1, 0)])  10.7 us
    all_to_all x1, starting transfers between devices, whole(): prior = lax.all_to_all(sums.reshape(-1, DH), SEQ, 0, 0, tiled=True)  9.7 us
    all_to_all x1, starting transfers between devices, whole(): shares = lax.all_to_all(states, SEQ, 0, 0, tiled=True)  8.49 us
    ppermute x6, starting transfers between devices, shift(): return lax.ppermute(block, SEQ, pairs)  7.98 us
    ppermute x6, waiting for transfers between devices, shift(): return lax.ppermute(block, SEQ, pairs)  6.84 us
  transfers between devices with their start and end apart: 28, of which 11 were waited for; matrix products, arithmetic and copies ran while one was open for 0% of the time, Pallas kernels for 13%

profile of v4, /device:TPU:1, one launch (start us, length us, event | category | flops | bytes accessed | tf_op | source)
XLA Modules:
  0.0 160.3 jit_solution(17710015525777494343)
XLA Ops:
  0.0 0.9 copy-done.9
  0.9 0.0 copy-start.10
  0.9 0.6 copy-done.10
  1.5 26.3 %all_to_all.22.column_ref = bf16[8,24,1536]{2,1,0:T(8,128)(2,1)S(1)} all-to-all(bf16[8,24,1536]{2,1,0:T(8,128)(2,1)S(1)} %get-tuple-element.14), channel_id=1, replica_groups=mesh['y'=4,'z'=8,'x'=4,'head'=2] {'z'}, dimensions={0} | all-to-all | bytes 1179648 | tf_op jit(solution)/shard_map/all_to_all | solution.py:253
  27.9 2.8 %collective-permute-start.11 = (bf16[8,24,768]{2,1,0:T(8,128)(2,1)S(1)}, bf16[8,24,768]{2,1,0:T(8,128)(2,1)S(1)}, u32[]{:S(2)}, u32[]{:S(2)}) collective-permute-start(bf16[8,24,768]{2,1,0:T(8,128)(2,1)S(1)} %get-tuple-element.15.refs_0_), channel_id=1, source_target_pairs={{0,64},{1,193},{2,66},{3,195},{4,68},{5,197},{6,70},{7,199},{8,72}... | collective-permute-start | bytes 884744 | tf_op jit(solution)/shard_map/ppermute | solution.py:149
  30.7 2.5 %collective-permute-start.16 = (bf16[8,24,768]{2,1,0:T(8,128)(2,1)S(1)}, bf16[8,24,768]{2,1,0:T(8,128)(2,1)S(1)}, u32[]{:S(2)}, u32[]{:S(2)}) collective-permute-start(bf16[8,24,768]{2,1,0:T(8,128)(2,1)S(1)} %get-tuple-element.16.refs_0_), channel_id=1, source_target_pairs={{0,2},{1,7},{2,4},{3,1},{4,6},{5,3},{6,0},{7,5},{8,10},{9,15},{10,... | collective-permute-start | bytes 884744 | tf_op jit(solution)/shard_map/ppermute | solution.py:149
  33.2 0.0 collective-permute-start.12
  33.2 1.2 collective-permute-done.11.refs_1_
  34.4 3.4 %collective-permute-start.13 = (bf16[8,24,768]{2,1,0:T(8,128)(2,1)S(1)}, bf16[8,24,768]{2,1,0:T(8,128)(2,1)S(1)}, u32[]{:S(2)}, u32[]{:S(2)}) collective-permute-start(bf16[8,24,768]{2,1,0:T(8,128)(2,1)S(1)} %collective-permute-done.11.refs_1_), channel_id=1, source_target_pairs={{0,64},{1,193},{2,66},{3,195},{4,68},{5,197},{6,70},{7,199},{8,72}... | collective-permute-start | bytes 884744 | tf_op jit(solution)/shard_map/ppermute | solution.py:149
  37.8 0.9 collective-permute-start.17
  38.7 0.0 collective-permute-done.16.refs_1_
  38.7 1.8 %collective-permute-start.18 = (bf16[8,24,768]{2,1,0:T(8,128)(2,1)S(1)}, bf16[8,24,768]{2,1,0:T(8,128)(2,1)S(1)}, u32[]{:S(2)}, u32[]{:S(2)}) collective-permute-start(bf16[8,24,768]{2,1,0:T(8,128)(2,1)S(1)} %collective-permute-done.16.refs_1_), channel_id=1, source_target_pairs={{0,2},{1,7},{2,4},{3,1},{4,6},{5,3},{6,0},{7,5},{8,10},{9,15},{10,... | collective-permute-start | bytes 884744 | tf_op jit(solution)/shard_map/ppermute | solution.py:149
  40.5 0.1 pad_add_fusion.place_ref
  40.6 0.1 collective-permute-done.12.refs_2_
  40.7 1.9 %collective-permute-done.13.refs_3_ = bf16[8,24,768]{2,1,0:T(8,128)(2,1)S(1)} collective-permute-done((bf16[8,24,768]{2,1,0:T(8,128)(2,1)S(1)}, bf16[8,24,768]{2,1,0:T(8,128)(2,1)S(1)}, u32[]{:S(2)}, u32[]{:S(2)}) %collective-permute-start.13) | collective-permute-done | bytes 294944 | tf_op jit(solution)/shard_map/ppermute | solution.py:149
  42.6 0.6 shard_map.57.refs_6_
  43.2 0.0 copy-start.11
  43.2 1.5 collective-permute-start.14
  44.8 0.1 collective-permute-done.17.refs_2_
  44.9 0.4 collective-permute-done.18.refs_3_
  45.3 1.7 %shard_map.58.refs_9_ = bf16[8,4,24,768]{3,2,1,0:T(8,128)(2,1)} custom-call(s32[4]{0:T(128)S(1)} %pad_add_fusion.place_ref, bf16[8,24,768]{2,1,0:T(8,128)(2,1)S(1)} %get-tuple-element.16.refs_0_, bf16[8,24,768]{2,1,0:T(8,128)(2,1)S(1)} %collective-permute-done.16.refs_1_, bf16[8,24,768]{2,1,0:T(8,128)(2,1)S(1)} %collective-permute-done.17.refs_2_, ...), custom_call_target="tpu_custom_call" | custom-call | tf_op jit(solution)/shard_map/pallas_call | solution.py:185
  47.0 2.2 %collective-permute-start.19 = (bf16[8,4,24,768]{3,2,1,0:T(8,128)(2,1)}, bf16[8,4,24,768]{3,2,1,0:T(8,128)(2,1)}, u32[]{:S(2)}, u32[]{:S(2)}) collective-permute-start(bf16[8,4,24,768]{3,2,1,0:T(8,128)(2,1)} %shard_map.58.refs_9_), channel_id=1, source_target_pairs={{0,64},{1,193},{2,66},{3,195},{4,68},{5,197},{6,70},{7,199},{8,72}... | collective-permute-start | bytes 3538952 | tf_op jit(solution)/shard_map/ppermute | solution.py:149
  49.2 0.0 collective-permute-start
  49.2 2.3 %collective-permute-start.1 = (bf16[24,512]{1,0:T(8,128)(2,1)S(1)}, bf16[24,512]{1,0:T(8,128)(2,1)S(1)}, u32[]{:S(2)}, u32[]{:S(2)}) collective-permute-start(bf16[24,512]{1,0:T(8,128)(2,1)S(1)} %copy-done.11), channel_id=1, source_target_pairs={{0,4},{2,6},{4,0},{6,2},{8,12},{10,14},{12,8},{14,10},{16,20},{18,... | collective-permute-start | bytes 73736 | tf_op jit(solution)/shard_map/ppermute | solution.py:130
  51.5 1.2 collective-permute-start.2
  52.6 4.0 %local_states.1 = bf16[2048,128]{1,0:T(8,128)(2,1)} custom-call(bf16[256,2048]{1,0:T(8,128)(2,1)} %k_ref.3, bf16[256,2048]{1,0:T(8,128)(2,1)} %v_ref.3), custom_call_target="tpu_custom_call" | custom-call | tf_op jit(solution)/shard_map/local_states/pallas_call | solution.py:39
  56.6 8.5 %all-to-all-start = ((bf16[128,16,128]{2,1,0:T(8,128)(2,1)}), bf16[128,16,128]{2,1,0:T(8,128)(2,1)S(1)}, u32[]{:S(2)}, u32[]{:S(2)}) async-start(bf16[128,16,128]{2,1,0:T(8,128)(2,1)} %bitcast.4), calls=%async_computation | async-start | bytes 1048576 | tf_op jit(solution)/shard_map/all_to_all | solution.py:374
  65.1 0.0 collective-permute-done.refs_1_
  65.1 0.0 collective-permute-done.1.refs_2_
  65.1 0.6 shard_map.55.refs_0_
  65.7 0.8 collective-permute-start.3
  66.4 2.8 %collective-permute-start.4 = (bf16[4,24,512]{2,1,0:T(8,128)(2,1)S(1)}, bf16[4,24,512]{2,1,0:T(8,128)(2,1)S(1)}, u32[]{:S(2)}, u32[]{:S(2)}) collective-permute-start(bf16[4,24,512]{2,1,0:T(8,128)(2,1)S(1)} %shard_map.55.refs_0_), channel_id=1, source_target_pairs={{0,128},{2,130},{4,132},{6,134},{8,136},{10,138},{12,140},{14,142}... | collective-permute-start | bytes 294920 | tf_op jit(solution)/shard_map/ppermute | solution.py:130
  69.3 1.0 collective-permute-start.5
  70.2 2.5 %collective-permute-done.3.refs_1_ = bf16[4,24,512]{2,1,0:T(8,128)(2,1)S(1)} collective-permute-done((bf16[4,24,512]{2,1,0:T(8,128)(2,1)S(1)}, bf16[4,24,512]{2,1,0:T(8,128)(2,1)S(1)}, u32[]{:S(2)}, u32[]{:S(2)}) %collective-permute-start.3) | collective-permute-done | bytes 98336 | tf_op jit(solution)/shard_map/ppermute | solution.py:130
  72.7 4.4 %collective-permute-done.4.refs_2_ = bf16[4,24,512]{2,1,0:T(8,128)(2,1)S(1)} collective-permute-done((bf16[4,24,512]{2,1,0:T(8,128)(2,1)S(1)}, bf16[4,24,512]{2,1,0:T(8,128)(2,1)S(1)}, u32[]{:S(2)}, u32[]{:S(2)}) %collective-permute-start.4) | collective-permute-done | bytes 98336 | tf_op jit(solution)/shard_map/ppermute | solution.py:130
  77.1 0.0 collective-permute-done.5.refs_3_
  77.1 0.6 shard_map.56.refs_0_
  77.7 0.1 collective-permute-start.6
  77.7 1.5 collective-permute-start.9
  79.2 5.5 %collective-permute-done.6.refs_1_ = bf16[4,4,24,512]{3,2,1,0:T(8,128)(2,1)S(1)} collective-permute-done((bf16[4,4,24,512]{3,2,1,0:T(8,128)(2,1)S(1)}, bf16[4,4,24,512]{3,2,1,0:T(8,128)(2,1)S(1)}, u32[]{:S(2)}, u32[]{:S(2)}) %collective-permute-start.6) | collective-permute-done | bytes 393248 | tf_op jit(solution)/shard_map/ppermute | solution.py:149
  84.7 1.3 collective-permute-start.7
  86.0 0.8 copy-done.5
  86.7 1.2 collective-permute-start.15
  88.0 0.0 collective-permute-done.9.refs_4_
  88.0 7.6 %collective-permute-done.7.refs_2_ = bf16[4,4,24,512]{3,2,1,0:T(8,128)(2,1)S(1)} collective-permute-done((bf16[4,4,24,512]{3,2,1,0:T(8,128)(2,1)S(1)}, bf16[4,4,24,512]{3,2,1,0:T(8,128)(2,1)S(1)}, u32[]{:S(2)}, u32[]{:S(2)}) %collective-permute-start.7) | collective-permute-done | bytes 393248 | tf_op jit(solution)/shard_map/ppermute | solution.py:149
  95.6 2.7 %collective-permute-start.23 = (bf16[4,8,24,768]{3,2,1,0:T(8,128)(2,1)}, bf16[4,8,24,768]{3,2,1,0:T(8,128)(2,1)}, u32[]{:S(2)}, u32[]{:S(2)}) collective-permute-start(bf16[4,8,24,768]{3,2,1,0:T(8,128)(2,1)} %collective-permute-done.14.refs_7_), channel_id=1, source_target_pairs={{0,2},{1,7},{2,4},{3,1},{4,6},{5,3},{6,0},{7,5},{8,10},{9,15},{10,... | collective-permute-start | bytes 3538952 | tf_op jit(solution)/shard_map/ppermute | solution.py:149
  98.3 2.6 %collective-permute-start.24 = (bf16[8,4,24,768]{3,2,1,0:T(8,128)(2,1)}, bf16[8,4,24,768]{3,2,1,0:T(8,128)(2,1)}, u32[]{:S(2)}, u32[]{:S(2)}) collective-permute-start(bf16[8,4,24,768]{3,2,1,0:T(8,128)(2,1)} %collective-permute-done.19.refs_10_), channel_id=1, source_target_pairs={{0,64},{1,193},{2,66},{3,195},{4,68},{5,197},{6,70},{7,199},{8,72}... | collective-permute-start | bytes 3538952 | tf_op jit(solution)/shard_map/ppermute | solution.py:149
  100.9 1.0 exclusive_sums.1
  101.9 9.7 %all-to-all-start.1 = ((bf16[128,16,128]{2,1,0:T(8,128)(2,1)}), bf16[128,16,128]{2,1,0:T(8,128)(2,1)}, u32[]{:S(2)}, u32[]{:S(2)}) async-start(bf16[128,16,128]{2,1,0:T(8,128)(2,1)} %exclusive_sums.1), calls=%async_computation.1 | async-start | bytes 1048576 | tf_op jit(solution)/shard_map/all_to_all | solution.py:376
  111.6 0.0 copy-start.12
  111.6 1.9 %collective-permute-start.8 = (bf16[4,4,24,512]{3,2,1,0:T(8,128)(2,1)}, bf16[4,4,24,512]{3,2,1,0:T(8,128)(2,1)}, u32[]{:S(2)}, u32[]{:S(2)}) collective-permute-start(bf16[4,4,24,512]{3,2,1,0:T(8,128)(2,1)} %copy-done.7), channel_id=1, source_target_pairs={{0,8},{1,57},{2,10},{3,59},{4,12},{5,61},{6,14},{7,63},{8,16},{9,1... | collective-permute-start | bytes 1179656 | tf_op jit(solution)/shard_map/ppermute | solution.py:149
  113.5 10.6 %collective-permute-done.8.refs_3_ = bf16[4,4,24,512]{3,2,1,0:T(8,128)(2,1)} collective-permute-done((bf16[4,4,24,512]{3,2,1,0:T(8,128)(2,1)}, bf16[4,4,24,512]{3,2,1,0:T(8,128)(2,1)}, u32[]{:S(2)}, u32[]{:S(2)}) %collective-permute-start.8) | collective-permute-done | bytes 393248 | tf_op jit(solution)/shard_map/ppermute | solution.py:149
  124.1 1.1 collective-permute-start.22
  125.2 1.1 copy-done.3
  126.3 2.0 %collective-permute-start.21 = (bf16[4,4,24,512]{3,2,1,0:T(8,128)(2,1)}, bf16[4,4,24,512]{3,2,1,0:T(8,128)(2,1)}, u32[]{:S(2)}, u32[]{:S(2)}) collective-permute-start(bf16[4,4,24,512]{3,2,1,0:T(8,128)(2,1)} %collective-permute-done.8.refs_3_), channel_id=1, source_target_pairs={{0,8},{1,57},{2,10},{3,59},{4,12},{5,61},{6,14},{7,63},{8,16},{9,1... | collective-permute-start | bytes 1179656 | tf_op jit(solution)/shard_map/ppermute | solution.py:149
  128.4 5.1 %inner_attention.1.i_ref = f32[256,2048]{1,0:T(8,128)S(1)} custom-call(bf16[256,2048]{1,0:T(8,128)(2,1)} %q_ref.3, bf16[256,2048]{1,0:T(8,128)(2,1)} %k_ref.3, bf16[256,2048]{1,0:T(8,128)(2,1)} %v_ref.3), custom_call_target="tpu_custom_call" | custom-call | tf_op jit(solution)/shard_map/inner_attention/pallas_call | solution.py:85
  133.5 0.0 copy-start
  133.5 1.2 copy-done
  134.7 2.0 %normed_attention.1.n_ref = bf16[256,2048]{1,0:T(8,128)(2,1)S(1)} custom-call(bf16[256,2048]{1,0:T(8,128)(2,1)S(1)} %copy-done, f32[256,2048]{1,0:T(8,128)S(1)} %inner_attention.1.i_ref, bf16[2048,128]{1,0:T(8,128)(2,1)} %bitcast.5.s_ref, f32[1,2048]{1,0:T(1,128)S(1)} %bitcast.13), custom_call_target="tpu_custom_call" | custom-call | tf_op jit(solution)/shard_map/normed_attention/pallas_call | solution.py:105
  136.8 5.5 %project_early.1 = (f32[4,8,4,24,128]{4,3,2,1,0:T(8,128)S(1)}, f32[4,8,4,24,128]{4,3,2,1,0:T(8,128)S(1)}) custom-call(s32[4]{0:T(128)S(1)} %pad_add_fusion.place_ref, bf16[256,2048]{1,0:T(8,128)(2,1)S(1)} %normed_attention.1.n_ref, bf16[4,4,24,512]{3,2,1,0:T(8,128)(2,1)S(1)} %copy-done.2, bf16[4,4,24,512]{3,2,1,0:T(8,128)(2,1)S(1)} %copy-done.6, ...), custom_call_target="tpu_custom_call" | custom-call | tf_op jit(solution)/shard_map/project_early/pallas_call | solution.py:334
  142.3 3.0 %project_late.1 = (f32[4,8,4,24,128]{4,3,2,1,0:T(8,128)S(1)}, f32[4,8,4,24,128]{4,3,2,1,0:T(8,128)S(1)}) custom-call(s32[4]{0:T(128)S(1)} %pad_add_fusion.place_ref, bf16[256,2048]{1,0:T(8,128)(2,1)S(1)} %normed_attention.1.n_ref, f32[4,8,4,24,128]{4,3,2,1,0:T(8,128)S(1)} %get-tuple-element.17._mine, ...), custom_call_target="tpu_custom_call", output_to_operand_aliasing={{0}: (2, {}), {1}: (3, {})} | custom-call | tf_op jit(solution)/shard_map/project_late/pallas_call | solution.py:346
  145.4 10.7 %collective-permute-start.25 = (f32[3072,128]{1,0:T(8,128)S(1)}, f32[3072,128]{1,0:T(8,128)S(1)}, u32[]{:S(2)}, u32[]{:S(2)}) collective-permute-start(f32[3072,128]{1,0:T(8,128)S(1)} %bitcast.11), channel_id=1, source_target_pairs={{0,1},{1,0},{2,3},{3,2},{4,5},{5,4},{6,7},{7,6},{8,9},{9,8},{10,11... | collective-permute-start | bytes 4718600 | tf_op jit(solution)/shard_map/ppermute | solution.py:384
  156.1 3.0 %collective-permute-done.25.other_ref = f32[3072,128]{1,0:T(8,128)S(1)} collective-permute-done((f32[3072,128]{1,0:T(8,128)S(1)}, f32[3072,128]{1,0:T(8,128)S(1)}, u32[]{:S(2)}, u32[]{:S(2)}) %collective-permute-start.25) | collective-permute-done | bytes 1572896 | tf_op jit(solution)/shard_map/ppermute | solution.py:384
  159.2 1.2 finish.1
  (33 shorter events, 0.1 us)
Async XLA Ops:
  0.0 0.9 copy-start.9
  0.9 0.6 copy-start.10
  27.9 6.5 %collective-permute-start.11 = (bf16[8,24,768]{2,1,0:T(8,128)(2,1)S(1)}, bf16[8,24,768]{2,1,0:T(8,128)(2,1)S(1)}, u32[]{:S(2)}, u32[]{:S(2)}) collective-permute-start(bf16[8,24,768]{2,1,0:T(8,128)(2,1)S(1)} %get-tuple-element.15.refs_0_), channel_id=1, source_target_pairs={{0,64},{1,193},{2,66},{3,195},{4,68},{5,197},{6,70},{7,199},{8,72}... | collective-permute-start | bytes 884744 | tf_op jit(solution)/shard_map/ppermute | solution.py:149
  30.7 8.0 %collective-permute-start.16 = (bf16[8,24,768]{2,1,0:T(8,128)(2,1)S(1)}, bf16[8,24,768]{2,1,0:T(8,128)(2,1)S(1)}, u32[]{:S(2)}, u32[]{:S(2)}) collective-permute-start(bf16[8,24,768]{2,1,0:T(8,128)(2,1)S(1)} %get-tuple-element.16.refs_0_), channel_id=1, source_target_pairs={{0,2},{1,7},{2,4},{3,1},{4,6},{5,3},{6,0},{7,5},{8,10},{9,15},{10,... | collective-permute-start | bytes 884744 | tf_op jit(solution)/shard_map/ppermute | solution.py:149
  33.2 7.5 %collective-permute-start.12 = (bf16[8,24,768]{2,1,0:T(8,128)(2,1)S(1)}, bf16[8,24,768]{2,1,0:T(8,128)(2,1)S(1)}, u32[]{:S(2)}, u32[]{:S(2)}) collective-permute-start(bf16[8,24,768]{2,1,0:T(8,128)(2,1)S(1)} %get-tuple-element.15.refs_0_), channel_id=1, source_target_pairs={{0,192},{1,65},{2,194},{3,67},{4,196},{5,69},{6,198},{7,71},{8,200... | collective-permute-start | bytes 884744 | tf_op jit(solution)/shard_map/ppermute | solution.py:149
  34.4 8.2 %collective-permute-start.13 = (bf16[8,24,768]{2,1,0:T(8,128)(2,1)S(1)}, bf16[8,24,768]{2,1,0:T(8,128)(2,1)S(1)}, u32[]{:S(2)}, u32[]{:S(2)}) collective-permute-start(bf16[8,24,768]{2,1,0:T(8,128)(2,1)S(1)} %collective-permute-done.11.refs_1_), channel_id=1, source_target_pairs={{0,64},{1,193},{2,66},{3,195},{4,68},{5,197},{6,70},{7,199},{8,72}... | collective-permute-start | bytes 884744 | tf_op jit(solution)/shard_map/ppermute | solution.py:149
  37.8 7.1 %collective-permute-start.17 = (bf16[8,24,768]{2,1,0:T(8,128)(2,1)S(1)}, bf16[8,24,768]{2,1,0:T(8,128)(2,1)S(1)}, u32[]{:S(2)}, u32[]{:S(2)}) collective-permute-start(bf16[8,24,768]{2,1,0:T(8,128)(2,1)S(1)} %get-tuple-element.16.refs_0_), channel_id=1, source_target_pairs={{0,6},{1,3},{2,0},{3,5},{4,2},{5,7},{6,4},{7,1},{8,14},{9,11},{10,... | collective-permute-start | bytes 884744 | tf_op jit(solution)/shard_map/ppermute | solution.py:149
  38.7 6.6 %collective-permute-start.18 = (bf16[8,24,768]{2,1,0:T(8,128)(2,1)S(1)}, bf16[8,24,768]{2,1,0:T(8,128)(2,1)S(1)}, u32[]{:S(2)}, u32[]{:S(2)}) collective-permute-start(bf16[8,24,768]{2,1,0:T(8,128)(2,1)S(1)} %collective-permute-done.16.refs_1_), channel_id=1, source_target_pairs={{0,2},{1,7},{2,4},{3,1},{4,6},{5,3},{6,0},{7,5},{8,10},{9,15},{10,... | collective-permute-start | bytes 884744 | tf_op jit(solution)/shard_map/ppermute | solution.py:149
  43.2 6.0 %copy-start.11 = (bf16[24,512]{1,0:T(8,128)(2,1)S(1)}, bf16[24,512]{1,0:T(8,128)(2,1)}, u32[]{:S(2)}) copy-start(bf16[24,512]{1,0:T(8,128)(2,1)} %copy-done.10) | copy-start | bytes 73732
  43.2 52.4 %collective-permute-start.14 = (bf16[4,8,24,768]{3,2,1,0:T(8,128)(2,1)S(1)}, bf16[4,8,24,768]{3,2,1,0:T(8,128)(2,1)}, u32[]{:S(2)}, u32[]{:S(2)}) collective-permute-start(bf16[4,8,24,768]{3,2,1,0:T(8,128)(2,1)S(1)} %shard_map.57.refs_6_), channel_id=1, source_target_pairs={{0,2},{1,7},{2,4},{3,1},{4,6},{5,3},{6,0},{7,5},{8,10},{9,15},{10,... | collective-permute-start | bytes 3538952 | tf_op jit(solution)/shard_map/ppermute | solution.py:149
  47.0 51.4 %collective-permute-start.19 = (bf16[8,4,24,768]{3,2,1,0:T(8,128)(2,1)}, bf16[8,4,24,768]{3,2,1,0:T(8,128)(2,1)}, u32[]{:S(2)}, u32[]{:S(2)}) collective-permute-start(bf16[8,4,24,768]{3,2,1,0:T(8,128)(2,1)} %shard_map.58.refs_9_), channel_id=1, source_target_pairs={{0,64},{1,193},{2,66},{3,195},{4,68},{5,197},{6,70},{7,199},{8,72}... | collective-permute-start | bytes 3538952 | tf_op jit(solution)/shard_map/ppermute | solution.py:149
  49.2 15.9 %collective-permute-start = (bf16[24,512]{1,0:T(8,128)(2,1)S(1)}, bf16[24,512]{1,0:T(8,128)(2,1)S(1)}, u32[]{:S(2)}, u32[]{:S(2)}) collective-permute-start(bf16[24,512]{1,0:T(8,128)(2,1)S(1)} %copy-done.11), channel_id=1, source_target_pairs={{0,2},{2,4},{4,6},{6,0},{8,10},{10,12},{12,14},{14,8},{16,18},{18,... | collective-permute-start | bytes 73736 | tf_op jit(solution)/shard_map/ppermute | solution.py:130
  49.2 15.9 %collective-permute-start.1 = (bf16[24,512]{1,0:T(8,128)(2,1)S(1)}, bf16[24,512]{1,0:T(8,128)(2,1)S(1)}, u32[]{:S(2)}, u32[]{:S(2)}) collective-permute-start(bf16[24,512]{1,0:T(8,128)(2,1)S(1)} %copy-done.11), channel_id=1, source_target_pairs={{0,4},{2,6},{4,0},{6,2},{8,12},{10,14},{12,8},{14,10},{16,20},{18,... | collective-permute-start | bytes 73736 | tf_op jit(solution)/shard_map/ppermute | solution.py:130
  51.5 13.6 %collective-permute-start.2 = (bf16[24,512]{1,0:T(8,128)(2,1)S(1)}, bf16[24,512]{1,0:T(8,128)(2,1)S(1)}, u32[]{:S(2)}, u32[]{:S(2)}) collective-permute-start(bf16[24,512]{1,0:T(8,128)(2,1)S(1)} %copy-done.11), channel_id=1, source_target_pairs={{0,6},{2,0},{4,2},{6,4},{8,14},{10,8},{12,10},{14,12},{16,22},{18,... | collective-permute-start | bytes 73736 | tf_op jit(solution)/shard_map/ppermute | solution.py:130
  56.6 44.3 %all-to-all-start = ((bf16[128,16,128]{2,1,0:T(8,128)(2,1)}), bf16[128,16,128]{2,1,0:T(8,128)(2,1)S(1)}, u32[]{:S(2)}, u32[]{:S(2)}) async-start(bf16[128,16,128]{2,1,0:T(8,128)(2,1)} %bitcast.4), calls=%async_computation | async-start | bytes 1048576 | tf_op jit(solution)/shard_map/all_to_all | solution.py:374
  65.7 7.0 %collective-permute-start.3 = (bf16[4,24,512]{2,1,0:T(8,128)(2,1)S(1)}, bf16[4,24,512]{2,1,0:T(8,128)(2,1)S(1)}, u32[]{:S(2)}, u32[]{:S(2)}) collective-permute-start(bf16[4,24,512]{2,1,0:T(8,128)(2,1)S(1)} %shard_map.55.refs_0_), channel_id=1, source_target_pairs={{0,64},{2,66},{4,68},{6,70},{8,72},{10,74},{12,76},{14,78},{16,80}... | collective-permute-start | bytes 294920 | tf_op jit(solution)/shard_map/ppermute | solution.py:130
  66.4 10.6 %collective-permute-start.4 = (bf16[4,24,512]{2,1,0:T(8,128)(2,1)S(1)}, bf16[4,24,512]{2,1,0:T(8,128)(2,1)S(1)}, u32[]{:S(2)}, u32[]{:S(2)}) collective-permute-start(bf16[4,24,512]{2,1,0:T(8,128)(2,1)S(1)} %shard_map.55.refs_0_), channel_id=1, source_target_pairs={{0,128},{2,130},{4,132},{6,134},{8,136},{10,138},{12,140},{14,142}... | collective-permute-start | bytes 294920 | tf_op jit(solution)/shard_map/ppermute | solution.py:130
  69.3 7.8 %collective-permute-start.5 = (bf16[4,24,512]{2,1,0:T(8,128)(2,1)S(1)}, bf16[4,24,512]{2,1,0:T(8,128)(2,1)S(1)}, u32[]{:S(2)}, u32[]{:S(2)}) collective-permute-start(bf16[4,24,512]{2,1,0:T(8,128)(2,1)S(1)} %shard_map.55.refs_0_), channel_id=1, source_target_pairs={{0,192},{2,194},{4,196},{6,198},{8,200},{10,202},{12,204},{14,206}... | collective-permute-start | bytes 294920 | tf_op jit(solution)/shard_map/ppermute | solution.py:130
  77.6 47.6 %copy-start.1 = (bf16[4,4,24,512]{3,2,1,0:T(8,128)(2,1)}, bf16[4,4,24,512]{3,2,1,0:T(8,128)(2,1)S(1)}, u32[]{:S(2)}) copy-start(bf16[4,4,24,512]{3,2,1,0:T(8,128)(2,1)S(1)} %shard_map.56.refs_0_) | copy-start | bytes 1179652
  77.7 7.0 %collective-permute-start.6 = (bf16[4,4,24,512]{3,2,1,0:T(8,128)(2,1)S(1)}, bf16[4,4,24,512]{3,2,1,0:T(8,128)(2,1)S(1)}, u32[]{:S(2)}, u32[]{:S(2)}) collective-permute-start(bf16[4,4,24,512]{3,2,1,0:T(8,128)(2,1)S(1)} %shard_map.56.refs_0_), channel_id=1, source_target_pairs={{0,8},{1,57},{2,10},{3,59},{4,12},{5,61},{6,14},{7,63},{8,16},{9,1... | collective-permute-start | bytes 1179656 | tf_op jit(solution)/shard_map/ppermute | solution.py:149
  77.7 10.2 %collective-permute-start.9 = (bf16[4,4,24,512]{3,2,1,0:T(8,128)(2,1)S(1)}, bf16[4,4,24,512]{3,2,1,0:T(8,128)(2,1)}, u32[]{:S(2)}, u32[]{:S(2)}) collective-permute-start(bf16[4,4,24,512]{3,2,1,0:T(8,128)(2,1)S(1)} %shard_map.56.refs_0_), channel_id=1, source_target_pairs={{0,56},{1,9},{2,58},{3,11},{4,60},{5,13},{6,62},{7,15},{8,0},{9,17... | collective-permute-start | bytes 1179656 | tf_op jit(solution)/shard_map/ppermute | solution.py:149
  84.7 11.0 %collective-permute-start.7 = (bf16[4,4,24,512]{3,2,1,0:T(8,128)(2,1)S(1)}, bf16[4,4,24,512]{3,2,1,0:T(8,128)(2,1)S(1)}, u32[]{:S(2)}, u32[]{:S(2)}) collective-permute-start(bf16[4,4,24,512]{3,2,1,0:T(8,128)(2,1)S(1)} %collective-permute-done.6.refs_1_), channel_id=1, source_target_pairs={{0,8},{1,57},{2,10},{3,59},{4,12},{5,61},{6,14},{7,63},{8,16},{9,1... | collective-permute-start | bytes 1179656 | tf_op jit(solution)/shard_map/ppermute | solution.py:149
  86.0 0.8 copy-start.5
  86.7 38.5 %collective-permute-start.15 = (bf16[4,8,24,768]{3,2,1,0:T(8,128)(2,1)S(1)}, bf16[4,8,24,768]{3,2,1,0:T(8,128)(2,1)S(1)}, u32[]{:S(2)}, u32[]{:S(2)}) collective-permute-start(bf16[4,8,24,768]{3,2,1,0:T(8,128)(2,1)S(1)} %shard_map.57.refs_6_), channel_id=1, source_target_pairs={{0,6},{1,3},{2,0},{3,5},{4,2},{5,7},{6,4},{7,1},{8,14},{9,11},{10,... | collective-permute-start | bytes 3538952 | tf_op jit(solution)/shard_map/ppermute | solution.py:149
  88.0 23.6 %collective-permute-start.10 = (bf16[4,4,24,512]{3,2,1,0:T(8,128)(2,1)}, bf16[4,4,24,512]{3,2,1,0:T(8,128)(2,1)}, u32[]{:S(2)}, u32[]{:S(2)}) collective-permute-start(bf16[4,4,24,512]{3,2,1,0:T(8,128)(2,1)} %collective-permute-done.9.refs_4_), channel_id=1, source_target_pairs={{0,56},{1,9},{2,58},{3,11},{4,60},{5,13},{6,62},{7,15},{8,0},{9,17... | collective-permute-start | bytes 1179656 | tf_op jit(solution)/shard_map/ppermute | solution.py:149
  95.6 2.7 %copy-start.7 = (bf16[4,4,24,512]{3,2,1,0:T(8,128)(2,1)}, bf16[4,4,24,512]{3,2,1,0:T(8,128)(2,1)S(1)}, u32[]{:S(2)}) copy-start(bf16[4,4,24,512]{3,2,1,0:T(8,128)(2,1)S(1)} %collective-permute-done.7.refs_2_) | copy-start | bytes 1179652
  95.6 41.1 %collective-permute-start.20 = (bf16[8,4,24,768]{3,2,1,0:T(8,128)(2,1)}, bf16[8,4,24,768]{3,2,1,0:T(8,128)(2,1)}, u32[]{:S(2)}, u32[]{:S(2)}) collective-permute-start(bf16[8,4,24,768]{3,2,1,0:T(8,128)(2,1)} %shard_map.58.refs_9_), channel_id=1, source_target_pairs={{0,192},{1,65},{2,194},{3,67},{4,196},{5,69},{6,198},{7,71},{8,200... | collective-permute-start | bytes 3538952 | tf_op jit(solution)/shard_map/ppermute | solution.py:149
  95.6 46.7 %collective-permute-start.23 = (bf16[4,8,24,768]{3,2,1,0:T(8,128)(2,1)}, bf16[4,8,24,768]{3,2,1,0:T(8,128)(2,1)}, u32[]{:S(2)}, u32[]{:S(2)}) collective-permute-start(bf16[4,8,24,768]{3,2,1,0:T(8,128)(2,1)} %collective-permute-done.14.refs_7_), channel_id=1, source_target_pairs={{0,2},{1,7},{2,4},{3,1},{4,6},{5,3},{6,0},{7,5},{8,10},{9,15},{10,... | collective-permute-start | bytes 3538952 | tf_op jit(solution)/shard_map/ppermute | solution.py:149
  98.3 44.0 %collective-permute-start.24 = (bf16[8,4,24,768]{3,2,1,0:T(8,128)(2,1)}, bf16[8,4,24,768]{3,2,1,0:T(8,128)(2,1)}, u32[]{:S(2)}, u32[]{:S(2)}) collective-permute-start(bf16[8,4,24,768]{3,2,1,0:T(8,128)(2,1)} %collective-permute-done.19.refs_10_), channel_id=1, source_target_pairs={{0,64},{1,193},{2,66},{3,195},{4,68},{5,197},{6,70},{7,199},{8,72}... | collective-permute-start | bytes 3538952 | tf_op jit(solution)/shard_map/ppermute | solution.py:149
  101.9 31.6 %all-to-all-start.1 = ((bf16[128,16,128]{2,1,0:T(8,128)(2,1)}), bf16[128,16,128]{2,1,0:T(8,128)(2,1)}, u32[]{:S(2)}, u32[]{:S(2)}) async-start(bf16[128,16,128]{2,1,0:T(8,128)(2,1)} %exclusive_sums.1), calls=%async_computation.1 | async-start | bytes 1048576 | tf_op jit(solution)/shard_map/all_to_all | solution.py:376
  111.6 21.9 %copy-start.12 = (f32[2048]{0:T(1024)S(1)}, f32[2048]{0:T(1024)}, u32[]{:S(2)}) copy-start(f32[2048]{0:T(1024)} %param.8) | copy-start | bytes 24580
  111.6 12.5 %collective-permute-start.8 = (bf16[4,4,24,512]{3,2,1,0:T(8,128)(2,1)}, bf16[4,4,24,512]{3,2,1,0:T(8,128)(2,1)}, u32[]{:S(2)}, u32[]{:S(2)}) collective-permute-start(bf16[4,4,24,512]{3,2,1,0:T(8,128)(2,1)} %copy-done.7), channel_id=1, source_target_pairs={{0,8},{1,57},{2,10},{3,59},{4,12},{5,61},{6,14},{7,63},{8,16},{9,1... | collective-permute-start | bytes 1179656 | tf_op jit(solution)/shard_map/ppermute | solution.py:149
  124.1 18.2 %collective-permute-start.22 = (bf16[4,4,24,512]{3,2,1,0:T(8,128)(2,1)}, bf16[4,4,24,512]{3,2,1,0:T(8,128)(2,1)}, u32[]{:S(2)}, u32[]{:S(2)}) collective-permute-start(bf16[4,4,24,512]{3,2,1,0:T(8,128)(2,1)} %collective-permute-done.10.refs_5_), channel_id=1, source_target_pairs={{0,56},{1,9},{2,58},{3,11},{4,60},{5,13},{6,62},{7,15},{8,0},{9,17... | collective-permute-start | bytes 1179656 | tf_op jit(solution)/shard_map/ppermute | solution.py:149
  125.2 1.1 copy-start.3
  126.3 16.0 %collective-permute-start.21 = (bf16[4,4,24,512]{3,2,1,0:T(8,128)(2,1)}, bf16[4,4,24,512]{3,2,1,0:T(8,128)(2,1)}, u32[]{:S(2)}, u32[]{:S(2)}) collective-permute-start(bf16[4,4,24,512]{3,2,1,0:T(8,128)(2,1)} %collective-permute-done.8.refs_3_), channel_id=1, source_target_pairs={{0,8},{1,57},{2,10},{3,59},{4,12},{5,61},{6,14},{7,63},{8,16},{9,1... | collective-permute-start | bytes 1179656 | tf_op jit(solution)/shard_map/ppermute | solution.py:149
  133.5 1.2 copy-start
  134.7 2.0 %copy-start.2 = (bf16[4,4,24,512]{3,2,1,0:T(8,128)(2,1)S(1)}, bf16[4,4,24,512]{3,2,1,0:T(8,128)(2,1)}, u32[]{:S(2)}) copy-start(bf16[4,4,24,512]{3,2,1,0:T(8,128)(2,1)} %copy-done.1) | copy-start | bytes 1179652
  134.7 2.0 %copy-start.4 = (bf16[4,8,24,768]{3,2,1,0:T(8,128)(2,1)S(1)}, bf16[4,8,24,768]{3,2,1,0:T(8,128)(2,1)}, u32[]{:S(2)}) copy-start(bf16[4,8,24,768]{3,2,1,0:T(8,128)(2,1)} %copy-done.3) | copy-start | bytes 3538948
  134.7 2.0 %copy-start.6 = (bf16[4,4,24,512]{3,2,1,0:T(8,128)(2,1)S(1)}, bf16[4,4,24,512]{3,2,1,0:T(8,128)(2,1)}, u32[]{:S(2)}) copy-start(bf16[4,4,24,512]{3,2,1,0:T(8,128)(2,1)} %copy-done.5) | copy-start | bytes 1179652
  134.7 2.1 %copy-start.8 = (bf16[4,4,24,512]{3,2,1,0:T(8,128)(2,1)S(1)}, bf16[4,4,24,512]{3,2,1,0:T(8,128)(2,1)}, u32[]{:S(2)}) copy-start(bf16[4,4,24,512]{3,2,1,0:T(8,128)(2,1)} %copy-done.7) | copy-start | bytes 1179652
  145.4 13.8 %collective-permute-start.25 = (f32[3072,128]{1,0:T(8,128)S(1)}, f32[3072,128]{1,0:T(8,128)S(1)}, u32[]{:S(2)}, u32[]{:S(2)}) collective-permute-start(f32[3072,128]{1,0:T(8,128)S(1)} %bitcast.11), channel_id=1, source_target_pairs={{0,1},{1,0},{2,3},{3,2},{4,5},{5,4},{6,7},{7,6},{8,9},{9,8},{10,11... | collective-permute-start | bytes 4718600 | tf_op jit(solution)/shard_map/ppermute | solution.py:384

commit v5 on v4

--- a/solution.py
+++ b/solution.py
@@ -1,3 +1,5 @@
+import functools
+
 import jax
 import jax.numpy as jnp
 from jax import lax
@@ -87,29 +89,38 @@
         grid=(cols // width,),
         in_specs=[spec, spec, spec],
         out_specs=spec,
-        out_shape=pltpu.VMEM((rows, cols), F32),
+        out_shape=pltpu.HBM((rows, cols), F32),
         compiler_params=SMALL,
         name="inner_attention",
     )(*away(queries, keys, values))
 
 
-def normed_kernel(q_ref, i_ref, s_ref, g_ref, o_ref):
-    for h in range(q_ref.shape[1] // DH):
-        c = slice(h * DH, (h + 1) * DH)
-        attn = dot(q_ref[:, c], s_ref[c, :], ((1,), (0,))) + i_ref[:, c]
-        meansq = jnp.mean(attn * attn, axis=-1, keepdims=True)
-        o_ref[:, c] = (attn * lax.rsqrt(meansq + 1e-06) * g_ref[:, c]).astype(BF)
-
-
-def normed_attention(queries, inner, prior, gain):
+def normed_kernel(place_ref, q_ref, i_ref, s_ref, g_ref, o_ref):
+    rows = q_ref.shape[0] // 2
+    for half in (0, 1):
+        at = pl.ds(pl.multiple_of(lax.rem(place_ref[3] + half, 2) * rows, rows), rows)
+        t = slice(half * rows, (half + 1) * rows)
+        for h in range(q_ref.shape[1] // DH):
+            c = slice(h * DH, (h + 1) * DH)
+            state = s_ref[pl.ds(pl.multiple_of(pl.program_id(0) * q_ref.shape[1] + h * DH, DH), DH), :]
+            attn = dot(q_ref[t, c], state, ((1,), (0,))) + i_ref[t, c]
+            meansq = jnp.mean(attn * attn, axis=-1, keepdims=True)
+            o_ref[at, c] = (attn * lax.rsqrt(meansq + 1e-06) * g_ref[:, c]).astype(BF)
+
+
+def normed_attention(place, queries, inner, prior, gain, heads_per_step=4):
+    rows, cols = queries.shape
+    width = heads_per_step * DH
+    spec = pl.BlockSpec((rows, width), lambda i: (0, i))
     return pl.pallas_call(
         normed_kernel,
-        in_specs=[VMEM] * 4,
-        out_specs=VMEM,
+        grid=(cols // width,),
+        in_specs=[SMEM, spec, spec, VMEM, pl.BlockSpec((1, width), lambda i: (0, i))],
+        out_specs=spec,
         out_shape=pltpu.VMEM(queries.shape, BF),
         compiler_params=SMALL,
         name="normed_attention",
-    )(*near(queries, inner, prior, gain))
+    )(place, *away(queries, inner), *near(prior), gain)
 
 
 SEQ = ("y", "z", "x")
@@ -264,61 +275,38 @@
     return dot(flat, normed, ((1,), (1,))).reshape(w.shape[:3] + normed.shape[:1])
 
 
-def split(terms, me):
-    rows = terms.shape[-1] // 2
-    first, second = terms[..., :rows], terms[..., rows:]
-    return jnp.where(me == 0, first, second), jnp.where(me == 0, second, first)
-
-
 HALVES = (slice(0, NZ // 2), slice(NZ // 2, NZ))
-
-
-HALVES = (slice(0, NZ // 2), slice(NZ // 2, NZ))
-A_EARLY, A_LATE = (0, 1, 2, 3, 5, 6), (4, 7)
-
-
-def parts_of(n_ref):
-    return n_ref[:, :PART_A], n_ref[:, PART_A:CUT], n_ref[:, CUT:]
-
-
-def adder(place_ref, mine_ref, theirs_ref):
+STAGES = (((0, 1, 2, 5, 6), (0, 1)), ((3, 7), (2,)), ((4,), (3,)))
+
+
+def project_kernel(stage, place_ref, n_ref, *refs):
+    from_a, from_bc = STAGES[stage]
+    fresh = stage == 0
+    refs = refs if fresh else refs[2:]
+    a_refs, refs = refs[: len(from_a)], refs[len(from_a) :]
+    b_refs, refs = refs[: len(from_bc)], refs[len(from_bc) :]
+    c_refs, (mine_ref, theirs_ref) = refs[: len(from_bc)], refs[len(from_bc) :]
+    rows = mine_ref.shape[-1]
+    normed_a, normed_b, normed_c = n_ref[:, :PART_A], n_ref[:, PART_A:CUT], n_ref[:, CUT:]
+
     def add(at, piece, normed, fresh=False):
-        kept, sent = split(multiply(piece, normed), place_ref[3])
+        terms = multiply(piece, normed)
+        kept, sent = terms[..., :rows], terms[..., rows:]
         mine_ref[at] = kept if fresh else mine_ref[at] + kept
         theirs_ref[at] = sent if fresh else theirs_ref[at] + sent
 
-    return add
-
-
-def early_kernel(place_ref, n_ref, *refs):
-    count = len(A_EARLY)
-    pieces_a, pieces_b, pieces_c = refs[:count], refs[count : count + 3], refs[count + 3 : count + 6]
-    mine_ref, theirs_ref = refs[count + 6 :]
-    add = adder(place_ref, mine_ref, theirs_ref)
-    normed_a, normed_b, normed_c = parts_of(n_ref)
-    for ref in (mine_ref, theirs_ref):
-        ref[:, :, source(place_ref, 2, 3)] = jnp.zeros(ref.shape[:2] + ref.shape[3:], F32)
-    for i in range(3):
+    if fresh:
+        for i in (2, 3):
+            for ref in (mine_ref, theirs_ref):
+                ref[:, :, source(place_ref, 2, i)] = jnp.zeros(ref.shape[:2] + ref.shape[3:], F32)
+    for i, piece in zip(from_bc, b_refs):
         for lane in HALVES:
-            at = (slice(None), lane, source(place_ref, 2, i))
-            add(at, pieces_b[i][:, lane], normed_b, fresh=True)
-    for i in range(3):
+            add((slice(None), lane, source(place_ref, 2, i)), piece[:, lane], normed_b, fresh)
+    for i, piece in zip(from_bc, c_refs):
         for lane in HALVES:
-            add((source(place_ref, 0, i), lane), pieces_c[i][lane], normed_c)
-    for i, piece in zip(A_EARLY, pieces_a):
+            add((source(place_ref, 0, i), lane), piece[lane], normed_c)
+    for i, piece in zip(from_a, a_refs):
         add((slice(None), layer(place_ref, i)), piece[...], normed_a)
-
-
-def late_kernel(place_ref, n_ref, _mine, _theirs, *refs):
-    count = len(A_LATE)
-    pieces_a, (b_ref, c_ref, mine_ref, theirs_ref) = refs[:count], refs[count:]
-    add = adder(place_ref, mine_ref, theirs_ref)
-    normed_a, normed_b, normed_c = parts_of(n_ref)
-    for i, piece in zip(A_LATE, pieces_a):
-        add((slice(None), layer(place_ref, i)), piece[...], normed_a)
-    for lane in HALVES:
-        add((slice(None), lane, source(place_ref, 2, 3)), b_ref[:, lane], normed_b)
-        add((source(place_ref, 0, 3), lane), c_ref[lane], normed_c)
 
 
 def finish_kernel(mine_ref, other_ref, o_ref):
@@ -328,29 +316,17 @@
         o_ref[:, at] = (mine_ref[at] + other_ref[at]).T.astype(BF)
 
 
-def project_early(place, normed, pieces):
-    n = pieces[-1].shape[2]
-    half = pltpu.VMEM((NY, NZ, NX, n, normed.shape[0] // 2), F32)
-    return pl.pallas_call(
-        early_kernel,
-        in_specs=[SMEM] + [VMEM] * (1 + len(pieces)),
+def project(stage, place, normed, terms, parts_a, parts_b, parts_c):
+    from_a, from_bc = STAGES[stage]
+    pieces = [parts_a[i] for i in from_a] + [p[i] for p in (parts_b, parts_c) for i in from_bc]
+    half = pltpu.VMEM((NY, NZ, NX, pieces[0].shape[2], normed.shape[0] // 2), F32)
+    return pl.pallas_call(
+        functools.partial(project_kernel, stage),
+        in_specs=[SMEM] + [VMEM] * (1 + len(terms) + len(pieces)),
         out_specs=[VMEM, VMEM],
         out_shape=[half, half],
-        compiler_params=SMALL,
-        name="project_early",
-    )(place, *near(normed, *pieces))
-
-
-def project_late(place, normed, terms, pieces):
-    half = pltpu.VMEM(terms[0].shape, F32)
-    return pl.pallas_call(
-        late_kernel,
-        in_specs=[SMEM] + [VMEM] * (3 + len(pieces)),
-        out_specs=[VMEM, VMEM],
-        out_shape=[half, half],
-        input_output_aliases={2: 0, 3: 1},
-        compiler_params=SMALL,
-        name="project_late",
+        input_output_aliases={2: 0, 3: 1} if terms else {},
+        compiler_params=SMALL,
     )(place, *near(normed, *terms, *pieces))
 
 
@@ -375,12 +351,11 @@
     sums = exclusive_sums(shares.reshape(devices, -1, DH))
     prior = lax.all_to_all(sums.reshape(-1, DH), SEQ, 0, 0, tiled=True)
     inner = inner_attention(queries, keys, values)
-    normed = normed_attention(queries, inner, prior, gain.reshape(1, -1))
-    early = [parts_a[i] for i in A_EARLY] + parts_b[:3] + parts_c[:3]
-    late = [parts_a[i] for i in A_LATE] + parts_b[3:] + parts_c[3:]
-    terms = project_early(place, normed, early)
-    mine, theirs = project_late(place, normed, terms, late)
-    mine, theirs = (a.reshape(-1, a.shape[-1]) for a in (mine, theirs))
+    normed = normed_attention(place, queries, inner, prior, gain.reshape(1, -1))
+    terms = ()
+    for stage in range(len(STAGES)):
+        terms = project(stage, place, normed, terms, parts_a, parts_b, parts_c)
+    mine, theirs = (a.reshape(-1, a.shape[-1]) for a in terms)
     other = lax.ppermute(theirs, "head", [(0, 1), (1, 0)])
     return finish(mine, other)
 

time: 161 us -> 166 us (1.031)
  Pallas kernels: 25.2 us -> 28.6 us
  waiting for transfers between devices: 37.4 us -> 39.3 us
    pallas_call x3 -> x4, Pallas kernels: 10.5 us -> 13.1 us  [the longest x3 9.47 us: project(): pl.pallas_call(functools.partial(project_kernel, stage), in_specs=[SMEM]...]
    ppermute x19, waiting for transfers between devices: 27.5 us -> 29.6 us  [turn(): return lax.ppermute(block, SEQ + ('head',), pairs)]
    unnamed x26 -> x20, local copies, waits for them, and re-layouts: 4.63 us -> 3.18 us
  transfers between devices with their start and end apart: 28 -> 28, of which waited for: 11 -> 12; matrix products, arithmetic and copies ran while one was open for 0% -> 0% of each run, Pallas kernels for 13% -> 15%
where the time goes in v5:
time: 166 us; the launch traced here: 165 us
  starting transfers between devices  67.1 us (40%)
  waiting for transfers between devices  39.3 us (24%)
  Pallas kernels  28.6 us (17%)
  blocking collectives  26.3 us (16%)
  local copies, waits for them, and re-layouts  3.18 us (2%)
    ppermute x19, waiting for transfers between devices, turn(): return lax.ppermute(block, SEQ + ('head',), pairs)  29.6 us
    ppermute x19, starting transfers between devices, turn(): return lax.ppermute(block, SEQ + ('head',), pairs)  29 us
    all_to_all x1, blocking collectives, gather_bc(): column = lax.all_to_all(copies, 'z', 0, 0)  26.3 us
    ppermute x1, starting transfers between devices, whole(): other = lax.ppermute(theirs, 'head', [(0, 1), (1, 0)])  12 us
    all_to_all x1, starting transfers between devices, whole(): prior = lax.all_to_all(sums.reshape(-1, DH), SEQ, 0, 0, tiled=True)  9.64 us
    pallas_call x3, Pallas kernels, project(): pl.pallas_call(functools.partial(project_kernel, stage), in_specs=[SMEM]...  9.47 us
    all_to_all x1, starting transfers between devices, whole(): shares = lax.all_to_all(states, SEQ, 0, 0, tiled=True)  8.5 us
    ppermute x6, starting transfers between devices, shift(): return lax.ppermute(block, SEQ, pairs)  7.98 us
  transfers between devices with their start and end apart: 28, of which 12 were waited for; matrix products, arithmetic and copies ran while one was open for 0% of the time, Pallas kernels for 15%

profile of v5, /device:TPU:1, one launch (start us, length us, event | category | flops | bytes accessed | tf_op | source)
XLA Modules:
  0.0 164.8 jit_solution(4865226786665540414)
XLA Ops:
  0.0 0.9 copy-done.8
  0.9 0.6 cut_own.1
  1.5 26.3 %all_to_all.22.column_ref = bf16[8,24,1536]{2,1,0:T(8,128)(2,1)S(1)} all-to-all(bf16[8,24,1536]{2,1,0:T(8,128)(2,1)S(1)} %get-tuple-element.16), channel_id=1, replica_groups=mesh['y'=4,'z'=8,'x'=4,'head'=2] {'z'}, dimensions={0} | all-to-all | bytes 1179648 | tf_op jit(solution)/shard_map/all_to_all | solution.py:264
  27.9 2.8 %collective-permute-start.10 = (bf16[8,24,768]{2,1,0:T(8,128)(2,1)S(1)}, bf16[8,24,768]{2,1,0:T(8,128)(2,1)S(1)}, u32[]{:S(2)}, u32[]{:S(2)}) collective-permute-start(bf16[8,24,768]{2,1,0:T(8,128)(2,1)S(1)} %get-tuple-element.17.refs_0_), channel_id=1, source_target_pairs={{0,64},{1,193},{2,66},{3,195},{4,68},{5,197},{6,70},{7,199},{8,72}... | collective-permute-start | bytes 884744 | tf_op jit(solution)/shard_map/ppermute | solution.py:160
  30.7 2.5 %collective-permute-start.14 = (bf16[8,24,768]{2,1,0:T(8,128)(2,1)S(1)}, bf16[8,24,768]{2,1,0:T(8,128)(2,1)S(1)}, u32[]{:S(2)}, u32[]{:S(2)}) collective-permute-start(bf16[8,24,768]{2,1,0:T(8,128)(2,1)S(1)} %get-tuple-element.18.refs_0_), channel_id=1, source_target_pairs={{0,2},{1,7},{2,4},{3,1},{4,6},{5,3},{6,0},{7,5},{8,10},{9,15},{10,... | collective-permute-start | bytes 884744 | tf_op jit(solution)/shard_map/ppermute | solution.py:160
  33.2 0.0 collective-permute-start.11
  33.2 1.2 collective-permute-done.10.refs_1_
  34.4 3.4 %collective-permute-start.12 = (bf16[8,24,768]{2,1,0:T(8,128)(2,1)S(1)}, bf16[8,24,768]{2,1,0:T(8,128)(2,1)S(1)}, u32[]{:S(2)}, u32[]{:S(2)}) collective-permute-start(bf16[8,24,768]{2,1,0:T(8,128)(2,1)S(1)} %collective-permute-done.10.refs_1_), channel_id=1, source_target_pairs={{0,64},{1,193},{2,66},{3,195},{4,68},{5,197},{6,70},{7,199},{8,72}... | collective-permute-start | bytes 884744 | tf_op jit(solution)/shard_map/ppermute | solution.py:160
  37.8 0.9 collective-permute-start.15
  38.7 1.8 %collective-permute-start.16 = (bf16[8,24,768]{2,1,0:T(8,128)(2,1)S(1)}, bf16[8,24,768]{2,1,0:T(8,128)(2,1)S(1)}, u32[]{:S(2)}, u32[]{:S(2)}) collective-permute-start(bf16[8,24,768]{2,1,0:T(8,128)(2,1)S(1)} %collective-permute-done.14.refs_1_), channel_id=1, source_target_pairs={{0,2},{1,7},{2,4},{3,1},{4,6},{5,3},{6,0},{7,5},{8,10},{9,15},{10,... | collective-permute-start | bytes 884744 | tf_op jit(solution)/shard_map/ppermute | solution.py:160
  40.5 0.1 pad_add_fusion.place_ref
  40.6 0.1 collective-permute-done.11.refs_2_
  40.7 1.9 %collective-permute-done.12.refs_3_ = bf16[8,24,768]{2,1,0:T(8,128)(2,1)S(1)} collective-permute-done((bf16[8,24,768]{2,1,0:T(8,128)(2,1)S(1)}, bf16[8,24,768]{2,1,0:T(8,128)(2,1)S(1)}, u32[]{:S(2)}, u32[]{:S(2)}) %collective-permute-start.12) | collective-permute-done | bytes 294944 | tf_op jit(solution)/shard_map/ppermute | solution.py:160
  42.6 0.6 shard_map.57.refs_5_
  43.2 1.5 collective-permute-start.13
  44.7 0.2 collective-permute-done.15.refs_2_
  44.9 0.4 collective-permute-done.16.refs_3_
  45.3 0.6 shard_map.58.refs_7_
  45.9 2.3 %collective-permute-start.17 = (bf16[8,4,24,768]{3,2,1,0:T(8,128)(2,1)S(1)}, bf16[8,4,24,768]{3,2,1,0:T(8,128)(2,1)}, u32[]{:S(2)}, u32[]{:S(2)}) collective-permute-start(bf16[8,4,24,768]{3,2,1,0:T(8,128)(2,1)S(1)} %shard_map.58.refs_7_), channel_id=1, source_target_pairs={{0,64},{1,193},{2,66},{3,195},{4,68},{5,197},{6,70},{7,199},{8,72}... | collective-permute-start | bytes 3538952 | tf_op jit(solution)/shard_map/ppermute | solution.py:160
  48.2 2.3 %collective-permute-start.1 = (bf16[24,512]{1,0:T(8,128)(2,1)}, bf16[24,512]{1,0:T(8,128)(2,1)S(1)}, u32[]{:S(2)}, u32[]{:S(2)}) collective-permute-start(bf16[24,512]{1,0:T(8,128)(2,1)} %get-tuple-element.15.refs_0_), channel_id=1, source_target_pairs={{0,4},{2,6},{4,0},{6,2},{8,12},{10,14},{12,8},{14,10},{16,20},{18,... | collective-permute-start | bytes 73736 | tf_op jit(solution)/shard_map/ppermute | solution.py:141
  50.5 1.2 collective-permute-start.2
  51.7 4.0 %local_states.1 = bf16[2048,128]{1,0:T(8,128)(2,1)} custom-call(bf16[256,2048]{1,0:T(8,128)(2,1)} %k_ref.3, bf16[256,2048]{1,0:T(8,128)(2,1)} %v_ref.3), custom_call_target="tpu_custom_call" | custom-call | tf_op jit(solution)/shard_map/local_states/pallas_call | solution.py:41
  55.6 8.5 %all-to-all-start = ((bf16[128,16,128]{2,1,0:T(8,128)(2,1)}), bf16[128,16,128]{2,1,0:T(8,128)(2,1)S(1)}, u32[]{:S(2)}, u32[]{:S(2)}) async-start(bf16[128,16,128]{2,1,0:T(8,128)(2,1)} %bitcast.4), calls=%async_computation | async-start | bytes 1048576 | tf_op jit(solution)/shard_map/all_to_all | solution.py:350
  64.1 0.0 collective-permute-done.1.refs_2_
  64.1 0.8 shard_map.55.refs_0_
  64.9 0.8 collective-permute-start.3
  65.7 2.8 %collective-permute-start.4 = (bf16[4,24,512]{2,1,0:T(8,128)(2,1)S(1)}, bf16[4,24,512]{2,1,0:T(8,128)(2,1)S(1)}, u32[]{:S(2)}, u32[]{:S(2)}) collective-permute-start(bf16[4,24,512]{2,1,0:T(8,128)(2,1)S(1)} %shard_map.55.refs_0_), channel_id=1, source_target_pairs={{0,128},{2,130},{4,132},{6,134},{8,136},{10,138},{12,140},{14,142}... | collective-permute-start | bytes 294920 | tf_op jit(solution)/shard_map/ppermute | solution.py:141
  68.5 1.0 collective-permute-start.5
  69.5 2.5 %collective-permute-done.3.refs_1_ = bf16[4,24,512]{2,1,0:T(8,128)(2,1)S(1)} collective-permute-done((bf16[4,24,512]{2,1,0:T(8,128)(2,1)S(1)}, bf16[4,24,512]{2,1,0:T(8,128)(2,1)S(1)}, u32[]{:S(2)}, u32[]{:S(2)}) %collective-permute-start.3) | collective-permute-done | bytes 98336 | tf_op jit(solution)/shard_map/ppermute | solution.py:141
  72.0 4.1 %collective-permute-done.4.refs_2_ = bf16[4,24,512]{2,1,0:T(8,128)(2,1)S(1)} collective-permute-done((bf16[4,24,512]{2,1,0:T(8,128)(2,1)S(1)}, bf16[4,24,512]{2,1,0:T(8,128)(2,1)S(1)}, u32[]{:S(2)}, u32[]{:S(2)}) %collective-permute-start.4) | collective-permute-done | bytes 98336 | tf_op jit(solution)/shard_map/ppermute | solution.py:141
  76.1 0.0 collective-permute-done.5.refs_3_
  76.1 0.6 shard_map.56.refs_0_
  76.7 0.1 collective-permute-start.6
  76.8 1.5 collective-permute-start.8
  78.2 5.5 %collective-permute-done.6.refs_1_ = bf16[4,4,24,512]{3,2,1,0:T(8,128)(2,1)S(1)} collective-permute-done((bf16[4,4,24,512]{3,2,1,0:T(8,128)(2,1)S(1)}, bf16[4,4,24,512]{3,2,1,0:T(8,128)(2,1)S(1)}, u32[]{:S(2)}, u32[]{:S(2)}) %collective-permute-start.6) | collective-permute-done | bytes 393248 | tf_op jit(solution)/shard_map/ppermute | solution.py:160
  83.7 1.3 collective-permute-start.7
  85.0 0.8 copy-done
  85.8 0.0 collective-permute-done.8.refs_3_
  85.8 0.1 collective-permute-start.9
  85.9 0.8 copy-done.2
  86.7 1.2 collective-permute-start.20
  87.9 6.6 %collective-permute-done.7.refs_2_ = bf16[4,4,24,512]{3,2,1,0:T(8,128)(2,1)} collective-permute-done((bf16[4,4,24,512]{3,2,1,0:T(8,128)(2,1)S(1)}, bf16[4,4,24,512]{3,2,1,0:T(8,128)(2,1)}, u32[]{:S(2)}, u32[]{:S(2)}) %collective-permute-start.7) | collective-permute-done | bytes 393248 | tf_op jit(solution)/shard_map/ppermute | solution.py:160
  94.5 0.1 collective-permute-start.21
  94.6 0.1 collective-permute-done.9.refs_4_
  94.6 3.4 %collective-permute-start.18 = (bf16[4,4,24,512]{3,2,1,0:T(8,128)(2,1)}, bf16[4,4,24,512]{3,2,1,0:T(8,128)(2,1)}, u32[]{:S(2)}, u32[]{:S(2)}) collective-permute-start(bf16[4,4,24,512]{3,2,1,0:T(8,128)(2,1)} %collective-permute-done.7.refs_2_), channel_id=1, source_target_pairs={{0,8},{1,57},{2,10},{3,59},{4,12},{5,61},{6,14},{7,63},{8,16},{9,1... | collective-permute-start | bytes 1179656 | tf_op jit(solution)/shard_map/ppermute | solution.py:160
  98.0 0.0 collective-permute-done.13.refs_6_
  98.0 2.6 %collective-permute-start.23 = (bf16[4,8,24,768]{3,2,1,0:T(8,128)(2,1)}, bf16[4,8,24,768]{3,2,1,0:T(8,128)(2,1)}, u32[]{:S(2)}, u32[]{:S(2)}) collective-permute-start(bf16[4,8,24,768]{3,2,1,0:T(8,128)(2,1)} %collective-permute-done.13.refs_6_), channel_id=1, source_target_pairs={{0,2},{1,7},{2,4},{3,1},{4,6},{5,3},{6,0},{7,5},{8,10},{9,15},{10,... | collective-permute-start | bytes 3538952 | tf_op jit(solution)/shard_map/ppermute | solution.py:160
  100.6 1.1 collective-permute-start.24
  101.7 0.0 all-to-all-done.x_ref
  101.7 1.0 exclusive_sums.1
  102.7 9.6 %all-to-all-start.1 = ((bf16[128,16,128]{2,1,0:T(8,128)(2,1)}), bf16[128,16,128]{2,1,0:T(8,128)(2,1)S(1)}, u32[]{:S(2)}, u32[]{:S(2)}) async-start(bf16[128,16,128]{2,1,0:T(8,128)(2,1)} %exclusive_sums.1), calls=%async_computation.1 | async-start | bytes 1048576 | tf_op jit(solution)/shard_map/all_to_all | solution.py:352
  112.3 0.0 copy-start.9
  112.4 0.7 collective-permute-start.19
  113.0 13.7 %collective-permute-done.19.refs_3_ = bf16[4,4,24,512]{3,2,1,0:T(8,128)(2,1)S(1)} collective-permute-done((bf16[4,4,24,512]{3,2,1,0:T(8,128)(2,1)}, bf16[4,4,24,512]{3,2,1,0:T(8,128)(2,1)S(1)}, u32[]{:S(2)}, u32[]{:S(2)}) %collective-permute-start.19) | collective-permute-done | bytes 393248 | tf_op jit(solution)/shard_map/ppermute | solution.py:160
  126.7 0.7 copy-done.6
  127.5 1.7 %collective-permute-start.22 = (bf16[4,4,24,512]{3,2,1,0:T(8,128)(2,1)}, bf16[4,4,24,512]{3,2,1,0:T(8,128)(2,1)}, u32[]{:S(2)}, u32[]{:S(2)}) collective-permute-start(bf16[4,4,24,512]{3,2,1,0:T(8,128)(2,1)} %collective-permute-done.18.refs_2_), channel_id=1, source_target_pairs={{0,8},{1,57},{2,10},{3,59},{4,12},{5,61},{6,14},{7,63},{8,16},{9,1... | collective-permute-start | bytes 1179656 | tf_op jit(solution)/shard_map/ppermute | solution.py:160
  129.2 6.1 %inner_attention.1.i_ref = f32[256,2048]{1,0:T(8,128)} custom-call(bf16[256,2048]{1,0:T(8,128)(2,1)} %q_ref.3, bf16[256,2048]{1,0:T(8,128)(2,1)} %k_ref.3, bf16[256,2048]{1,0:T(8,128)(2,1)} %v_ref.3), custom_call_target="tpu_custom_call" | custom-call | tf_op jit(solution)/shard_map/inner_attention/pallas_call | solution.py:87
  135.3 3.7 %normed_attention.1.n_ref = bf16[256,2048]{1,0:T(8,128)(2,1)S(1)} custom-call(s32[4]{0:T(128)S(1)} %pad_add_fusion.place_ref, bf16[256,2048]{1,0:T(8,128)(2,1)} %q_ref.3, f32[256,2048]{1,0:T(8,128)} %inner_attention.1.i_ref, bf16[2048,128]{1,0:T(8,128)(2,1)S(1)} %bitcast.12, f32[1,2048]{1,0:T(1,128)S(1)} %bitcast.14), custom_call_target="tpu_custom_call" | custom-call | tf_op jit(solution)/shard_map/normed_attention/pallas_call | solution.py:115
  139.0 3.9 %shard_map.59 = (f32[4,8,4,24,128]{4,3,2,1,0:T(8,128)S(1)}, f32[4,8,4,24,128]{4,3,2,1,0:T(8,128)S(1)}) custom-call(s32[4]{0:T(128)S(1)} %pad_add_fusion.place_ref, bf16[256,2048]{1,0:T(8,128)(2,1)S(1)} %normed_attention.1.n_ref, bf16[4,4,24,512]{3,2,1,0:T(8,128)(2,1)S(1)} %shard_map.56.refs_0_, bf16[4,4,24,512]{3,2,1,0:T(8,128)(2,1)S(1)} %copy-done.1, ...), custom_call_target="tpu_custom_call" | custom-call | tf_op jit(solution)/shard_map/pallas_call | solution.py:323
  143.0 2.8 %shard_map.60 = (f32[4,8,4,24,128]{4,3,2,1,0:T(8,128)S(1)}, f32[4,8,4,24,128]{4,3,2,1,0:T(8,128)S(1)}) custom-call(s32[4]{0:T(128)S(1)} %pad_add_fusion.place_ref, bf16[256,2048]{1,0:T(8,128)(2,1)S(1)} %normed_attention.1.n_ref, f32[4,8,4,24,128]{4,3,2,1,0:T(8,128)S(1)} %get-tuple-element.19.refs_0_, ...), custom_call_target="tpu_custom_call", output_to_operand_aliasing={{0}: (2, {}), {1}: (3, {})} | custom-call | tf_op jit(solution)/shard_map/pallas_call | solution.py:323
  145.8 2.7 %shard_map.61 = (f32[4,8,4,24,128]{4,3,2,1,0:T(8,128)S(1)}, f32[4,8,4,24,128]{4,3,2,1,0:T(8,128)S(1)}) custom-call(s32[4]{0:T(128)S(1)} %pad_add_fusion.place_ref, bf16[256,2048]{1,0:T(8,128)(2,1)S(1)} %normed_attention.1.n_ref, f32[4,8,4,24,128]{4,3,2,1,0:T(8,128)S(1)} %get-tuple-element.21.refs_0_, ...), custom_call_target="tpu_custom_call", output_to_operand_aliasing={{0}: (2, {}), {1}: (3, {})} | custom-call | tf_op jit(solution)/shard_map/pallas_call | solution.py:323
  148.6 12.0 %collective-permute-start.25 = (f32[3072,128]{1,0:T(8,128)S(1)}, f32[3072,128]{1,0:T(8,128)S(1)}, u32[]{:S(2)}, u32[]{:S(2)}) collective-permute-start(f32[3072,128]{1,0:T(8,128)S(1)} %bitcast.11), channel_id=1, source_target_pairs={{0,1},{1,0},{2,3},{3,2},{4,5},{5,4},{6,7},{7,6},{8,9},{9,8},{10,11... | collective-permute-start | bytes 4718600 | tf_op jit(solution)/shard_map/ppermute | solution.py:359
  160.6 3.0 %collective-permute-done.25.other_ref = f32[3072,128]{1,0:T(8,128)S(1)} collective-permute-done((f32[3072,128]{1,0:T(8,128)S(1)}, f32[3072,128]{1,0:T(8,128)S(1)}, u32[]{:S(2)}, u32[]{:S(2)}) %collective-permute-start.25) | collective-permute-done | bytes 1572896 | tf_op jit(solution)/shard_map/ppermute | solution.py:359
  163.6 1.2 finish.1
  (28 shorter events, 0.1 us)
Async XLA Ops:
  0.0 0.9 copy-start.8
  27.9 6.5 %collective-permute-start.10 = (bf16[8,24,768]{2,1,0:T(8,128)(2,1)S(1)}, bf16[8,24,768]{2,1,0:T(8,128)(2,1)S(1)}, u32[]{:S(2)}, u32[]{:S(2)}) collective-permute-start(bf16[8,24,768]{2,1,0:T(8,128)(2,1)S(1)} %get-tuple-element.17.refs_0_), channel_id=1, source_target_pairs={{0,64},{1,193},{2,66},{3,195},{4,68},{5,197},{6,70},{7,199},{8,72}... | collective-permute-start | bytes 884744 | tf_op jit(solution)/shard_map/ppermute | solution.py:160
  30.7 8.0 %collective-permute-start.14 = (bf16[8,24,768]{2,1,0:T(8,128)(2,1)S(1)}, bf16[8,24,768]{2,1,0:T(8,128)(2,1)S(1)}, u32[]{:S(2)}, u32[]{:S(2)}) collective-permute-start(bf16[8,24,768]{2,1,0:T(8,128)(2,1)S(1)} %get-tuple-element.18.refs_0_), channel_id=1, source_target_pairs={{0,2},{1,7},{2,4},{3,1},{4,6},{5,3},{6,0},{7,5},{8,10},{9,15},{10,... | collective-permute-start | bytes 884744 | tf_op jit(solution)/shard_map/ppermute | solution.py:160
  33.2 7.5 %collective-permute-start.11 = (bf16[8,24,768]{2,1,0:T(8,128)(2,1)S(1)}, bf16[8,24,768]{2,1,0:T(8,128)(2,1)S(1)}, u32[]{:S(2)}, u32[]{:S(2)}) collective-permute-start(bf16[8,24,768]{2,1,0:T(8,128)(2,1)S(1)} %get-tuple-element.17.refs_0_), channel_id=1, source_target_pairs={{0,192},{1,65},{2,194},{3,67},{4,196},{5,69},{6,198},{7,71},{8,200... | collective-permute-start | bytes 884744 | tf_op jit(solution)/shard_map/ppermute | solution.py:160
  34.4 8.2 %collective-permute-start.12 = (bf16[8,24,768]{2,1,0:T(8,128)(2,1)S(1)}, bf16[8,24,768]{2,1,0:T(8,128)(2,1)S(1)}, u32[]{:S(2)}, u32[]{:S(2)}) collective-permute-start(bf16[8,24,768]{2,1,0:T(8,128)(2,1)S(1)} %collective-permute-done.10.refs_1_), channel_id=1, source_target_pairs={{0,64},{1,193},{2,66},{3,195},{4,68},{5,197},{6,70},{7,199},{8,72}... | collective-permute-start | bytes 884744 | tf_op jit(solution)/shard_map/ppermute | solution.py:160
  37.8 7.1 %collective-permute-start.15 = (bf16[8,24,768]{2,1,0:T(8,128)(2,1)S(1)}, bf16[8,24,768]{2,1,0:T(8,128)(2,1)S(1)}, u32[]{:S(2)}, u32[]{:S(2)}) collective-permute-start(bf16[8,24,768]{2,1,0:T(8,128)(2,1)S(1)} %get-tuple-element.18.refs_0_), channel_id=1, source_target_pairs={{0,6},{1,3},{2,0},{3,5},{4,2},{5,7},{6,4},{7,1},{8,14},{9,11},{10,... | collective-permute-start | bytes 884744 | tf_op jit(solution)/shard_map/ppermute | solution.py:160
  38.7 6.6 %collective-permute-start.16 = (bf16[8,24,768]{2,1,0:T(8,128)(2,1)S(1)}, bf16[8,24,768]{2,1,0:T(8,128)(2,1)S(1)}, u32[]{:S(2)}, u32[]{:S(2)}) collective-permute-start(bf16[8,24,768]{2,1,0:T(8,128)(2,1)S(1)} %collective-permute-done.14.refs_1_), channel_id=1, source_target_pairs={{0,2},{1,7},{2,4},{3,1},{4,6},{5,3},{6,0},{7,5},{8,10},{9,15},{10,... | collective-permute-start | bytes 884744 | tf_op jit(solution)/shard_map/ppermute | solution.py:160
  43.2 54.8 %collective-permute-start.13 = (bf16[4,8,24,768]{3,2,1,0:T(8,128)(2,1)S(1)}, bf16[4,8,24,768]{3,2,1,0:T(8,128)(2,1)}, u32[]{:S(2)}, u32[]{:S(2)}) collective-permute-start(bf16[4,8,24,768]{3,2,1,0:T(8,128)(2,1)S(1)} %shard_map.57.refs_5_), channel_id=1, source_target_pairs={{0,2},{1,7},{2,4},{3,1},{4,6},{5,3},{6,0},{7,5},{8,10},{9,15},{10,... | collective-permute-start | bytes 3538952 | tf_op jit(solution)/shard_map/ppermute | solution.py:160
  45.9 54.7 %collective-permute-start.17 = (bf16[8,4,24,768]{3,2,1,0:T(8,128)(2,1)S(1)}, bf16[8,4,24,768]{3,2,1,0:T(8,128)(2,1)}, u32[]{:S(2)}, u32[]{:S(2)}) collective-permute-start(bf16[8,4,24,768]{3,2,1,0:T(8,128)(2,1)S(1)} %shard_map.58.refs_7_), channel_id=1, source_target_pairs={{0,64},{1,193},{2,66},{3,195},{4,68},{5,197},{6,70},{7,199},{8,72}... | collective-permute-start | bytes 3538952 | tf_op jit(solution)/shard_map/ppermute | solution.py:160
  48.2 15.9 %collective-permute-start = (bf16[24,512]{1,0:T(8,128)(2,1)}, bf16[24,512]{1,0:T(8,128)(2,1)S(1)}, u32[]{:S(2)}, u32[]{:S(2)}) collective-permute-start(bf16[24,512]{1,0:T(8,128)(2,1)} %get-tuple-element.15.refs_0_), channel_id=1, source_target_pairs={{0,2},{2,4},{4,6},{6,0},{8,10},{10,12},{12,14},{14,8},{16,18},{18,... | collective-permute-start | bytes 73736 | tf_op jit(solution)/shard_map/ppermute | solution.py:141
  48.2 15.9 %collective-permute-start.1 = (bf16[24,512]{1,0:T(8,128)(2,1)}, bf16[24,512]{1,0:T(8,128)(2,1)S(1)}, u32[]{:S(2)}, u32[]{:S(2)}) collective-permute-start(bf16[24,512]{1,0:T(8,128)(2,1)} %get-tuple-element.15.refs_0_), channel_id=1, source_target_pairs={{0,4},{2,6},{4,0},{6,2},{8,12},{10,14},{12,8},{14,10},{16,20},{18,... | collective-permute-start | bytes 73736 | tf_op jit(solution)/shard_map/ppermute | solution.py:141
  50.5 13.6 %collective-permute-start.2 = (bf16[24,512]{1,0:T(8,128)(2,1)}, bf16[24,512]{1,0:T(8,128)(2,1)S(1)}, u32[]{:S(2)}, u32[]{:S(2)}) collective-permute-start(bf16[24,512]{1,0:T(8,128)(2,1)} %get-tuple-element.15.refs_0_), channel_id=1, source_target_pairs={{0,6},{2,0},{4,2},{6,4},{8,14},{10,8},{12,10},{14,12},{16,22},{18,... | collective-permute-start | bytes 73736 | tf_op jit(solution)/shard_map/ppermute | solution.py:141
  55.6 46.1 %all-to-all-start = ((bf16[128,16,128]{2,1,0:T(8,128)(2,1)}), bf16[128,16,128]{2,1,0:T(8,128)(2,1)S(1)}, u32[]{:S(2)}, u32[]{:S(2)}) async-start(bf16[128,16,128]{2,1,0:T(8,128)(2,1)} %bitcast.4), calls=%async_computation | async-start | bytes 1048576 | tf_op jit(solution)/shard_map/all_to_all | solution.py:350
  64.9 7.1 %collective-permute-start.3 = (bf16[4,24,512]{2,1,0:T(8,128)(2,1)S(1)}, bf16[4,24,512]{2,1,0:T(8,128)(2,1)S(1)}, u32[]{:S(2)}, u32[]{:S(2)}) collective-permute-start(bf16[4,24,512]{2,1,0:T(8,128)(2,1)S(1)} %shard_map.55.refs_0_), channel_id=1, source_target_pairs={{0,64},{2,66},{4,68},{6,70},{8,72},{10,74},{12,76},{14,78},{16,80}... | collective-permute-start | bytes 294920 | tf_op jit(solution)/shard_map/ppermute | solution.py:141
  65.7 10.4 %collective-permute-start.4 = (bf16[4,24,512]{2,1,0:T(8,128)(2,1)S(1)}, bf16[4,24,512]{2,1,0:T(8,128)(2,1)S(1)}, u32[]{:S(2)}, u32[]{:S(2)}) collective-permute-start(bf16[4,24,512]{2,1,0:T(8,128)(2,1)S(1)} %shard_map.55.refs_0_), channel_id=1, source_target_pairs={{0,128},{2,130},{4,132},{6,134},{8,136},{10,138},{12,140},{14,142}... | collective-permute-start | bytes 294920 | tf_op jit(solution)/shard_map/ppermute | solution.py:141
  68.5 7.6 %collective-permute-start.5 = (bf16[4,24,512]{2,1,0:T(8,128)(2,1)S(1)}, bf16[4,24,512]{2,1,0:T(8,128)(2,1)S(1)}, u32[]{:S(2)}, u32[]{:S(2)}) collective-permute-start(bf16[4,24,512]{2,1,0:T(8,128)(2,1)S(1)} %shard_map.55.refs_0_), channel_id=1, source_target_pairs={{0,192},{2,194},{4,196},{6,198},{8,200},{10,202},{12,204},{14,206}... | collective-permute-start | bytes 294920 | tf_op jit(solution)/shard_map/ppermute | solution.py:141
  76.7 7.0 %collective-permute-start.6 = (bf16[4,4,24,512]{3,2,1,0:T(8,128)(2,1)S(1)}, bf16[4,4,24,512]{3,2,1,0:T(8,128)(2,1)S(1)}, u32[]{:S(2)}, u32[]{:S(2)}) collective-permute-start(bf16[4,4,24,512]{3,2,1,0:T(8,128)(2,1)S(1)} %shard_map.56.refs_0_), channel_id=1, source_target_pairs={{0,8},{1,57},{2,10},{3,59},{4,12},{5,61},{6,14},{7,63},{8,16},{9,1... | collective-permute-start | bytes 1179656 | tf_op jit(solution)/shard_map/ppermute | solution.py:160
  76.8 9.0 %collective-permute-start.8 = (bf16[4,4,24,512]{3,2,1,0:T(8,128)(2,1)S(1)}, bf16[4,4,24,512]{3,2,1,0:T(8,128)(2,1)S(1)}, u32[]{:S(2)}, u32[]{:S(2)}) collective-permute-start(bf16[4,4,24,512]{3,2,1,0:T(8,128)(2,1)S(1)} %shard_map.56.refs_0_), channel_id=1, source_target_pairs={{0,56},{1,9},{2,58},{3,11},{4,60},{5,13},{6,62},{7,15},{8,0},{9,17... | collective-permute-start | bytes 1179656 | tf_op jit(solution)/shard_map/ppermute | solution.py:160
  83.7 10.8 %collective-permute-start.7 = (bf16[4,4,24,512]{3,2,1,0:T(8,128)(2,1)S(1)}, bf16[4,4,24,512]{3,2,1,0:T(8,128)(2,1)}, u32[]{:S(2)}, u32[]{:S(2)}) collective-permute-start(bf16[4,4,24,512]{3,2,1,0:T(8,128)(2,1)S(1)} %collective-permute-done.6.refs_1_), channel_id=1, source_target_pairs={{0,8},{1,57},{2,10},{3,59},{4,12},{5,61},{6,14},{7,63},{8,16},{9,1... | collective-permute-start | bytes 1179656 | tf_op jit(solution)/shard_map/ppermute | solution.py:160
  85.0 0.8 copy-start
  85.8 8.8 %collective-permute-start.9 = (bf16[4,4,24,512]{3,2,1,0:T(8,128)(2,1)S(1)}, bf16[4,4,24,512]{3,2,1,0:T(8,128)(2,1)S(1)}, u32[]{:S(2)}, u32[]{:S(2)}) collective-permute-start(bf16[4,4,24,512]{3,2,1,0:T(8,128)(2,1)S(1)} %collective-permute-done.8.refs_3_), channel_id=1, source_target_pairs={{0,56},{1,9},{2,58},{3,11},{4,60},{5,13},{6,62},{7,15},{8,0},{9,17... | collective-permute-start | bytes 1179656 | tf_op jit(solution)/shard_map/ppermute | solution.py:160
  85.9 0.8 copy-start.2
  86.7 56.3 %collective-permute-start.20 = (bf16[4,8,24,768]{3,2,1,0:T(8,128)(2,1)S(1)}, bf16[4,8,24,768]{3,2,1,0:T(8,128)(2,1)}, u32[]{:S(2)}, u32[]{:S(2)}) collective-permute-start(bf16[4,8,24,768]{3,2,1,0:T(8,128)(2,1)S(1)} %shard_map.57.refs_5_), channel_id=1, source_target_pairs={{0,6},{1,3},{2,0},{3,5},{4,2},{5,7},{6,4},{7,1},{8,14},{9,11},{10,... | collective-permute-start | bytes 3538952 | tf_op jit(solution)/shard_map/ppermute | solution.py:160
  94.5 48.5 %collective-permute-start.21 = (bf16[8,4,24,768]{3,2,1,0:T(8,128)(2,1)S(1)}, bf16[8,4,24,768]{3,2,1,0:T(8,128)(2,1)}, u32[]{:S(2)}, u32[]{:S(2)}) collective-permute-start(bf16[8,4,24,768]{3,2,1,0:T(8,128)(2,1)S(1)} %shard_map.58.refs_7_), channel_id=1, source_target_pairs={{0,192},{1,65},{2,194},{3,67},{4,196},{5,69},{6,198},{7,71},{8,200... | collective-permute-start | bytes 3538952 | tf_op jit(solution)/shard_map/ppermute | solution.py:160
  94.6 6.0 %copy-start.4 = (bf16[4,4,24,512]{3,2,1,0:T(8,128)(2,1)}, bf16[4,4,24,512]{3,2,1,0:T(8,128)(2,1)S(1)}, u32[]{:S(2)}) copy-start(bf16[4,4,24,512]{3,2,1,0:T(8,128)(2,1)S(1)} %collective-permute-done.9.refs_4_) | copy-start | bytes 1179652
  94.6 17.8 %collective-permute-start.18 = (bf16[4,4,24,512]{3,2,1,0:T(8,128)(2,1)}, bf16[4,4,24,512]{3,2,1,0:T(8,128)(2,1)}, u32[]{:S(2)}, u32[]{:S(2)}) collective-permute-start(bf16[4,4,24,512]{3,2,1,0:T(8,128)(2,1)} %collective-permute-done.7.refs_2_), channel_id=1, source_target_pairs={{0,8},{1,57},{2,10},{3,59},{4,12},{5,61},{6,14},{7,63},{8,16},{9,1... | collective-permute-start | bytes 1179656 | tf_op jit(solution)/shard_map/ppermute | solution.py:160
  98.0 47.8 %collective-permute-start.23 = (bf16[4,8,24,768]{3,2,1,0:T(8,128)(2,1)}, bf16[4,8,24,768]{3,2,1,0:T(8,128)(2,1)}, u32[]{:S(2)}, u32[]{:S(2)}) collective-permute-start(bf16[4,8,24,768]{3,2,1,0:T(8,128)(2,1)} %collective-permute-done.13.refs_6_), channel_id=1, source_target_pairs={{0,2},{1,7},{2,4},{3,1},{4,6},{5,3},{6,0},{7,5},{8,10},{9,15},{10,... | collective-permute-start | bytes 3538952 | tf_op jit(solution)/shard_map/ppermute | solution.py:160
  100.6 45.2 %collective-permute-start.24 = (bf16[8,4,24,768]{3,2,1,0:T(8,128)(2,1)}, bf16[8,4,24,768]{3,2,1,0:T(8,128)(2,1)}, u32[]{:S(2)}, u32[]{:S(2)}) collective-permute-start(bf16[8,4,24,768]{3,2,1,0:T(8,128)(2,1)} %collective-permute-done.17.refs_8_), channel_id=1, source_target_pairs={{0,64},{1,193},{2,66},{3,195},{4,68},{5,197},{6,70},{7,199},{8,72}... | collective-permute-start | bytes 3538952 | tf_op jit(solution)/shard_map/ppermute | solution.py:160
  102.7 32.6 %all-to-all-start.1 = ((bf16[128,16,128]{2,1,0:T(8,128)(2,1)}), bf16[128,16,128]{2,1,0:T(8,128)(2,1)S(1)}, u32[]{:S(2)}, u32[]{:S(2)}) async-start(bf16[128,16,128]{2,1,0:T(8,128)(2,1)} %exclusive_sums.1), calls=%async_computation.1 | async-start | bytes 1048576 | tf_op jit(solution)/shard_map/all_to_all | solution.py:352
  112.3 22.9 %copy-start.9 = (f32[2048]{0:T(1024)S(1)}, f32[2048]{0:T(1024)}, u32[]{:S(2)}) copy-start(f32[2048]{0:T(1024)} %param.8) | copy-start | bytes 24580
  112.4 14.3 %collective-permute-start.19 = (bf16[4,4,24,512]{3,2,1,0:T(8,128)(2,1)}, bf16[4,4,24,512]{3,2,1,0:T(8,128)(2,1)S(1)}, u32[]{:S(2)}, u32[]{:S(2)}) collective-permute-start(bf16[4,4,24,512]{3,2,1,0:T(8,128)(2,1)} %copy-done.4), channel_id=1, source_target_pairs={{0,56},{1,9},{2,58},{3,11},{4,60},{5,13},{6,62},{7,15},{8,0},{9,17... | collective-permute-start | bytes 1179656 | tf_op jit(solution)/shard_map/ppermute | solution.py:160
  126.7 0.7 copy-start.6
  127.5 18.4 %collective-permute-start.22 = (bf16[4,4,24,512]{3,2,1,0:T(8,128)(2,1)}, bf16[4,4,24,512]{3,2,1,0:T(8,128)(2,1)}, u32[]{:S(2)}, u32[]{:S(2)}) collective-permute-start(bf16[4,4,24,512]{3,2,1,0:T(8,128)(2,1)} %collective-permute-done.18.refs_2_), channel_id=1, source_target_pairs={{0,8},{1,57},{2,10},{3,59},{4,12},{5,61},{6,14},{7,63},{8,16},{9,1... | collective-permute-start | bytes 1179656 | tf_op jit(solution)/shard_map/ppermute | solution.py:160
  135.3 3.7 %copy-start.1 = (bf16[4,4,24,512]{3,2,1,0:T(8,128)(2,1)S(1)}, bf16[4,4,24,512]{3,2,1,0:T(8,128)(2,1)}, u32[]{:S(2)}) copy-start(bf16[4,4,24,512]{3,2,1,0:T(8,128)(2,1)} %copy-done) | copy-start | bytes 1179652
  135.3 3.7 %copy-start.3 = (bf16[4,4,24,512]{3,2,1,0:T(8,128)(2,1)S(1)}, bf16[4,4,24,512]{3,2,1,0:T(8,128)(2,1)}, u32[]{:S(2)}) copy-start(bf16[4,4,24,512]{3,2,1,0:T(8,128)(2,1)} %copy-done.2) | copy-start | bytes 1179652
  135.3 3.7 %copy-start.5 = (bf16[4,4,24,512]{3,2,1,0:T(8,128)(2,1)S(1)}, bf16[4,4,24,512]{3,2,1,0:T(8,128)(2,1)}, u32[]{:S(2)}) copy-start(bf16[4,4,24,512]{3,2,1,0:T(8,128)(2,1)} %copy-done.4) | copy-start | bytes 1179652
  139.0 4.0 %copy-start.7 = (bf16[4,4,24,512]{3,2,1,0:T(8,128)(2,1)S(1)}, bf16[4,4,24,512]{3,2,1,0:T(8,128)(2,1)}, u32[]{:S(2)}) copy-start(bf16[4,4,24,512]{3,2,1,0:T(8,128)(2,1)} %copy-done.6) | copy-start | bytes 1179652
  148.6 15.1 %collective-permute-start.25 = (f32[3072,128]{1,0:T(8,128)S(1)}, f32[3072,128]{1,0:T(8,128)S(1)}, u32[]{:S(2)}, u32[]{:S(2)}) collective-permute-start(f32[3072,128]{1,0:T(8,128)S(1)} %bitcast.11), channel_id=1, source_target_pairs={{0,1},{1,0},{2,3},{3,2},{4,5},{5,4},{6,7},{7,6},{8,9},{9,8},{10,11... | collective-permute-start | bytes 4718600 | tf_op jit(solution)/shard_map/ppermute | solution.py:359

commit v6 on v5

--- a/solution.py
+++ b/solution.py
@@ -178,14 +178,13 @@
 
 def round_z(block):
     ahead, back = [block], [block]
-    for step in range(1, 5):
+    for _ in range(1, 4):
         ahead.append(turn(ahead[-1], "z", 1))
-        if step < 4:
-            back.append(turn(back[-1], "z", -1))
-    return ahead + back[1:]
-
-
-def assemble(place, sources, pieces, outs, cuts):
+        back.append(turn(back[-1], "z", -1))
+    return ahead + [turn(block, "z", 4)] + back[1:]
+
+
+def assemble(place, sources, pieces, outs, cuts, stored=0):
     count = len(pieces)
 
     def kernel(place_ref, *refs):
@@ -199,7 +198,7 @@
         out_specs=[vmem] * len(outs),
         out_shape=[pltpu.VMEM(o, BF) for o in outs],
         compiler_params=SMALL,
-    )(place, *near(*pieces))
+    )(place, *away(*pieces[:stored]), *near(*pieces[stored:]))
 
 
 def gather_a(own, place):
@@ -266,7 +265,7 @@
     on_y, on_x = (lambda p, i: source(p, 0, i)), (lambda p, i: source(p, 2, i))
     along_y, along_x = around(col_b, "y"), around(col_c, "x")
     (plane_b,) = assemble(place, on_y, along_y, [(NY, NZ, n, PART_B)], cut_y)
-    (plane_c,) = assemble(place, on_x, along_x, [(NZ, NX, n, PART_C)], cut_x)
+    (plane_c,) = assemble(place, on_x, along_x, [(NZ, NX, n, PART_C)], cut_x, 2)
     return around(plane_b, "x"), around(plane_c, "y")
 
 
@@ -276,7 +275,7 @@
 
 
 HALVES = (slice(0, NZ // 2), slice(NZ // 2, NZ))
-STAGES = (((0, 1, 2, 5, 6), (0, 1)), ((3, 7), (2,)), ((4,), (3,)))
+STAGES = (((0, 1, 5), (0, 1)), ((2, 4, 6), (2,)), ((3, 7), (3,)))
 
 
 def project_kernel(stage, place_ref, n_ref, *refs):

time: 166 us -> 170 us (1.024)
  starting transfers between devices: 67.1 us -> 70.2 us
  waiting for transfers between devices: 39.3 us -> 42.3 us
    ppermute x1, starting transfers between devices: 12 us -> 15.9 us  [whole(): other = lax.ppermute(theirs, 'head', [(0, 1), (1, 0)])]
    all_to_all x1, starting transfers between devices: 9.64 us -> 6.25 us  [whole(): prior = lax.all_to_all(sums.reshape(-1, DH), SEQ, 0, 0, tiled=True)]
    ppermute x19, waiting for transfers between devices: 29.6 us -> 32.7 us  [turn(): return lax.ppermute(block, SEQ + ('head',), pairs)]
    ppermute x19, starting transfers between devices: 29 us -> 31.2 us  [turn(): return lax.ppermute(block, SEQ + ('head',), pairs)]
  transfers between devices with their start and end apart: 28 -> 28, of which waited for: 12 -> 10; matrix products, arithmetic and copies ran while one was open for 0% -> 0% of each run, Pallas kernels for 15% -> 14%
where the time goes in v6:
time: 170 us; the launch traced here: 169 us
  starting transfers between devices  70.2 us (41%)
  waiting for transfers between devices  42.3 us (25%)
  Pallas kernels  28.5 us (17%)
  blocking collectives  26.4 us (16%)
    ppermute x19, waiting for transfers between devices, turn(): return lax.ppermute(block, SEQ + ('head',), pairs)  32.7 us
    ppermute x19, starting transfers between devices, turn(): return lax.ppermute(block, SEQ + ('head',), pairs)  31.2 us
    all_to_all x1, blocking collectives, gather_bc(): column = lax.all_to_all(copies, 'z', 0, 0)  26.4 us
    ppermute x1, starting transfers between devices, whole(): other = lax.ppermute(theirs, 'head', [(0, 1), (1, 0)])  15.9 us
    pallas_call x3, Pallas kernels, project(): pl.pallas_call(functools.partial(project_kernel, stage), in_specs=[SMEM]...  9.7 us
    all_to_all x1, starting transfers between devices, whole(): shares = lax.all_to_all(states, SEQ, 0, 0, tiled=True)  8.92 us
    ppermute x6, starting transfers between devices, shift(): return lax.ppermute(block, SEQ, pairs)  7.98 us
    ppermute x6, waiting for transfers between devices, shift(): return lax.ppermute(block, SEQ, pairs)  6.56 us
  transfers between devices with their start and end apart: 28, of which 10 were waited for; matrix products, arithmetic and copies ran while one was open for 0% of the time, Pallas kernels for 14%

profile of v6, /device:TPU:1, one launch (start us, length us, event | category | flops | bytes accessed | tf_op | source)
XLA Modules:
  0.0 169.4 jit_solution(5912564463671794077)
XLA Ops:
  0.0 0.9 copy-done.5
  0.9 26.4 %all_to_all.22.column_ref = bf16[8,24,1536]{2,1,0:T(8,128)(2,1)S(1)} all-to-all(bf16[8,24,1536]{2,1,0:T(8,128)(2,1)S(1)} %get-tuple-element.16), channel_id=1, replica_groups=mesh['y'=4,'z'=8,'x'=4,'head'=2] {'z'}, dimensions={0} | all-to-all | bytes 1179648 | tf_op jit(solution)/shard_map/all_to_all | solution.py:263
  27.3 0.0 copy-start.4
  27.4 2.8 %collective-permute-start.8 = (bf16[8,24,768]{2,1,0:T(8,128)(2,1)S(1)}, bf16[8,24,768]{2,1,0:T(8,128)(2,1)S(1)}, u32[]{:S(2)}, u32[]{:S(2)}) collective-permute-start(bf16[8,24,768]{2,1,0:T(8,128)(2,1)S(1)} %get-tuple-element.17.refs_0_), channel_id=1, source_target_pairs={{0,64},{1,193},{2,66},{3,195},{4,68},{5,197},{6,70},{7,199},{8,72}... | collective-permute-start | bytes 884744 | tf_op jit(solution)/shard_map/ppermute | solution.py:160
  30.2 2.5 %collective-permute-start.12 = (bf16[8,24,768]{2,1,0:T(8,128)(2,1)S(1)}, bf16[8,24,768]{2,1,0:T(8,128)(2,1)}, u32[]{:S(2)}, u32[]{:S(2)}) collective-permute-start(bf16[8,24,768]{2,1,0:T(8,128)(2,1)S(1)} %get-tuple-element.18.refs_0_), channel_id=1, source_target_pairs={{0,2},{1,7},{2,4},{3,1},{4,6},{5,3},{6,0},{7,5},{8,10},{9,15},{10,... | collective-permute-start | bytes 884744 | tf_op jit(solution)/shard_map/ppermute | solution.py:160
  32.6 0.0 collective-permute-start.9
  32.6 1.2 collective-permute-done.8.refs_1_
  33.8 3.5 %collective-permute-start.10 = (bf16[8,24,768]{2,1,0:T(8,128)(2,1)S(1)}, bf16[8,24,768]{2,1,0:T(8,128)(2,1)S(1)}, u32[]{:S(2)}, u32[]{:S(2)}) collective-permute-start(bf16[8,24,768]{2,1,0:T(8,128)(2,1)S(1)} %collective-permute-done.8.refs_1_), channel_id=1, source_target_pairs={{0,64},{1,193},{2,66},{3,195},{4,68},{5,197},{6,70},{7,199},{8,72}... | collective-permute-start | bytes 884744 | tf_op jit(solution)/shard_map/ppermute | solution.py:160
  37.3 0.8 collective-permute-start.13
  38.2 1.9 %collective-permute-start.14 = (bf16[8,24,768]{2,1,0:T(8,128)(2,1)}, bf16[8,24,768]{2,1,0:T(8,128)(2,1)S(1)}, u32[]{:S(2)}, u32[]{:S(2)}) collective-permute-start(bf16[8,24,768]{2,1,0:T(8,128)(2,1)} %collective-permute-done.12.refs_1_), channel_id=1, source_target_pairs={{0,2},{1,7},{2,4},{3,1},{4,6},{5,3},{6,0},{7,5},{8,10},{9,15},{10,... | collective-permute-start | bytes 884744 | tf_op jit(solution)/shard_map/ppermute | solution.py:160
  40.0 0.1 pad_add_fusion.place_ref
  40.1 0.0 collective-permute-done.9.refs_2_
  40.1 1.9 %collective-permute-done.10.refs_3_ = bf16[8,24,768]{2,1,0:T(8,128)(2,1)S(1)} collective-permute-done((bf16[8,24,768]{2,1,0:T(8,128)(2,1)S(1)}, bf16[8,24,768]{2,1,0:T(8,128)(2,1)S(1)}, u32[]{:S(2)}, u32[]{:S(2)}) %collective-permute-start.10) | collective-permute-done | bytes 294944 | tf_op jit(solution)/shard_map/ppermute | solution.py:160
  42.0 0.6 shard_map.57.refs_3_
  42.6 1.5 collective-permute-start.11
  44.2 0.3 collective-permute-done.13.refs_2_
  44.4 0.7 collective-permute-done.14.refs_3_
  45.1 1.1 shard_map.58.refs_5_
  46.3 1.9 %collective-permute-start.15 = (bf16[8,4,24,768]{3,2,1,0:T(8,128)(2,1)S(1)}, bf16[8,4,24,768]{3,2,1,0:T(8,128)(2,1)}, u32[]{:S(2)}, u32[]{:S(2)}) collective-permute-start(bf16[8,4,24,768]{3,2,1,0:T(8,128)(2,1)S(1)} %shard_map.58.refs_5_), channel_id=1, source_target_pairs={{0,64},{1,193},{2,66},{3,195},{4,68},{5,197},{6,70},{7,199},{8,72}... | collective-permute-start | bytes 3538952 | tf_op jit(solution)/shard_map/ppermute | solution.py:160
  48.2 0.0 collective-permute-start
  48.2 2.3 %collective-permute-start.1 = (bf16[24,512]{1,0:T(8,128)(2,1)S(1)}, bf16[24,512]{1,0:T(8,128)(2,1)S(1)}, u32[]{:S(2)}, u32[]{:S(2)}) collective-permute-start(bf16[24,512]{1,0:T(8,128)(2,1)S(1)} %get-tuple-element.15.refs_0_), channel_id=1, source_target_pairs={{0,4},{2,6},{4,0},{6,2},{8,12},{10,14},{12,8},{14,10},{16,20},{18,... | collective-permute-start | bytes 73736 | tf_op jit(solution)/shard_map/ppermute | solution.py:141
  50.5 1.2 collective-permute-start.2
  51.6 4.0 %local_states.1 = bf16[2048,128]{1,0:T(8,128)(2,1)} custom-call(bf16[256,2048]{1,0:T(8,128)(2,1)} %k_ref.3, bf16[256,2048]{1,0:T(8,128)(2,1)} %v_ref.3), custom_call_target="tpu_custom_call" | custom-call | tf_op jit(solution)/shard_map/local_states/pallas_call | solution.py:41
  55.6 8.9 %all-to-all-start = ((bf16[128,16,128]{2,1,0:T(8,128)(2,1)}), bf16[128,16,128]{2,1,0:T(8,128)(2,1)S(1)}, u32[]{:S(2)}, u32[]{:S(2)}) async-start(bf16[128,16,128]{2,1,0:T(8,128)(2,1)} %bitcast.4), calls=%async_computation | async-start | bytes 1048576 | tf_op jit(solution)/shard_map/all_to_all | solution.py:349
  64.5 0.0 collective-permute-done.2.refs_3_
  64.5 0.6 shard_map.55.refs_0_
  65.1 0.8 collective-permute-start.3
  65.8 2.8 %collective-permute-start.4 = (bf16[4,24,512]{2,1,0:T(8,128)(2,1)S(1)}, bf16[4,24,512]{2,1,0:T(8,128)(2,1)S(1)}, u32[]{:S(2)}, u32[]{:S(2)}) collective-permute-start(bf16[4,24,512]{2,1,0:T(8,128)(2,1)S(1)} %shard_map.55.refs_0_), channel_id=1, source_target_pairs={{0,128},{2,130},{4,132},{6,134},{8,136},{10,138},{12,140},{14,142}... | collective-permute-start | bytes 294920 | tf_op jit(solution)/shard_map/ppermute | solution.py:141
  68.7 1.0 collective-permute-start.5
  69.6 2.5 %collective-permute-done.3.refs_1_ = bf16[4,24,512]{2,1,0:T(8,128)(2,1)S(1)} collective-permute-done((bf16[4,24,512]{2,1,0:T(8,128)(2,1)S(1)}, bf16[4,24,512]{2,1,0:T(8,128)(2,1)S(1)}, u32[]{:S(2)}, u32[]{:S(2)}) %collective-permute-start.3) | collective-permute-done | bytes 98336 | tf_op jit(solution)/shard_map/ppermute | solution.py:141
  72.1 4.1 %collective-permute-done.4.refs_2_ = bf16[4,24,512]{2,1,0:T(8,128)(2,1)S(1)} collective-permute-done((bf16[4,24,512]{2,1,0:T(8,128)(2,1)S(1)}, bf16[4,24,512]{2,1,0:T(8,128)(2,1)S(1)}, u32[]{:S(2)}, u32[]{:S(2)}) %collective-permute-start.4) | collective-permute-done | bytes 98336 | tf_op jit(solution)/shard_map/ppermute | solution.py:141
  76.2 0.0 collective-permute-done.5.refs_3_
  76.2 0.6 shard_map.56.refs_0_
  76.8 0.1 collective-permute-start.6
  76.9 1.4 collective-permute-start.7
  78.3 2.9 %collective-permute-start.17 = (bf16[4,4,24,512]{3,2,1,0:T(8,128)(2,1)S(1)}, bf16[4,4,24,512]{3,2,1,0:T(8,128)(2,1)S(1)}, u32[]{:S(2)}, u32[]{:S(2)}) collective-permute-start(bf16[4,4,24,512]{3,2,1,0:T(8,128)(2,1)S(1)} %shard_map.56.refs_0_), channel_id=1, source_target_pairs={{0,32},{1,33},{2,34},{3,35},{4,36},{5,37},{6,38},{7,39},{8,40},{9,... | collective-permute-start | bytes 1179656 | tf_op jit(solution)/shard_map/ppermute | solution.py:160
  81.2 2.5 %collective-permute-done.6.refs_1_ = bf16[4,4,24,512]{3,2,1,0:T(8,128)(2,1)} collective-permute-done((bf16[4,4,24,512]{3,2,1,0:T(8,128)(2,1)S(1)}, bf16[4,4,24,512]{3,2,1,0:T(8,128)(2,1)}, u32[]{:S(2)}, u32[]{:S(2)}) %collective-permute-start.6) | collective-permute-done | bytes 393248 | tf_op jit(solution)/shard_map/ppermute | solution.py:160
  83.8 4.6 %collective-permute-start.19 = (bf16[4,8,24,768]{3,2,1,0:T(8,128)(2,1)S(1)}, bf16[4,8,24,768]{3,2,1,0:T(8,128)(2,1)}, u32[]{:S(2)}, u32[]{:S(2)}) collective-permute-start(bf16[4,8,24,768]{3,2,1,0:T(8,128)(2,1)S(1)} %shard_map.57.refs_3_), channel_id=1, source_target_pairs={{0,6},{1,3},{2,0},{3,5},{4,2},{5,7},{6,4},{7,1},{8,14},{9,11},{10,... | collective-permute-start | bytes 3538952 | tf_op jit(solution)/shard_map/ppermute | solution.py:160
  88.4 0.0 collective-permute-done.7.refs_2_
  88.4 0.0 collective-permute-start.20
  88.4 10.2 %collective-permute-done.17.refs_3_ = bf16[4,4,24,512]{3,2,1,0:T(8,128)(2,1)S(1)} collective-permute-done((bf16[4,4,24,512]{3,2,1,0:T(8,128)(2,1)S(1)}, bf16[4,4,24,512]{3,2,1,0:T(8,128)(2,1)S(1)}, u32[]{:S(2)}, u32[]{:S(2)}) %collective-permute-start.17) | collective-permute-done | bytes 393248 | tf_op jit(solution)/shard_map/ppermute | solution.py:160
  98.6 0.7 copy-done
  99.3 0.0 collective-permute-done.11.refs_4_
  99.3 1.4 collective-permute-start.23
  100.7 0.0 collective-permute-done.15.refs_6_
  100.7 3.7 %collective-permute-start.24 = (bf16[8,4,24,768]{3,2,1,0:T(8,128)(2,1)}, bf16[8,4,24,768]{3,2,1,0:T(8,128)(2,1)}, u32[]{:S(2)}, u32[]{:S(2)}) collective-permute-start(bf16[8,4,24,768]{3,2,1,0:T(8,128)(2,1)} %collective-permute-done.15.refs_6_), channel_id=1, source_target_pairs={{0,64},{1,193},{2,66},{3,195},{4,68},{5,197},{6,70},{7,199},{8,72}... | collective-permute-start | bytes 3538952 | tf_op jit(solution)/shard_map/ppermute | solution.py:160
  104.4 0.0 all-to-all-done.x_ref
  104.4 1.0 exclusive_sums.1
  105.4 6.3 %all-to-all-start.1 = ((bf16[128,16,128]{2,1,0:T(8,128)(2,1)}), bf16[128,16,128]{2,1,0:T(8,128)(2,1)S(1)}, u32[]{:S(2)}, u32[]{:S(2)}) async-start(bf16[128,16,128]{2,1,0:T(8,128)(2,1)} %exclusive_sums.1), calls=%async_computation.1 | async-start | bytes 1048576 | tf_op jit(solution)/shard_map/all_to_all | solution.py:351
  111.7 0.0 copy-start.6
  111.7 0.0 collective-permute-done.16.refs_2_
  111.7 0.7 collective-permute-start.18
  112.4 15.9 %collective-permute-done.18.refs_4_ = bf16[4,4,24,512]{3,2,1,0:T(8,128)(2,1)} collective-permute-done((bf16[4,4,24,512]{3,2,1,0:T(8,128)(2,1)}, bf16[4,4,24,512]{3,2,1,0:T(8,128)(2,1)}, u32[]{:S(2)}, u32[]{:S(2)}) %collective-permute-start.18) | collective-permute-done | bytes 393248 | tf_op jit(solution)/shard_map/ppermute | solution.py:160
  128.3 1.2 collective-permute-start.21
  129.4 0.0 collective-permute-done.19.refs_5_
  129.4 0.3 collective-permute-start.22
  129.7 6.1 %inner_attention.1.i_ref = f32[256,2048]{1,0:T(8,128)} custom-call(bf16[256,2048]{1,0:T(8,128)(2,1)} %q_ref.3, bf16[256,2048]{1,0:T(8,128)(2,1)} %k_ref.3, bf16[256,2048]{1,0:T(8,128)(2,1)} %v_ref.3), custom_call_target="tpu_custom_call" | custom-call | tf_op jit(solution)/shard_map/inner_attention/pallas_call | solution.py:87
  135.8 3.6 %normed_attention.1.n_ref = bf16[256,2048]{1,0:T(8,128)(2,1)S(1)} custom-call(s32[4]{0:T(128)S(1)} %pad_add_fusion.place_ref, bf16[256,2048]{1,0:T(8,128)(2,1)} %q_ref.3, f32[256,2048]{1,0:T(8,128)} %inner_attention.1.i_ref, bf16[2048,128]{1,0:T(8,128)(2,1)S(1)} %bitcast.12, f32[1,2048]{1,0:T(1,128)S(1)} %bitcast.14), custom_call_target="tpu_custom_call" | custom-call | tf_op jit(solution)/shard_map/normed_attention/pallas_call | solution.py:115
  139.5 3.7 %shard_map.59 = (f32[4,8,4,24,128]{4,3,2,1,0:T(8,128)S(1)}, f32[4,8,4,24,128]{4,3,2,1,0:T(8,128)S(1)}) custom-call(s32[4]{0:T(128)S(1)} %pad_add_fusion.place_ref, bf16[256,2048]{1,0:T(8,128)(2,1)S(1)} %normed_attention.1.n_ref, bf16[4,4,24,512]{3,2,1,0:T(8,128)(2,1)S(1)} %shard_map.56.refs_0_, bf16[4,4,24,512]{3,2,1,0:T(8,128)(2,1)} %collective-permute-done.6.refs_1_, ...), custom_call_target="tpu_custom_call" | custom-call | tf_op jit(solution)/shard_map/pallas_call | solution.py:322
  143.2 3.1 %shard_map.60 = (f32[4,8,4,24,128]{4,3,2,1,0:T(8,128)S(1)}, f32[4,8,4,24,128]{4,3,2,1,0:T(8,128)S(1)}) custom-call(s32[4]{0:T(128)S(1)} %pad_add_fusion.place_ref, bf16[256,2048]{1,0:T(8,128)(2,1)S(1)} %normed_attention.1.n_ref, f32[4,8,4,24,128]{4,3,2,1,0:T(8,128)S(1)} %get-tuple-element.19.refs_0_, ...), custom_call_target="tpu_custom_call", output_to_operand_aliasing={{0}: (2, {}), {1}: (3, {})} | custom-call | tf_op jit(solution)/shard_map/pallas_call | solution.py:322
  146.3 2.9 %shard_map.61 = (f32[4,8,4,24,128]{4,3,2,1,0:T(8,128)S(1)}, f32[4,8,4,24,128]{4,3,2,1,0:T(8,128)S(1)}) custom-call(s32[4]{0:T(128)S(1)} %pad_add_fusion.place_ref, bf16[256,2048]{1,0:T(8,128)(2,1)S(1)} %normed_attention.1.n_ref, f32[4,8,4,24,128]{4,3,2,1,0:T(8,128)S(1)} %get-tuple-element.21.refs_0_, ...), custom_call_target="tpu_custom_call", output_to_operand_aliasing={{0}: (2, {}), {1}: (3, {})} | custom-call | tf_op jit(solution)/shard_map/pallas_call | solution.py:322
  149.3 15.9 %collective-permute-start.25 = (f32[3072,128]{1,0:T(8,128)S(1)}, f32[3072,128]{1,0:T(8,128)S(1)}, u32[]{:S(2)}, u32[]{:S(2)}) collective-permute-start(f32[3072,128]{1,0:T(8,128)S(1)} %bitcast.11), channel_id=1, source_target_pairs={{0,1},{1,0},{2,3},{3,2},{4,5},{5,4},{6,7},{7,6},{8,9},{9,8},{10,11... | collective-permute-start | bytes 4718600 | tf_op jit(solution)/shard_map/ppermute | solution.py:358
  165.2 3.0 %collective-permute-done.25.other_ref = f32[3072,128]{1,0:T(8,128)S(1)} collective-permute-done((f32[3072,128]{1,0:T(8,128)S(1)}, f32[3072,128]{1,0:T(8,128)S(1)}, u32[]{:S(2)}, u32[]{:S(2)}) %collective-permute-start.25) | collective-permute-done | bytes 1572896 | tf_op jit(solution)/shard_map/ppermute | solution.py:358
  168.2 1.2 finish.1
  (22 shorter events, 0.1 us)
Async XLA Ops:
  0.0 0.9 copy-start.5
  27.3 17.8 %copy-start.4 = (bf16[8,24,768]{2,1,0:T(8,128)(2,1)}, bf16[8,24,768]{2,1,0:T(8,128)(2,1)S(1)}, u32[]{:S(2)}) copy-start(bf16[8,24,768]{2,1,0:T(8,128)(2,1)S(1)} %get-tuple-element.18.refs_0_) | copy-start | bytes 884740
  27.4 6.5 %collective-permute-start.8 = (bf16[8,24,768]{2,1,0:T(8,128)(2,1)S(1)}, bf16[8,24,768]{2,1,0:T(8,128)(2,1)S(1)}, u32[]{:S(2)}, u32[]{:S(2)}) collective-permute-start(bf16[8,24,768]{2,1,0:T(8,128)(2,1)S(1)} %get-tuple-element.17.refs_0_), channel_id=1, source_target_pairs={{0,64},{1,193},{2,66},{3,195},{4,68},{5,197},{6,70},{7,199},{8,72}... | collective-permute-start | bytes 884744 | tf_op jit(solution)/shard_map/ppermute | solution.py:160
  30.2 8.0 %collective-permute-start.12 = (bf16[8,24,768]{2,1,0:T(8,128)(2,1)S(1)}, bf16[8,24,768]{2,1,0:T(8,128)(2,1)}, u32[]{:S(2)}, u32[]{:S(2)}) collective-permute-start(bf16[8,24,768]{2,1,0:T(8,128)(2,1)S(1)} %get-tuple-element.18.refs_0_), channel_id=1, source_target_pairs={{0,2},{1,7},{2,4},{3,1},{4,6},{5,3},{6,0},{7,5},{8,10},{9,15},{10,... | collective-permute-start | bytes 884744 | tf_op jit(solution)/shard_map/ppermute | solution.py:160
  32.6 7.5 %collective-permute-start.9 = (bf16[8,24,768]{2,1,0:T(8,128)(2,1)S(1)}, bf16[8,24,768]{2,1,0:T(8,128)(2,1)S(1)}, u32[]{:S(2)}, u32[]{:S(2)}) collective-permute-start(bf16[8,24,768]{2,1,0:T(8,128)(2,1)S(1)} %get-tuple-element.17.refs_0_), channel_id=1, source_target_pairs={{0,192},{1,65},{2,194},{3,67},{4,196},{5,69},{6,198},{7,71},{8,200... | collective-permute-start | bytes 884744 | tf_op jit(solution)/shard_map/ppermute | solution.py:160
  33.8 8.2 %collective-permute-start.10 = (bf16[8,24,768]{2,1,0:T(8,128)(2,1)S(1)}, bf16[8,24,768]{2,1,0:T(8,128)(2,1)S(1)}, u32[]{:S(2)}, u32[]{:S(2)}) collective-permute-start(bf16[8,24,768]{2,1,0:T(8,128)(2,1)S(1)} %collective-permute-done.8.refs_1_), channel_id=1, source_target_pairs={{0,64},{1,193},{2,66},{3,195},{4,68},{5,197},{6,70},{7,199},{8,72}... | collective-permute-start | bytes 884744 | tf_op jit(solution)/shard_map/ppermute | solution.py:160
  37.3 7.1 %collective-permute-start.13 = (bf16[8,24,768]{2,1,0:T(8,128)(2,1)S(1)}, bf16[8,24,768]{2,1,0:T(8,128)(2,1)S(1)}, u32[]{:S(2)}, u32[]{:S(2)}) collective-permute-start(bf16[8,24,768]{2,1,0:T(8,128)(2,1)S(1)} %get-tuple-element.18.refs_0_), channel_id=1, source_target_pairs={{0,6},{1,3},{2,0},{3,5},{4,2},{5,7},{6,4},{7,1},{8,14},{9,11},{10,... | collective-permute-start | bytes 884744 | tf_op jit(solution)/shard_map/ppermute | solution.py:160
  38.2 7.0 %collective-permute-start.14 = (bf16[8,24,768]{2,1,0:T(8,128)(2,1)}, bf16[8,24,768]{2,1,0:T(8,128)(2,1)S(1)}, u32[]{:S(2)}, u32[]{:S(2)}) collective-permute-start(bf16[8,24,768]{2,1,0:T(8,128)(2,1)} %collective-permute-done.12.refs_1_), channel_id=1, source_target_pairs={{0,2},{1,7},{2,4},{3,1},{4,6},{5,3},{6,0},{7,5},{8,10},{9,15},{10,... | collective-permute-start | bytes 884744 | tf_op jit(solution)/shard_map/ppermute | solution.py:160
  42.6 56.7 %collective-permute-start.11 = (bf16[4,8,24,768]{3,2,1,0:T(8,128)(2,1)S(1)}, bf16[4,8,24,768]{3,2,1,0:T(8,128)(2,1)}, u32[]{:S(2)}, u32[]{:S(2)}) collective-permute-start(bf16[4,8,24,768]{3,2,1,0:T(8,128)(2,1)S(1)} %shard_map.57.refs_3_), channel_id=1, source_target_pairs={{0,2},{1,7},{2,4},{3,1},{4,6},{5,3},{6,0},{7,5},{8,10},{9,15},{10,... | collective-permute-start | bytes 3538952 | tf_op jit(solution)/shard_map/ppermute | solution.py:160
  46.3 54.4 %collective-permute-start.15 = (bf16[8,4,24,768]{3,2,1,0:T(8,128)(2,1)S(1)}, bf16[8,4,24,768]{3,2,1,0:T(8,128)(2,1)}, u32[]{:S(2)}, u32[]{:S(2)}) collective-permute-start(bf16[8,4,24,768]{3,2,1,0:T(8,128)(2,1)S(1)} %shard_map.58.refs_5_), channel_id=1, source_target_pairs={{0,64},{1,193},{2,66},{3,195},{4,68},{5,197},{6,70},{7,199},{8,72}... | collective-permute-start | bytes 3538952 | tf_op jit(solution)/shard_map/ppermute | solution.py:160
  48.2 16.3 %collective-permute-start = (bf16[24,512]{1,0:T(8,128)(2,1)S(1)}, bf16[24,512]{1,0:T(8,128)(2,1)S(1)}, u32[]{:S(2)}, u32[]{:S(2)}) collective-permute-start(bf16[24,512]{1,0:T(8,128)(2,1)S(1)} %get-tuple-element.15.refs_0_), channel_id=1, source_target_pairs={{0,2},{2,4},{4,6},{6,0},{8,10},{10,12},{12,14},{14,8},{16,18},{18,... | collective-permute-start | bytes 73736 | tf_op jit(solution)/shard_map/ppermute | solution.py:141
  48.2 16.3 %collective-permute-start.1 = (bf16[24,512]{1,0:T(8,128)(2,1)S(1)}, bf16[24,512]{1,0:T(8,128)(2,1)S(1)}, u32[]{:S(2)}, u32[]{:S(2)}) collective-permute-start(bf16[24,512]{1,0:T(8,128)(2,1)S(1)} %get-tuple-element.15.refs_0_), channel_id=1, source_target_pairs={{0,4},{2,6},{4,0},{6,2},{8,12},{10,14},{12,8},{14,10},{16,20},{18,... | collective-permute-start | bytes 73736 | tf_op jit(solution)/shard_map/ppermute | solution.py:141
  50.5 14.1 %collective-permute-start.2 = (bf16[24,512]{1,0:T(8,128)(2,1)S(1)}, bf16[24,512]{1,0:T(8,128)(2,1)S(1)}, u32[]{:S(2)}, u32[]{:S(2)}) collective-permute-start(bf16[24,512]{1,0:T(8,128)(2,1)S(1)} %get-tuple-element.15.refs_0_), channel_id=1, source_target_pairs={{0,6},{2,0},{4,2},{6,4},{8,14},{10,8},{12,10},{14,12},{16,22},{18,... | collective-permute-start | bytes 73736 | tf_op jit(solution)/shard_map/ppermute | solution.py:141
  55.6 48.9 %all-to-all-start = ((bf16[128,16,128]{2,1,0:T(8,128)(2,1)}), bf16[128,16,128]{2,1,0:T(8,128)(2,1)S(1)}, u32[]{:S(2)}, u32[]{:S(2)}) async-start(bf16[128,16,128]{2,1,0:T(8,128)(2,1)} %bitcast.4), calls=%async_computation | async-start | bytes 1048576 | tf_op jit(solution)/shard_map/all_to_all | solution.py:349
  65.1 7.0 %collective-permute-start.3 = (bf16[4,24,512]{2,1,0:T(8,128)(2,1)S(1)}, bf16[4,24,512]{2,1,0:T(8,128)(2,1)S(1)}, u32[]{:S(2)}, u32[]{:S(2)}) collective-permute-start(bf16[4,24,512]{2,1,0:T(8,128)(2,1)S(1)} %shard_map.55.refs_0_), channel_id=1, source_target_pairs={{0,64},{2,66},{4,68},{6,70},{8,72},{10,74},{12,76},{14,78},{16,80}... | collective-permute-start | bytes 294920 | tf_op jit(solution)/shard_map/ppermute | solution.py:141
  65.8 10.3 %collective-permute-start.4 = (bf16[4,24,512]{2,1,0:T(8,128)(2,1)S(1)}, bf16[4,24,512]{2,1,0:T(8,128)(2,1)S(1)}, u32[]{:S(2)}, u32[]{:S(2)}) collective-permute-start(bf16[4,24,512]{2,1,0:T(8,128)(2,1)S(1)} %shard_map.55.refs_0_), channel_id=1, source_target_pairs={{0,128},{2,130},{4,132},{6,134},{8,136},{10,138},{12,140},{14,142}... | collective-permute-start | bytes 294920 | tf_op jit(solution)/shard_map/ppermute | solution.py:141
  68.7 7.5 %collective-permute-start.5 = (bf16[4,24,512]{2,1,0:T(8,128)(2,1)S(1)}, bf16[4,24,512]{2,1,0:T(8,128)(2,1)S(1)}, u32[]{:S(2)}, u32[]{:S(2)}) collective-permute-start(bf16[4,24,512]{2,1,0:T(8,128)(2,1)S(1)} %shard_map.55.refs_0_), channel_id=1, source_target_pairs={{0,192},{2,194},{4,196},{6,198},{8,200},{10,202},{12,204},{14,206}... | collective-permute-start | bytes 294920 | tf_op jit(solution)/shard_map/ppermute | solution.py:141
  76.8 7.0 %collective-permute-start.6 = (bf16[4,4,24,512]{3,2,1,0:T(8,128)(2,1)S(1)}, bf16[4,4,24,512]{3,2,1,0:T(8,128)(2,1)}, u32[]{:S(2)}, u32[]{:S(2)}) collective-permute-start(bf16[4,4,24,512]{3,2,1,0:T(8,128)(2,1)S(1)} %shard_map.56.refs_0_), channel_id=1, source_target_pairs={{0,8},{1,57},{2,10},{3,59},{4,12},{5,61},{6,14},{7,63},{8,16},{9,1... | collective-permute-start | bytes 1179656 | tf_op jit(solution)/shard_map/ppermute | solution.py:160
  76.9 11.4 %collective-permute-start.7 = (bf16[4,4,24,512]{3,2,1,0:T(8,128)(2,1)S(1)}, bf16[4,4,24,512]{3,2,1,0:T(8,128)(2,1)S(1)}, u32[]{:S(2)}, u32[]{:S(2)}) collective-permute-start(bf16[4,4,24,512]{3,2,1,0:T(8,128)(2,1)S(1)} %shard_map.56.refs_0_), channel_id=1, source_target_pairs={{0,56},{1,9},{2,58},{3,11},{4,60},{5,13},{6,62},{7,15},{8,0},{9,17... | collective-permute-start | bytes 1179656 | tf_op jit(solution)/shard_map/ppermute | solution.py:160
  78.3 20.2 %collective-permute-start.17 = (bf16[4,4,24,512]{3,2,1,0:T(8,128)(2,1)S(1)}, bf16[4,4,24,512]{3,2,1,0:T(8,128)(2,1)S(1)}, u32[]{:S(2)}, u32[]{:S(2)}) collective-permute-start(bf16[4,4,24,512]{3,2,1,0:T(8,128)(2,1)S(1)} %shard_map.56.refs_0_), channel_id=1, source_target_pairs={{0,32},{1,33},{2,34},{3,35},{4,36},{5,37},{6,38},{7,39},{8,40},{9,... | collective-permute-start | bytes 1179656 | tf_op jit(solution)/shard_map/ppermute | solution.py:160
  83.8 45.7 %collective-permute-start.19 = (bf16[4,8,24,768]{3,2,1,0:T(8,128)(2,1)S(1)}, bf16[4,8,24,768]{3,2,1,0:T(8,128)(2,1)}, u32[]{:S(2)}, u32[]{:S(2)}) collective-permute-start(bf16[4,8,24,768]{3,2,1,0:T(8,128)(2,1)S(1)} %shard_map.57.refs_3_), channel_id=1, source_target_pairs={{0,6},{1,3},{2,0},{3,5},{4,2},{5,7},{6,4},{7,1},{8,14},{9,11},{10,... | collective-permute-start | bytes 3538952 | tf_op jit(solution)/shard_map/ppermute | solution.py:160
  88.4 12.3 %copy-start.2 = (bf16[4,4,24,512]{3,2,1,0:T(8,128)(2,1)}, bf16[4,4,24,512]{3,2,1,0:T(8,128)(2,1)S(1)}, u32[]{:S(2)}) copy-start(bf16[4,4,24,512]{3,2,1,0:T(8,128)(2,1)S(1)} %collective-permute-done.7.refs_2_) | copy-start | bytes 1179652
  88.4 54.8 %collective-permute-start.20 = (bf16[8,4,24,768]{3,2,1,0:T(8,128)(2,1)S(1)}, bf16[8,4,24,768]{3,2,1,0:T(8,128)(2,1)}, u32[]{:S(2)}, u32[]{:S(2)}) collective-permute-start(bf16[8,4,24,768]{3,2,1,0:T(8,128)(2,1)S(1)} %shard_map.58.refs_5_), channel_id=1, source_target_pairs={{0,192},{1,65},{2,194},{3,67},{4,196},{5,69},{6,198},{7,71},{8,200... | collective-permute-start | bytes 3538952 | tf_op jit(solution)/shard_map/ppermute | solution.py:160
  98.6 0.8 copy-start
  99.3 12.4 %collective-permute-start.16 = (bf16[4,4,24,512]{3,2,1,0:T(8,128)(2,1)}, bf16[4,4,24,512]{3,2,1,0:T(8,128)(2,1)}, u32[]{:S(2)}, u32[]{:S(2)}) collective-permute-start(bf16[4,4,24,512]{3,2,1,0:T(8,128)(2,1)} %collective-permute-done.6.refs_1_), channel_id=1, source_target_pairs={{0,8},{1,57},{2,10},{3,59},{4,12},{5,61},{6,14},{7,63},{8,16},{9,1... | collective-permute-start | bytes 1179656 | tf_op jit(solution)/shard_map/ppermute | solution.py:160
  99.3 47.0 %collective-permute-start.23 = (bf16[4,8,24,768]{3,2,1,0:T(8,128)(2,1)}, bf16[4,8,24,768]{3,2,1,0:T(8,128)(2,1)}, u32[]{:S(2)}, u32[]{:S(2)}) collective-permute-start(bf16[4,8,24,768]{3,2,1,0:T(8,128)(2,1)} %collective-permute-done.11.refs_4_), channel_id=1, source_target_pairs={{0,2},{1,7},{2,4},{3,1},{4,6},{5,3},{6,0},{7,5},{8,10},{9,15},{10,... | collective-permute-start | bytes 3538952 | tf_op jit(solution)/shard_map/ppermute | solution.py:160
  100.7 45.6 %collective-permute-start.24 = (bf16[8,4,24,768]{3,2,1,0:T(8,128)(2,1)}, bf16[8,4,24,768]{3,2,1,0:T(8,128)(2,1)}, u32[]{:S(2)}, u32[]{:S(2)}) collective-permute-start(bf16[8,4,24,768]{3,2,1,0:T(8,128)(2,1)} %collective-permute-done.15.refs_6_), channel_id=1, source_target_pairs={{0,64},{1,193},{2,66},{3,195},{4,68},{5,197},{6,70},{7,199},{8,72}... | collective-permute-start | bytes 3538952 | tf_op jit(solution)/shard_map/ppermute | solution.py:160
  105.4 30.4 %all-to-all-start.1 = ((bf16[128,16,128]{2,1,0:T(8,128)(2,1)}), bf16[128,16,128]{2,1,0:T(8,128)(2,1)S(1)}, u32[]{:S(2)}, u32[]{:S(2)}) async-start(bf16[128,16,128]{2,1,0:T(8,128)(2,1)} %exclusive_sums.1), calls=%async_computation.1 | async-start | bytes 1048576 | tf_op jit(solution)/shard_map/all_to_all | solution.py:351
  111.7 24.1 %copy-start.6 = (f32[2048]{0:T(1024)S(1)}, f32[2048]{0:T(1024)}, u32[]{:S(2)}) copy-start(f32[2048]{0:T(1024)} %param.8) | copy-start | bytes 24580
  111.7 16.6 %collective-permute-start.18 = (bf16[4,4,24,512]{3,2,1,0:T(8,128)(2,1)}, bf16[4,4,24,512]{3,2,1,0:T(8,128)(2,1)}, u32[]{:S(2)}, u32[]{:S(2)}) collective-permute-start(bf16[4,4,24,512]{3,2,1,0:T(8,128)(2,1)} %copy-done.2), channel_id=1, source_target_pairs={{0,56},{1,9},{2,58},{3,11},{4,60},{5,13},{6,62},{7,15},{8,0},{9,17... | collective-permute-start | bytes 1179656 | tf_op jit(solution)/shard_map/ppermute | solution.py:160
  128.3 18.0 %collective-permute-start.21 = (bf16[4,4,24,512]{3,2,1,0:T(8,128)(2,1)}, bf16[4,4,24,512]{3,2,1,0:T(8,128)(2,1)}, u32[]{:S(2)}, u32[]{:S(2)}) collective-permute-start(bf16[4,4,24,512]{3,2,1,0:T(8,128)(2,1)} %collective-permute-done.16.refs_2_), channel_id=1, source_target_pairs={{0,8},{1,57},{2,10},{3,59},{4,12},{5,61},{6,14},{7,63},{8,16},{9,1... | collective-permute-start | bytes 1179656 | tf_op jit(solution)/shard_map/ppermute | solution.py:160
  129.4 16.9 %collective-permute-start.22 = (bf16[4,4,24,512]{3,2,1,0:T(8,128)(2,1)}, bf16[4,4,24,512]{3,2,1,0:T(8,128)(2,1)}, u32[]{:S(2)}, u32[]{:S(2)}) collective-permute-start(bf16[4,4,24,512]{3,2,1,0:T(8,128)(2,1)} %collective-permute-done.18.refs_4_), channel_id=1, source_target_pairs={{0,56},{1,9},{2,58},{3,11},{4,60},{5,13},{6,62},{7,15},{8,0},{9,17... | collective-permute-start | bytes 1179656 | tf_op jit(solution)/shard_map/ppermute | solution.py:160
  135.8 3.6 %copy-start.3 = (bf16[4,4,24,512]{3,2,1,0:T(8,128)(2,1)S(1)}, bf16[4,4,24,512]{3,2,1,0:T(8,128)(2,1)}, u32[]{:S(2)}) copy-start(bf16[4,4,24,512]{3,2,1,0:T(8,128)(2,1)} %copy-done.2) | copy-start | bytes 1179652
  139.5 3.7 %copy-start.1 = (bf16[4,4,24,512]{3,2,1,0:T(8,128)(2,1)S(1)}, bf16[4,4,24,512]{3,2,1,0:T(8,128)(2,1)}, u32[]{:S(2)}) copy-start(bf16[4,4,24,512]{3,2,1,0:T(8,128)(2,1)} %copy-done) | copy-start | bytes 1179652
  149.3 18.9 %collective-permute-start.25 = (f32[3072,128]{1,0:T(8,128)S(1)}, f32[3072,128]{1,0:T(8,128)S(1)}, u32[]{:S(2)}, u32[]{:S(2)}) collective-permute-start(f32[3072,128]{1,0:T(8,128)S(1)} %bitcast.11), channel_id=1, source_target_pairs={{0,1},{1,0},{2,3},{3,2},{4,5},{5,4},{6,7},{7,6},{8,9},{9,8},{10,11... | collective-permute-start | bytes 4718600 | tf_op jit(solution)/shard_map/ppermute | solution.py:358
